TPU v7x, 32 devices: a whole 2x2x4 slice. The times are simulated.
32 devices in a mesh: grp: 8 (over z, y), mem: 4 (over x, core).
Axes of the slice: x: 2, y: 2, z: 4, core: 2. Of those that a mesh axis runs over, the one named last changes fastest.
Arguments:
- potential: float32 [64, 512, 512], P(('grp', 'mem')), may hold values from -6 to 6
- source: float32 [64, 512, 512], P(('grp', 'mem')), may hold values from -20 to 20
- side_faces: float32 [32, 4, 256], P(('grp', 'mem')), may hold values from -6 to 6
- end_faces: float32 [2, 256, 256], replicated, may hold values from -6 to 6
Outputs:
- corrected: float32 [64, 512, 512], P(('grp', 'mem'))
- correction: float32 [32, 256, 256], P(('grp', 'mem'))
All inputs are finite; a program needn't handle non-finite values.
Results may differ from a plain program's by a relative error of at most 0.00002.
Values sent between devices are 32-bit elements; how exact they have to be, the bound alone decides.
No kernel may reach another device: no remote copies, remote signals or barrier semaphores. Data moves between devices by JAX's collectives and lax.ppermute only.
A program may use at most 64 MiB of HBM per device.

v0:
```python
import jax
import jax.numpy as jnp
from jax import lax
from jax.sharding import PartitionSpec as P

SWEEPS = 8


def extended(block, sides, width):
    for axis, dim in sides:
        count = lax.axis_size(axis)
        forward = [(i, i + 1) for i in range(count - 1)]
        backward = [(target, source) for source, target in forward]
        low = lax.ppermute(
            lax.slice_in_dim(block, block.shape[dim] - width, None, axis=dim), axis, forward
        )
        high = lax.ppermute(lax.slice_in_dim(block, 0, width, axis=dim), axis, backward)
        block = jnp.concatenate([low, block, high], axis=dim)
    return block


def from_behind(value, axis, steps):
    count = lax.axis_size(axis)
    initial, last = (max(0, -steps), min(count, count - steps))
    return lax.ppermute(value, axis, [(source, source + steps) for source in range(initial, last)])


def fine_operator(padded):
    center = padded[1:-1, 1:-1, 1:-1]
    beside = padded[2:, 1:-1, 1:-1] + padded[:-2, 1:-1, 1:-1]
    beside = beside + padded[1:-1, 2:, 1:-1] + padded[1:-1, :-2, 1:-1]
    beside = beside + padded[1:-1, 1:-1, 2:] + padded[1:-1, 1:-1, :-2]
    return 4.0 * (6.0 * center - beside)


def restrict_axis(values, direction, before):
    even_part = lax.slice_in_dim(values, 0, None, 2, direction)
    odd_part = lax.slice_in_dim(values, 1, None, 2, direction)
    length = odd_part.shape[direction]
    earlier = jnp.concatenate(
        [before, lax.slice_in_dim(odd_part, 0, length - 1, 1, direction)], direction
    )
    return 0.5 * even_part + 0.25 * (odd_part + earlier)


def zero_slice(values, direction):
    return jnp.zeros_like(lax.slice_in_dim(values, 0, 1, 1, direction))


def prolong_axis(values, direction, beyond):
    length = values.shape[direction]
    following = jnp.concatenate(
        [lax.slice_in_dim(values, 1, length, 1, direction), beyond], direction
    )
    middle = 0.5 * (values + following)
    paired = jnp.stack([values, middle], direction + 1)
    new_shape = list(values.shape)
    new_shape[direction] = 2 * length
    return paired.reshape(new_shape)


def last_slice(values, direction):
    length = values.shape[direction]
    return lax.slice_in_dim(values, length - 1, length, 1, direction)


def side_sum(values, side_faces):
    front_face = side_faces[:, 0:1, :]
    back_face = side_faces[:, 1:2, :]
    left_face = side_faces[:, 2, :][:, :, None]
    right_face = side_faces[:, 3, :][:, :, None]
    front_cells = jnp.concatenate([front_face, values[:, :-1, :]], 1)
    back_cells = jnp.concatenate([values[:, 1:, :], back_face], 1)
    left_cells = jnp.concatenate([left_face, values[:, :, :-1]], 2)
    right_cells = jnp.concatenate([values[:, :, 1:], right_face], 2)
    return front_cells + back_cells + (left_cells + right_cells)


def smooth_red_black(
    forcing, side_faces, end_faces, offset, at_first, at_last, neighbour_fn, initial
):
    planes = forcing.shape[0]
    depth_ids = offset + lax.broadcasted_iota(jnp.int32, forcing.shape, 0)
    row_ids = lax.broadcasted_iota(jnp.int32, forcing.shape, 1)
    col_ids = lax.broadcasted_iota(jnp.int32, forcing.shape, 2)
    parity = (depth_ids + row_ids + col_ids) % 2

    def one_sweep(counter, values):
        for colour in (0, 1):
            padded = neighbour_fn(values)
            lower_face = jnp.where(at_first, end_faces[0], padded[0])
            upper_face = jnp.where(at_last, end_faces[1], padded[-1])
            under_plane = jnp.concatenate([lower_face[None], padded[1:planes]], 0)
            over_plane = jnp.concatenate([padded[2 : planes + 1], upper_face[None]], 0)
            neighbours = under_plane + over_plane + side_sum(values, side_faces)
            update = jnp.logical_and(parity == colour, True)
            values = jnp.where(update, (forcing + neighbours) / 6.0, values)
        return values

    return lax.fori_loop(0, SWEEPS, one_sweep, initial)


def per_device(potential, source, side_faces, end_faces):
    groups = lax.axis_size("grp")
    members = lax.axis_size("mem")
    devices = groups * members
    position = lax.axis_index("grp") * members + lax.axis_index("mem")
    haloed = extended(potential, ((("grp", "mem"), 0),), 1)
    padded = jnp.pad(haloed, ((0, 0), (1, 1), (1, 1)))
    residual = source - fine_operator(padded)
    before = from_behind(residual[-1:], ("grp", "mem"), 1)
    forcing = restrict_axis(residual, 0, before)
    for direction in (1, 2):
        forcing = restrict_axis(forcing, direction, zero_slice(forcing, direction))
    planes = forcing.shape[0]

    def plane_neighbours(values):
        return extended(values, ((("grp", "mem"), 0),), 1)

    correction = smooth_red_black(
        forcing,
        side_faces,
        end_faces,
        position * planes,
        position == 0,
        position == devices - 1,
        plane_neighbours,
        jnp.zeros_like(forcing),
    )
    upper_plane = from_behind(correction, ("grp", "mem"), -1)
    beyond = jnp.where(position == devices - 1, correction, upper_plane)
    refined = prolong_axis(correction, 0, beyond)
    for direction in (1, 2):
        refined = prolong_axis(refined, direction, last_slice(refined, direction))
    return (potential + refined, correction)


def solution(mesh):
    placed = (
        P(("grp", "mem"), None, None),
        P(("grp", "mem"), None, None),
        P(("grp", "mem"), None, None),
        P(),
    )
    return jax.shard_map(
        per_device,
        mesh=mesh,
        in_specs=placed,
        out_specs=(P(("grp", "mem"), None, None), P(("grp", "mem"), None, None)),
        check_vma=False,
    )
```

profile of v0, /device:TPU:1, one launch (start us, length us, event | category | flops | bytes accessed | tf_op | source)
XLA Modules:
  0.0 317.0 jit_solution(882170910944027924)
XLA Ops:
  4.4 4.6 %collective-permute-start.5 = (f32[1,512,512]{2,1,0:T(8,128)S(1)}, f32[1,512,512]{2,1,0:T(8,128)S(1)}, u32[]{:S(2)}, u32[]{:S(2)}) collective-permute-start(f32[1,512,512]{2,1,0:T(8,128)S(1)} %get-tuple-element.105), channel_id=1, source_target_pairs={{0,1},{1,2},{2,3},{3,4},{4,5},{5,6},{6,7},{7,8},{8,9},{9,10},{10,1... | collective-permute-start | bytes 3145736 | tf_op jit(solution)/shard_map/ppermute | solution.py:14
  9.1 17.8 %collective-permute-done.4 = f32[1,512,512]{2,1,0:T(8,128)S(1)} collective-permute-done((f32[1,512,512]{2,1,0:T(8,128)S(1)}, f32[1,512,512]{2,1,0:T(8,128)S(1)}, u32[]{:S(2)}, u32[]{:S(2)}) %collective-permute-start.4) | collective-permute-done | bytes 1048608 | tf_op jit(solution)/shard_map/ppermute | solution.py:17
  26.9 5.0 %collective-permute-done.5 = f32[1,512,512]{2,1,0:T(8,128)S(1)} collective-permute-done((f32[1,512,512]{2,1,0:T(8,128)S(1)}, f32[1,512,512]{2,1,0:T(8,128)S(1)}, u32[]{:S(2)}, u32[]{:S(2)}) %collective-permute-start.5) | collective-permute-done | bytes 1048608 | tf_op jit(solution)/shard_map/ppermute | solution.py:14
  36.7 4.4 %collective-permute-start.6 = (f32[1,512,512]{2,1,0:T(8,128)S(1)}, f32[1,512,512]{2,1,0:T(8,128)}, u32[]{:S(2)}, u32[]{:S(2)}) collective-permute-start(f32[1,512,512]{2,1,0:T(8,128)S(1)} %slice.164), channel_id=1, source_target_pairs={{0,1},{1,2},{2,3},{3,4},{4,5},{5,6},{6,7},{7,8},{8,9},{9,10},{10,1... | collective-permute-start | bytes 3145736 | tf_op jit(solution)/shard_map/ppermute | solution.py:25
  41.1 11.7 %collective-permute-done.6 = f32[1,512,512]{2,1,0:T(8,128)} collective-permute-done((f32[1,512,512]{2,1,0:T(8,128)S(1)}, f32[1,512,512]{2,1,0:T(8,128)}, u32[]{:S(2)}, u32[]{:S(2)}) %collective-permute-start.6) | collective-permute-done | bytes 1048608 | tf_op jit(solution)/shard_map/ppermute | solution.py:25
  52.8 3.2 %fusion.27 = f32[1,512,512]{2,1,0:T(8,128)} fusion(f32[2,512,512]{2,1,0:T(8,128)} %copy-done.4, f32[1,512,512]{2,1,0:T(8,128)} %collective-permute-done.6), kind=kLoop, calls=%fused_computation.56 | loop fusion | flops 1048576 | bytes 4194304 | tf_op jit(solution)/shard_map/add | solution.py:43
  56.0 3.0 slice.128
  59.0 3.7 %slice.127 = f32[1,256,512]{2,1,0:T(8,128)} slice(f32[1,512,512]{2,1,0:T(8,128)} %fusion.27), slice={[0:1:1], [0:512:2], [0:512:1]} | slice | bytes 1048576 | tf_op jit(solution)/shard_map/slice | solution.py:37
  64.7 12.5 %slice.131 = f32[1,256,256]{2,1,0:T(8,128)S(1)} slice(f32[1,256,512]{2,1,0:T(8,128)} %multiply_add_fusion), slice={[0:1:1], [0:256:1], [1:512:2]} | slice | bytes 524288 | tf_op jit(solution)/shard_map/slice | solution.py:38
  77.2 13.0 %slice.130 = f32[1,256,256]{2,1,0:T(8,128)} slice(f32[1,256,512]{2,1,0:T(8,128)} %multiply_add_fusion), slice={[0:1:1], [0:256:1], [0:512:2]} | slice | bytes 524288 | tf_op jit(solution)/shard_map/slice | solution.py:37
  91.3 196.1 %while.11 = (s32[]{:T(128)}, f32[1,256,256]{2,1,0:T(8,128)S(1)}, pred[]{:T(512)}, f32[2,256,256]{2,1,0:T(8,128)S(1)}, pred[]{:T(512)}, /*index=5*/f32[1,4,256]{2...) while((s32[]{:T(128)}, f32[1,256,256]{2,1,0:T(8,128)S(1)}, ...), condition=%wide.region_1.2_spmd.clone, body=%wide.region_0.1_spmd.clone.sunk | while | flops 3670019 | bytes 14682416 | solution.py:100
  93.3 4.5 %collective-permute-start.1 = (f32[1,256,256]{2,1,0:T(8,128)S(1)}, f32[1,256,256]{2,1,0:T(8,128)}, u32[]{:S(2)}, u32[]{:S(2)}) collective-permute-start(f32[1,256,256]{2,1,0:T(8,128)S(1)} %broadcast_select_fusion.2), channel_id=1, source_target_pairs={{0,1},{1,2},{2,3},{3,4},{4,5},{5,6},{6,7},{7,8},{8,9},{9,10},{10,1... | collective-permute-start | bytes 786440 | tf_op jit(solution)/shard_map/while/body/eval_jaxpr/ppermute | solution.py:14
  105.4 3.8 %collective-permute-start.3 = (f32[1,256,256]{2,1,0:T(8,128)S(1)}, f32[1,256,256]{2,1,0:T(8,128)S(1)}, u32[]{:S(2)}, u32[]{:S(2)}) collective-permute-start(f32[1,256,256]{2,1,0:T(8,128)S(1)} %fusion.50), channel_id=1, source_target_pairs={{0,1},{1,2},{2,3},{3,4},{4,5},{5,6},{6,7},{7,8},{8,9},{9,10},{10,1... | collective-permute-start | bytes 786440 | tf_op jit(solution)/shard_map/while/body/eval_jaxpr/ppermute | solution.py:14
  114.8 4.4 %collective-permute-start.1 = (f32[1,256,256]{2,1,0:T(8,128)S(1)}, f32[1,256,256]{2,1,0:T(8,128)}, u32[]{:S(2)}, u32[]{:S(2)}) collective-permute-start(f32[1,256,256]{2,1,0:T(8,128)S(1)} %broadcast_select_fusion.2), channel_id=1, source_target_pairs={{0,1},{1,2},{2,3},{3,4},{4,5},{5,6},{6,7},{7,8},{8,9},{9,10},{10,1... | collective-permute-start | bytes 786440 | tf_op jit(solution)/shard_map/while/body/eval_jaxpr/ppermute | solution.py:14
  127.8 4.5 %collective-permute-start.3 = (f32[1,256,256]{2,1,0:T(8,128)S(1)}, f32[1,256,256]{2,1,0:T(8,128)S(1)}, u32[]{:S(2)}, u32[]{:S(2)}) collective-permute-start(f32[1,256,256]{2,1,0:T(8,128)S(1)} %fusion.50), channel_id=1, source_target_pairs={{0,1},{1,2},{2,3},{3,4},{4,5},{5,6},{6,7},{7,8},{8,9},{9,10},{10,1... | collective-permute-start | bytes 786440 | tf_op jit(solution)/shard_map/while/body/eval_jaxpr/ppermute | solution.py:14
  134.4 3.1 collective-permute-done.3
  139.8 4.4 %collective-permute-start.1 = (f32[1,256,256]{2,1,0:T(8,128)S(1)}, f32[1,256,256]{2,1,0:T(8,128)}, u32[]{:S(2)}, u32[]{:S(2)}) collective-permute-start(f32[1,256,256]{2,1,0:T(8,128)S(1)} %broadcast_select_fusion.2), channel_id=1, source_target_pairs={{0,1},{1,2},{2,3},{3,4},{4,5},{5,6},{6,7},{7,8},{8,9},{9,10},{10,1... | collective-permute-start | bytes 786440 | tf_op jit(solution)/shard_map/while/body/eval_jaxpr/ppermute | solution.py:14
  152.8 4.5 %collective-permute-start.3 = (f32[1,256,256]{2,1,0:T(8,128)S(1)}, f32[1,256,256]{2,1,0:T(8,128)S(1)}, u32[]{:S(2)}, u32[]{:S(2)}) collective-permute-start(f32[1,256,256]{2,1,0:T(8,128)S(1)} %fusion.50), channel_id=1, source_target_pairs={{0,1},{1,2},{2,3},{3,4},{4,5},{5,6},{6,7},{7,8},{8,9},{9,10},{10,1... | collective-permute-start | bytes 786440 | tf_op jit(solution)/shard_map/while/body/eval_jaxpr/ppermute | solution.py:14
  164.7 4.4 %collective-permute-start.1 = (f32[1,256,256]{2,1,0:T(8,128)S(1)}, f32[1,256,256]{2,1,0:T(8,128)}, u32[]{:S(2)}, u32[]{:S(2)}) collective-permute-start(f32[1,256,256]{2,1,0:T(8,128)S(1)} %broadcast_select_fusion.2), channel_id=1, source_target_pairs={{0,1},{1,2},{2,3},{3,4},{4,5},{5,6},{6,7},{7,8},{8,9},{9,10},{10,1... | collective-permute-start | bytes 786440 | tf_op jit(solution)/shard_map/while/body/eval_jaxpr/ppermute | solution.py:14
  177.7 4.5 %collective-permute-start.3 = (f32[1,256,256]{2,1,0:T(8,128)S(1)}, f32[1,256,256]{2,1,0:T(8,128)S(1)}, u32[]{:S(2)}, u32[]{:S(2)}) collective-permute-start(f32[1,256,256]{2,1,0:T(8,128)S(1)} %fusion.50), channel_id=1, source_target_pairs={{0,1},{1,2},{2,3},{3,4},{4,5},{5,6},{6,7},{7,8},{8,9},{9,10},{10,1... | collective-permute-start | bytes 786440 | tf_op jit(solution)/shard_map/while/body/eval_jaxpr/ppermute | solution.py:14
  189.6 4.4 %collective-permute-start.1 = (f32[1,256,256]{2,1,0:T(8,128)S(1)}, f32[1,256,256]{2,1,0:T(8,128)}, u32[]{:S(2)}, u32[]{:S(2)}) collective-permute-start(f32[1,256,256]{2,1,0:T(8,128)S(1)} %broadcast_select_fusion.2), channel_id=1, source_target_pairs={{0,1},{1,2},{2,3},{3,4},{4,5},{5,6},{6,7},{7,8},{8,9},{9,10},{10,1... | collective-permute-start | bytes 786440 | tf_op jit(solution)/shard_map/while/body/eval_jaxpr/ppermute | solution.py:14
  202.7 4.5 %collective-permute-start.3 = (f32[1,256,256]{2,1,0:T(8,128)S(1)}, f32[1,256,256]{2,1,0:T(8,128)S(1)}, u32[]{:S(2)}, u32[]{:S(2)}) collective-permute-start(f32[1,256,256]{2,1,0:T(8,128)S(1)} %fusion.50), channel_id=1, source_target_pairs={{0,1},{1,2},{2,3},{3,4},{4,5},{5,6},{6,7},{7,8},{8,9},{9,10},{10,1... | collective-permute-start | bytes 786440 | tf_op jit(solution)/shard_map/while/body/eval_jaxpr/ppermute | solution.py:14
  214.6 4.4 %collective-permute-start.1 = (f32[1,256,256]{2,1,0:T(8,128)S(1)}, f32[1,256,256]{2,1,0:T(8,128)}, u32[]{:S(2)}, u32[]{:S(2)}) collective-permute-start(f32[1,256,256]{2,1,0:T(8,128)S(1)} %broadcast_select_fusion.2), channel_id=1, source_target_pairs={{0,1},{1,2},{2,3},{3,4},{4,5},{5,6},{6,7},{7,8},{8,9},{9,10},{10,1... | collective-permute-start | bytes 786440 | tf_op jit(solution)/shard_map/while/body/eval_jaxpr/ppermute | solution.py:14
  227.6 4.5 %collective-permute-start.3 = (f32[1,256,256]{2,1,0:T(8,128)S(1)}, f32[1,256,256]{2,1,0:T(8,128)S(1)}, u32[]{:S(2)}, u32[]{:S(2)}) collective-permute-start(f32[1,256,256]{2,1,0:T(8,128)S(1)} %fusion.50), channel_id=1, source_target_pairs={{0,1},{1,2},{2,3},{3,4},{4,5},{5,6},{6,7},{7,8},{8,9},{9,10},{10,1... | collective-permute-start | bytes 786440 | tf_op jit(solution)/shard_map/while/body/eval_jaxpr/ppermute | solution.py:14
  239.5 4.4 %collective-permute-start.1 = (f32[1,256,256]{2,1,0:T(8,128)S(1)}, f32[1,256,256]{2,1,0:T(8,128)}, u32[]{:S(2)}, u32[]{:S(2)}) collective-permute-start(f32[1,256,256]{2,1,0:T(8,128)S(1)} %broadcast_select_fusion.2), channel_id=1, source_target_pairs={{0,1},{1,2},{2,3},{3,4},{4,5},{5,6},{6,7},{7,8},{8,9},{9,10},{10,1... | collective-permute-start | bytes 786440 | tf_op jit(solution)/shard_map/while/body/eval_jaxpr/ppermute | solution.py:14
  252.6 4.5 %collective-permute-start.3 = (f32[1,256,256]{2,1,0:T(8,128)S(1)}, f32[1,256,256]{2,1,0:T(8,128)S(1)}, u32[]{:S(2)}, u32[]{:S(2)}) collective-permute-start(f32[1,256,256]{2,1,0:T(8,128)S(1)} %fusion.50), channel_id=1, source_target_pairs={{0,1},{1,2},{2,3},{3,4},{4,5},{5,6},{6,7},{7,8},{8,9},{9,10},{10,1... | collective-permute-start | bytes 786440 | tf_op jit(solution)/shard_map/while/body/eval_jaxpr/ppermute | solution.py:14
  264.5 4.4 %collective-permute-start.1 = (f32[1,256,256]{2,1,0:T(8,128)S(1)}, f32[1,256,256]{2,1,0:T(8,128)}, u32[]{:S(2)}, u32[]{:S(2)}) collective-permute-start(f32[1,256,256]{2,1,0:T(8,128)S(1)} %broadcast_select_fusion.2), channel_id=1, source_target_pairs={{0,1},{1,2},{2,3},{3,4},{4,5},{5,6},{6,7},{7,8},{8,9},{9,10},{10,1... | collective-permute-start | bytes 786440 | tf_op jit(solution)/shard_map/while/body/eval_jaxpr/ppermute | solution.py:14
  277.5 4.5 %collective-permute-start.3 = (f32[1,256,256]{2,1,0:T(8,128)S(1)}, f32[1,256,256]{2,1,0:T(8,128)S(1)}, u32[]{:S(2)}, u32[]{:S(2)}) collective-permute-start(f32[1,256,256]{2,1,0:T(8,128)S(1)} %fusion.50), channel_id=1, source_target_pairs={{0,1},{1,2},{2,3},{3,4},{4,5},{5,6},{6,7},{7,8},{8,9},{9,10},{10,1... | collective-permute-start | bytes 786440 | tf_op jit(solution)/shard_map/while/body/eval_jaxpr/ppermute | solution.py:14
  292.0 3.9 %collective-permute-done.7 = f32[1,256,256]{2,1,0:T(8,128)S(1)} collective-permute-done((f32[1,256,256]{2,1,0:T(8,128)S(1)}, f32[1,256,256]{2,1,0:T(8,128)S(1)}, u32[]{:S(2)}, u32[]{:S(2)}) %collective-permute-start.7) | collective-permute-done | bytes 262176 | tf_op jit(solution)/shard_map/ppermute | solution.py:25
  302.6 6.3 %copy.17 = f32[2,512,256,2]{1,0,3,2:T(2,128)} copy(f32[2,512,256,2]{2,0,1,3:T(2,128)} %pad_maximum_fusion.10) | data formatting | bytes 4194304 | tf_op jit(solution)/shard_map/stack | solution.py:56
  308.9 4.0 %bitcast_add_fusion = f32[2,512,512]{1,0,2:T(2,128)} fusion(f32[2,512,512]{1,0,2:T(2,128)S(1)} %copy-done.5, f32[2,512,256,2]{1,0,3,2:T(2,128)} %copy.17), kind=kLoop, calls=%fused_computation.53 | loop fusion | flops 524288 | bytes 6291456 | tf_op jit(solution)/shard_map/add | solution.py:135
  312.9 4.1 %copy.19 = f32[2,512,512]{2,1,0:T(8,128)} copy(f32[2,512,512]{1,0,2:T(2,128)} %bitcast_add_fusion) | data formatting | bytes 4194304
  (179 shorter events, 144.6 us)
Async XLA Ops:
  2.5 24.4 %collective-permute-start.4 = (f32[1,512,512]{2,1,0:T(8,128)S(1)}, f32[1,512,512]{2,1,0:T(8,128)S(1)}, u32[]{:S(2)}, u32[]{:S(2)}) collective-permute-start(f32[1,512,512]{2,1,0:T(8,128)S(1)} %get-tuple-element.106), channel_id=1, source_target_pairs={{1,0},{2,1},{3,2},{4,3},{5,4},{6,5},{7,6},{8,7},{9,8},{10,9},{11,1... | collective-permute-start | bytes 3145736 | tf_op jit(solution)/shard_map/ppermute | solution.py:17
  4.4 27.4 %collective-permute-start.5 = (f32[1,512,512]{2,1,0:T(8,128)S(1)}, f32[1,512,512]{2,1,0:T(8,128)S(1)}, u32[]{:S(2)}, u32[]{:S(2)}) collective-permute-start(f32[1,512,512]{2,1,0:T(8,128)S(1)} %get-tuple-element.105), channel_id=1, source_target_pairs={{0,1},{1,2},{2,3},{3,4},{4,5},{5,6},{6,7},{7,8},{8,9},{9,10},{10,1... | collective-permute-start | bytes 3145736 | tf_op jit(solution)/shard_map/ppermute | solution.py:14
  36.7 16.1 %collective-permute-start.6 = (f32[1,512,512]{2,1,0:T(8,128)S(1)}, f32[1,512,512]{2,1,0:T(8,128)}, u32[]{:S(2)}, u32[]{:S(2)}) collective-permute-start(f32[1,512,512]{2,1,0:T(8,128)S(1)} %slice.164), channel_id=1, source_target_pairs={{0,1},{1,2},{2,3},{3,4},{4,5},{5,6},{6,7},{7,8},{8,9},{9,10},{10,1... | collective-permute-start | bytes 3145736 | tf_op jit(solution)/shard_map/ppermute | solution.py:25
  91.4 10.4 %collective-permute-start = (f32[1,256,256]{2,1,0:T(8,128)S(1)}, f32[1,256,256]{2,1,0:T(8,128)}, u32[]{:S(2)}, u32[]{:S(2)}) collective-permute-start(f32[1,256,256]{2,1,0:T(8,128)S(1)} %broadcast_select_fusion.2), channel_id=1, source_target_pairs={{1,0},{2,1},{3,2},{4,3},{5,4},{6,5},{7,6},{8,7},{9,8},{10,9},{11,1... | collective-permute-start | bytes 786440 | tf_op jit(solution)/shard_map/while/body/eval_jaxpr/ppermute | solution.py:17
  112.8 10.3 %collective-permute-start = (f32[1,256,256]{2,1,0:T(8,128)S(1)}, f32[1,256,256]{2,1,0:T(8,128)}, u32[]{:S(2)}, u32[]{:S(2)}) collective-permute-start(f32[1,256,256]{2,1,0:T(8,128)S(1)} %broadcast_select_fusion.2), channel_id=1, source_target_pairs={{1,0},{2,1},{3,2},{4,3},{5,4},{6,5},{7,6},{8,7},{9,8},{10,9},{11,1... | collective-permute-start | bytes 786440 | tf_op jit(solution)/shard_map/while/body/eval_jaxpr/ppermute | solution.py:17
  114.8 9.5 %collective-permute-start.1 = (f32[1,256,256]{2,1,0:T(8,128)S(1)}, f32[1,256,256]{2,1,0:T(8,128)}, u32[]{:S(2)}, u32[]{:S(2)}) collective-permute-start(f32[1,256,256]{2,1,0:T(8,128)S(1)} %broadcast_select_fusion.2), channel_id=1, source_target_pairs={{0,1},{1,2},{2,3},{3,4},{4,5},{5,6},{6,7},{7,8},{8,9},{9,10},{10,1... | collective-permute-start | bytes 786440 | tf_op jit(solution)/shard_map/while/body/eval_jaxpr/ppermute | solution.py:14
  125.8 8.5 %collective-permute-start.2 = (f32[1,256,256]{2,1,0:T(8,128)S(1)}, f32[1,256,256]{2,1,0:T(8,128)S(1)}, u32[]{:S(2)}, u32[]{:S(2)}) collective-permute-start(f32[1,256,256]{2,1,0:T(8,128)S(1)} %fusion.50), channel_id=1, source_target_pairs={{1,0},{2,1},{3,2},{4,3},{5,4},{6,5},{7,6},{8,7},{9,8},{10,9},{11,1... | collective-permute-start | bytes 786440 | tf_op jit(solution)/shard_map/while/body/eval_jaxpr/ppermute | solution.py:17
  127.8 9.7 %collective-permute-start.3 = (f32[1,256,256]{2,1,0:T(8,128)S(1)}, f32[1,256,256]{2,1,0:T(8,128)S(1)}, u32[]{:S(2)}, u32[]{:S(2)}) collective-permute-start(f32[1,256,256]{2,1,0:T(8,128)S(1)} %fusion.50), channel_id=1, source_target_pairs={{0,1},{1,2},{2,3},{3,4},{4,5},{5,6},{6,7},{7,8},{8,9},{9,10},{10,1... | collective-permute-start | bytes 786440 | tf_op jit(solution)/shard_map/while/body/eval_jaxpr/ppermute | solution.py:14
  137.8 10.3 %collective-permute-start = (f32[1,256,256]{2,1,0:T(8,128)S(1)}, f32[1,256,256]{2,1,0:T(8,128)}, u32[]{:S(2)}, u32[]{:S(2)}) collective-permute-start(f32[1,256,256]{2,1,0:T(8,128)S(1)} %broadcast_select_fusion.2), channel_id=1, source_target_pairs={{1,0},{2,1},{3,2},{4,3},{5,4},{6,5},{7,6},{8,7},{9,8},{10,9},{11,1... | collective-permute-start | bytes 786440 | tf_op jit(solution)/shard_map/while/body/eval_jaxpr/ppermute | solution.py:17
  139.8 9.5 %collective-permute-start.1 = (f32[1,256,256]{2,1,0:T(8,128)S(1)}, f32[1,256,256]{2,1,0:T(8,128)}, u32[]{:S(2)}, u32[]{:S(2)}) collective-permute-start(f32[1,256,256]{2,1,0:T(8,128)S(1)} %broadcast_select_fusion.2), channel_id=1, source_target_pairs={{0,1},{1,2},{2,3},{3,4},{4,5},{5,6},{6,7},{7,8},{8,9},{9,10},{10,1... | collective-permute-start | bytes 786440 | tf_op jit(solution)/shard_map/while/body/eval_jaxpr/ppermute | solution.py:14
  150.9 9.4 %collective-permute-start.2 = (f32[1,256,256]{2,1,0:T(8,128)S(1)}, f32[1,256,256]{2,1,0:T(8,128)S(1)}, u32[]{:S(2)}, u32[]{:S(2)}) collective-permute-start(f32[1,256,256]{2,1,0:T(8,128)S(1)} %fusion.50), channel_id=1, source_target_pairs={{1,0},{2,1},{3,2},{4,3},{5,4},{6,5},{7,6},{8,7},{9,8},{10,9},{11,1... | collective-permute-start | bytes 786440 | tf_op jit(solution)/shard_map/while/body/eval_jaxpr/ppermute | solution.py:17
  152.8 9.6 %collective-permute-start.3 = (f32[1,256,256]{2,1,0:T(8,128)S(1)}, f32[1,256,256]{2,1,0:T(8,128)S(1)}, u32[]{:S(2)}, u32[]{:S(2)}) collective-permute-start(f32[1,256,256]{2,1,0:T(8,128)S(1)} %fusion.50), channel_id=1, source_target_pairs={{0,1},{1,2},{2,3},{3,4},{4,5},{5,6},{6,7},{7,8},{8,9},{9,10},{10,1... | collective-permute-start | bytes 786440 | tf_op jit(solution)/shard_map/while/body/eval_jaxpr/ppermute | solution.py:14
  162.8 10.3 %collective-permute-start = (f32[1,256,256]{2,1,0:T(8,128)S(1)}, f32[1,256,256]{2,1,0:T(8,128)}, u32[]{:S(2)}, u32[]{:S(2)}) collective-permute-start(f32[1,256,256]{2,1,0:T(8,128)S(1)} %broadcast_select_fusion.2), channel_id=1, source_target_pairs={{1,0},{2,1},{3,2},{4,3},{5,4},{6,5},{7,6},{8,7},{9,8},{10,9},{11,1... | collective-permute-start | bytes 786440 | tf_op jit(solution)/shard_map/while/body/eval_jaxpr/ppermute | solution.py:17
  164.7 9.5 %collective-permute-start.1 = (f32[1,256,256]{2,1,0:T(8,128)S(1)}, f32[1,256,256]{2,1,0:T(8,128)}, u32[]{:S(2)}, u32[]{:S(2)}) collective-permute-start(f32[1,256,256]{2,1,0:T(8,128)S(1)} %broadcast_select_fusion.2), channel_id=1, source_target_pairs={{0,1},{1,2},{2,3},{3,4},{4,5},{5,6},{6,7},{7,8},{8,9},{9,10},{10,1... | collective-permute-start | bytes 786440 | tf_op jit(solution)/shard_map/while/body/eval_jaxpr/ppermute | solution.py:14
  175.8 9.4 %collective-permute-start.2 = (f32[1,256,256]{2,1,0:T(8,128)S(1)}, f32[1,256,256]{2,1,0:T(8,128)S(1)}, u32[]{:S(2)}, u32[]{:S(2)}) collective-permute-start(f32[1,256,256]{2,1,0:T(8,128)S(1)} %fusion.50), channel_id=1, source_target_pairs={{1,0},{2,1},{3,2},{4,3},{5,4},{6,5},{7,6},{8,7},{9,8},{10,9},{11,1... | collective-permute-start | bytes 786440 | tf_op jit(solution)/shard_map/while/body/eval_jaxpr/ppermute | solution.py:17
  177.7 9.6 %collective-permute-start.3 = (f32[1,256,256]{2,1,0:T(8,128)S(1)}, f32[1,256,256]{2,1,0:T(8,128)S(1)}, u32[]{:S(2)}, u32[]{:S(2)}) collective-permute-start(f32[1,256,256]{2,1,0:T(8,128)S(1)} %fusion.50), channel_id=1, source_target_pairs={{0,1},{1,2},{2,3},{3,4},{4,5},{5,6},{6,7},{7,8},{8,9},{9,10},{10,1... | collective-permute-start | bytes 786440 | tf_op jit(solution)/shard_map/while/body/eval_jaxpr/ppermute | solution.py:14
  187.7 10.3 %collective-permute-start = (f32[1,256,256]{2,1,0:T(8,128)S(1)}, f32[1,256,256]{2,1,0:T(8,128)}, u32[]{:S(2)}, u32[]{:S(2)}) collective-permute-start(f32[1,256,256]{2,1,0:T(8,128)S(1)} %broadcast_select_fusion.2), channel_id=1, source_target_pairs={{1,0},{2,1},{3,2},{4,3},{5,4},{6,5},{7,6},{8,7},{9,8},{10,9},{11,1... | collective-permute-start | bytes 786440 | tf_op jit(solution)/shard_map/while/body/eval_jaxpr/ppermute | solution.py:17
  189.6 9.5 %collective-permute-start.1 = (f32[1,256,256]{2,1,0:T(8,128)S(1)}, f32[1,256,256]{2,1,0:T(8,128)}, u32[]{:S(2)}, u32[]{:S(2)}) collective-permute-start(f32[1,256,256]{2,1,0:T(8,128)S(1)} %broadcast_select_fusion.2), channel_id=1, source_target_pairs={{0,1},{1,2},{2,3},{3,4},{4,5},{5,6},{6,7},{7,8},{8,9},{9,10},{10,1... | collective-permute-start | bytes 786440 | tf_op jit(solution)/shard_map/while/body/eval_jaxpr/ppermute | solution.py:14
  200.8 9.4 %collective-permute-start.2 = (f32[1,256,256]{2,1,0:T(8,128)S(1)}, f32[1,256,256]{2,1,0:T(8,128)S(1)}, u32[]{:S(2)}, u32[]{:S(2)}) collective-permute-start(f32[1,256,256]{2,1,0:T(8,128)S(1)} %fusion.50), channel_id=1, source_target_pairs={{1,0},{2,1},{3,2},{4,3},{5,4},{6,5},{7,6},{8,7},{9,8},{10,9},{11,1... | collective-permute-start | bytes 786440 | tf_op jit(solution)/shard_map/while/body/eval_jaxpr/ppermute | solution.py:17
  202.7 9.6 %collective-permute-start.3 = (f32[1,256,256]{2,1,0:T(8,128)S(1)}, f32[1,256,256]{2,1,0:T(8,128)S(1)}, u32[]{:S(2)}, u32[]{:S(2)}) collective-permute-start(f32[1,256,256]{2,1,0:T(8,128)S(1)} %fusion.50), channel_id=1, source_target_pairs={{0,1},{1,2},{2,3},{3,4},{4,5},{5,6},{6,7},{7,8},{8,9},{9,10},{10,1... | collective-permute-start | bytes 786440 | tf_op jit(solution)/shard_map/while/body/eval_jaxpr/ppermute | solution.py:14
  212.6 10.3 %collective-permute-start = (f32[1,256,256]{2,1,0:T(8,128)S(1)}, f32[1,256,256]{2,1,0:T(8,128)}, u32[]{:S(2)}, u32[]{:S(2)}) collective-permute-start(f32[1,256,256]{2,1,0:T(8,128)S(1)} %broadcast_select_fusion.2), channel_id=1, source_target_pairs={{1,0},{2,1},{3,2},{4,3},{5,4},{6,5},{7,6},{8,7},{9,8},{10,9},{11,1... | collective-permute-start | bytes 786440 | tf_op jit(solution)/shard_map/while/body/eval_jaxpr/ppermute | solution.py:17
  214.6 9.5 %collective-permute-start.1 = (f32[1,256,256]{2,1,0:T(8,128)S(1)}, f32[1,256,256]{2,1,0:T(8,128)}, u32[]{:S(2)}, u32[]{:S(2)}) collective-permute-start(f32[1,256,256]{2,1,0:T(8,128)S(1)} %broadcast_select_fusion.2), channel_id=1, source_target_pairs={{0,1},{1,2},{2,3},{3,4},{4,5},{5,6},{6,7},{7,8},{8,9},{9,10},{10,1... | collective-permute-start | bytes 786440 | tf_op jit(solution)/shard_map/while/body/eval_jaxpr/ppermute | solution.py:14
  225.7 9.4 %collective-permute-start.2 = (f32[1,256,256]{2,1,0:T(8,128)S(1)}, f32[1,256,256]{2,1,0:T(8,128)S(1)}, u32[]{:S(2)}, u32[]{:S(2)}) collective-permute-start(f32[1,256,256]{2,1,0:T(8,128)S(1)} %fusion.50), channel_id=1, source_target_pairs={{1,0},{2,1},{3,2},{4,3},{5,4},{6,5},{7,6},{8,7},{9,8},{10,9},{11,1... | collective-permute-start | bytes 786440 | tf_op jit(solution)/shard_map/while/body/eval_jaxpr/ppermute | solution.py:17
  227.6 9.6 %collective-permute-start.3 = (f32[1,256,256]{2,1,0:T(8,128)S(1)}, f32[1,256,256]{2,1,0:T(8,128)S(1)}, u32[]{:S(2)}, u32[]{:S(2)}) collective-permute-start(f32[1,256,256]{2,1,0:T(8,128)S(1)} %fusion.50), channel_id=1, source_target_pairs={{0,1},{1,2},{2,3},{3,4},{4,5},{5,6},{6,7},{7,8},{8,9},{9,10},{10,1... | collective-permute-start | bytes 786440 | tf_op jit(solution)/shard_map/while/body/eval_jaxpr/ppermute | solution.py:14
  237.6 10.3 %collective-permute-start = (f32[1,256,256]{2,1,0:T(8,128)S(1)}, f32[1,256,256]{2,1,0:T(8,128)}, u32[]{:S(2)}, u32[]{:S(2)}) collective-permute-start(f32[1,256,256]{2,1,0:T(8,128)S(1)} %broadcast_select_fusion.2), channel_id=1, source_target_pairs={{1,0},{2,1},{3,2},{4,3},{5,4},{6,5},{7,6},{8,7},{9,8},{10,9},{11,1... | collective-permute-start | bytes 786440 | tf_op jit(solution)/shard_map/while/body/eval_jaxpr/ppermute | solution.py:17
  239.5 9.5 %collective-permute-start.1 = (f32[1,256,256]{2,1,0:T(8,128)S(1)}, f32[1,256,256]{2,1,0:T(8,128)}, u32[]{:S(2)}, u32[]{:S(2)}) collective-permute-start(f32[1,256,256]{2,1,0:T(8,128)S(1)} %broadcast_select_fusion.2), channel_id=1, source_target_pairs={{0,1},{1,2},{2,3},{3,4},{4,5},{5,6},{6,7},{7,8},{8,9},{9,10},{10,1... | collective-permute-start | bytes 786440 | tf_op jit(solution)/shard_map/while/body/eval_jaxpr/ppermute | solution.py:14
  250.6 9.4 %collective-permute-start.2 = (f32[1,256,256]{2,1,0:T(8,128)S(1)}, f32[1,256,256]{2,1,0:T(8,128)S(1)}, u32[]{:S(2)}, u32[]{:S(2)}) collective-permute-start(f32[1,256,256]{2,1,0:T(8,128)S(1)} %fusion.50), channel_id=1, source_target_pairs={{1,0},{2,1},{3,2},{4,3},{5,4},{6,5},{7,6},{8,7},{9,8},{10,9},{11,1... | collective-permute-start | bytes 786440 | tf_op jit(solution)/shard_map/while/body/eval_jaxpr/ppermute | solution.py:17
  252.6 9.6 %collective-permute-start.3 = (f32[1,256,256]{2,1,0:T(8,128)S(1)}, f32[1,256,256]{2,1,0:T(8,128)S(1)}, u32[]{:S(2)}, u32[]{:S(2)}) collective-permute-start(f32[1,256,256]{2,1,0:T(8,128)S(1)} %fusion.50), channel_id=1, source_target_pairs={{0,1},{1,2},{2,3},{3,4},{4,5},{5,6},{6,7},{7,8},{8,9},{9,10},{10,1... | collective-permute-start | bytes 786440 | tf_op jit(solution)/shard_map/while/body/eval_jaxpr/ppermute | solution.py:14
  262.5 10.3 %collective-permute-start = (f32[1,256,256]{2,1,0:T(8,128)S(1)}, f32[1,256,256]{2,1,0:T(8,128)}, u32[]{:S(2)}, u32[]{:S(2)}) collective-permute-start(f32[1,256,256]{2,1,0:T(8,128)S(1)} %broadcast_select_fusion.2), channel_id=1, source_target_pairs={{1,0},{2,1},{3,2},{4,3},{5,4},{6,5},{7,6},{8,7},{9,8},{10,9},{11,1... | collective-permute-start | bytes 786440 | tf_op jit(solution)/shard_map/while/body/eval_jaxpr/ppermute | solution.py:17
  264.5 9.5 %collective-permute-start.1 = (f32[1,256,256]{2,1,0:T(8,128)S(1)}, f32[1,256,256]{2,1,0:T(8,128)}, u32[]{:S(2)}, u32[]{:S(2)}) collective-permute-start(f32[1,256,256]{2,1,0:T(8,128)S(1)} %broadcast_select_fusion.2), channel_id=1, source_target_pairs={{0,1},{1,2},{2,3},{3,4},{4,5},{5,6},{6,7},{7,8},{8,9},{9,10},{10,1... | collective-permute-start | bytes 786440 | tf_op jit(solution)/shard_map/while/body/eval_jaxpr/ppermute | solution.py:14
  275.6 9.4 %collective-permute-start.2 = (f32[1,256,256]{2,1,0:T(8,128)S(1)}, f32[1,256,256]{2,1,0:T(8,128)S(1)}, u32[]{:S(2)}, u32[]{:S(2)}) collective-permute-start(f32[1,256,256]{2,1,0:T(8,128)S(1)} %fusion.50), channel_id=1, source_target_pairs={{1,0},{2,1},{3,2},{4,3},{5,4},{6,5},{7,6},{8,7},{9,8},{10,9},{11,1... | collective-permute-start | bytes 786440 | tf_op jit(solution)/shard_map/while/body/eval_jaxpr/ppermute | solution.py:17
  277.5 9.6 %collective-permute-start.3 = (f32[1,256,256]{2,1,0:T(8,128)S(1)}, f32[1,256,256]{2,1,0:T(8,128)S(1)}, u32[]{:S(2)}, u32[]{:S(2)}) collective-permute-start(f32[1,256,256]{2,1,0:T(8,128)S(1)} %fusion.50), channel_id=1, source_target_pairs={{0,1},{1,2},{2,3},{3,4},{4,5},{5,6},{6,7},{7,8},{8,9},{9,10},{10,1... | collective-permute-start | bytes 786440 | tf_op jit(solution)/shard_map/while/body/eval_jaxpr/ppermute | solution.py:14
  (18 other events, 244.1 us)
where the time goes:
time: 319 us; the launch traced here: 317 us
  starting transfers between devices  114 us (36%)
  waiting for transfers between devices  83.7 us (26%)
  local copies, waits for them, and re-layouts  83 us (26%)
  other arithmetic  34.2 us (11%)
    ppermute x17, starting transfers between devices, extended(): lax.ppermute(lax.slice_in_dim(block, block.shape[dim] - width, None, axis...  75.1 us
    ppermute x17, waiting for transfers between devices, extended(): lax.ppermute(lax.slice_in_dim(block, 0, width, axis=dim), axis, backward)  38.7 us
    ppermute x17, starting transfers between devices, extended(): lax.ppermute(lax.slice_in_dim(block, 0, width, axis=dim), axis, backward)  32.7 us
    ppermute x17, waiting for transfers between devices, extended(): lax.ppermute(lax.slice_in_dim(block, block.shape[dim] - width, None, axis...  29.5 us
    slice x2, local copies, waits for them, and re-layouts, restrict_axis(): even_part = lax.slice_in_dim(values, 0, None, 2, direction)  16.7 us
    ppermute x2, waiting for transfers between devices, from_behind(): lax.ppermute(value, axis, [(source, source + steps) for source in range(i...  15.6 us
    slice x3, local copies, waits for them, and re-layouts, restrict_axis(): odd_part = lax.slice_in_dim(values, 1, None, 2, direction)  15.5 us
    select_n x16, other arithmetic, one_sweep(): values = jnp.where(update, (forcing + neighbours) / 6.0, values)  15.4 us
  transfers between devices with their start and end apart: 36, of which 27 were waited for; matrix products, arithmetic and copies ran while one was open for 11% of the time, Pallas kernels for 0%

commit v1 on v0

v1 whole, which is shorter than its diff:
```python
import functools

import jax
import jax.numpy as jnp
import numpy as np
from jax import lax
from jax.experimental import pallas as pl
from jax.experimental.pallas import tpu as pltpu
from jax.sharding import PartitionSpec as P

SWEEPS = 8
AXES = ("grp", "mem")
PAD = 8
LANES = 128
F32 = jnp.float32
BF16 = jnp.bfloat16
HIGHEST = lax.Precision.HIGHEST
VMEM = pl.BlockSpec(memory_space=pltpu.VMEM)
SMEM = pl.BlockSpec(memory_space=pltpu.SMEM)
ANY = pl.BlockSpec(memory_space=pl.ANY)


def restriction(fine):
    matrix = np.zeros((fine // 2, fine))
    for i in range(fine // 2):
        matrix[i, 2 * i] = 0.5
        matrix[i, 2 * i + 1] = 0.25
        if i > 0:
            matrix[i, 2 * i - 1] = 0.25
    return matrix


def neighbour_sum(n):
    return np.eye(n, k=1) + np.eye(n, k=-1)


def prolongation(coarse):
    matrix = np.zeros((2 * coarse, coarse))
    for i in range(coarse):
        matrix[2 * i, i] = 1.0
        matrix[2 * i + 1, i] += 0.5
        matrix[2 * i + 1, min(i + 1, coarse - 1)] += 0.5
    return matrix


def mode_order(n, devices):
    rows = n // devices
    if rows % 2:
        return np.arange(n)
    half = rows // 2
    low = np.arange(n // 2).reshape(devices, half)
    return np.concatenate([low, n - 1 - low], 1).reshape(-1)


def sine_matrix(n):
    index = np.arange(1, n + 1)
    return np.sqrt(2.0 / (n + 1)) * np.sin(np.pi * np.outer(index, index) / (n + 1))


def split3(x):
    high = x.astype(BF16)
    rest = x - high.astype(F32)
    mid = rest.astype(BF16)
    low = (rest - mid.astype(F32)).astype(BF16)
    return high, mid, low


def dot3(parts_ref, first, weights):
    total = None
    for part in (2, 1, 0):
        term = jnp.dot(parts_ref[first + part], weights, preferred_element_type=F32)
        total = term if total is None else total + term
    return total


def fine_kernel(
    pos_ref, pot_hbm, src_hbm, side_ref, end_hbm, rt_ref, gt_ref,
    own_ref, near_ref, far_ref,
    pot, src, end, mid, parts, sem, end_sem,
):
    fine = pot_hbm.shape[1]
    coarse = fine // 2
    position = pos_ref[0]
    last = pos_ref[1]
    copies = []
    for plane in (0, 1):
        for c in range(fine // LANES):
            for which, (hbm, buf) in enumerate(((pot_hbm, pot), (src_hbm, src))):
                copies.append(
                    pltpu.make_async_copy(
                        hbm.at[plane, :, pl.ds(c * LANES, LANES)],
                        buf.at[plane, c, pl.ds(PAD, fine), :],
                        sem.at[len(copies)],
                    )
                )
                copies[-1].start()
    at_end = jnp.where(position == last, 1, 0)
    end_copy = pltpu.make_async_copy(end_hbm.at[at_end], end, end_sem)
    end_copy.start()
    edge = jnp.zeros((2, fine // LANES, PAD, LANES), F32)
    for buf in (pot, src):
        buf[:, :, 0:PAD, :] = edge
        buf[:, :, PAD + fine : PAD + fine + PAD, :] = edge

    not_first = jnp.where(position > 0, 1.0, 0.0).astype(F32)
    block = 64
    waiting = iter(copies)
    for plane in (0, 1):
        for c in range(fine // LANES):
            next(waiting).wait()
            next(waiting).wait()
            columns = pl.ds(c * LANES, LANES)
            for start in range(0, coarse, block):

                def rows(buf, offset):
                    return buf[plane, c, pl.ds(PAD + 2 * start + offset, block, stride=2), :]

                even = rows(pot, 0)
                odds = rows(pot, 1) + rows(pot, -1)
                a = 0.5 * even + 0.25 * odds
                b = (rows(pot, -2) + rows(pot, 2)) + 2.0 * (odds + even)
                if start == 0:
                    row_ids = lax.broadcasted_iota(jnp.int32, (block, LANES), 0)
                    b = b - jnp.where(row_ids == 0, even, 0.0)
                b = b + (0.5 * rows(src, 0) + 0.25 * (rows(src, 1) + rows(src, -1)))
                where = pl.ds(start, block)
                for part, value in enumerate(split3(a)):
                    parts[3 * plane + part, where, columns] = value
                if plane == 0:
                    mid[where, columns] = a
                    combined = 0.5 * b + not_first * a
                else:
                    combined = 0.25 * b + (2.0 * a + mid[where, columns])
                for part, value in enumerate(split3(combined)):
                    parts[6 + 3 * plane + part, where, columns] = value

    down = dot3(parts, 0, rt_ref[...])
    up = dot3(parts, 9, rt_ref[...]) + 0.25 * dot3(parts, 3, gt_ref[...])
    own = dot3(parts, 6, rt_ref[...]) + 0.5 * dot3(parts, 0, gt_ref[...]) + up

    row_ids = lax.broadcasted_iota(jnp.int32, (coarse, coarse), 0)
    col_ids = lax.broadcasted_iota(jnp.int32, (coarse, coarse), 1)
    side = side_ref[0]
    columns = jnp.transpose(jnp.concatenate([side, side], 0))
    own = own + jnp.where(row_ids == 0, side[0:1], 0.0)
    own = own + jnp.where(row_ids == coarse - 1, side[1:2], 0.0)
    own = own + jnp.where(col_ids == 0, columns[:, 2:3], 0.0)
    own = own + jnp.where(col_ids == coarse - 1, columns[:, 3:4], 0.0)
    end_copy.wait()
    beside_end = jnp.logical_or(position == 0, position == last)
    own_ref[...] = own + jnp.where(beside_end, end[...], 0.0)
    is_even = lax.rem(position, 2) == 0
    near_ref[...] = jnp.where(is_even, up, down)
    far_ref[...] = jnp.where(is_even, down, up)


def fine_stage(position, last, potential, source, side_faces, end_faces):
    fine = potential.shape[1]
    coarse = fine // 2
    r = restriction(fine)
    g = -24.0 * r + 4.0 * (r @ neighbour_sum(fine))
    rt = jnp.asarray(r.T, BF16)
    gt = jnp.asarray(g.T, BF16)
    plane = jax.ShapeDtypeStruct((coarse, coarse), F32)
    return pl.pallas_call(
        fine_kernel,
        out_shape=(plane, plane, plane),
        in_specs=[SMEM, ANY, ANY, VMEM, ANY, VMEM, VMEM],
        out_specs=(VMEM, VMEM, VMEM),
        scratch_shapes=[
            pltpu.VMEM((2, fine // LANES, fine + 2 * PAD, LANES), F32),
            pltpu.VMEM((2, fine // LANES, fine + 2 * PAD, LANES), F32),
            pltpu.VMEM((coarse, coarse), F32),
            pltpu.VMEM((coarse, fine), F32),
            pltpu.VMEM((12, coarse, fine), BF16),
            pltpu.SemaphoreType.DMA((4 * (fine // LANES),)),
            pltpu.SemaphoreType.DMA,
        ],
        name="fine_stage",
    )(jnp.stack([position, last]), potential, source, side_faces, end_faces, rt, gt)


def rows_kernel(own_ref, near_ref, far_ref, sine_ref, out_ref):
    devices, _, rows, coarse = out_ref.shape
    sine = sine_ref[...]
    first = jnp.dot(sine, own_ref[...] + near_ref[...], precision=HIGHEST, preferred_element_type=F32)
    out_ref[:, 0] = first.reshape(devices, rows, coarse)
    second = jnp.dot(sine, far_ref[...], precision=HIGHEST, preferred_element_type=F32)
    out_ref[:, 1] = second.reshape(devices, rows, coarse)


def rows_stage(devices, own, near, far):
    coarse = own.shape[0]
    sine = jnp.asarray(sine_matrix(coarse)[mode_order(coarse, devices)], F32)
    return pl.pallas_call(
        rows_kernel,
        out_shape=jax.ShapeDtypeStruct((devices, 2, coarse // devices, coarse), F32),
        in_specs=[VMEM] * 4,
        out_specs=VMEM,
        name="rows_stage",
    )(own, near, far, sine)


def sweep_kernel(pos_ref, in_ref, alpha_ref, out_ref, values, force):
    planes, _, rows, coarse = in_ref.shape
    paired = rows % 2 == 0
    sixth = 1.0 / 6.0
    shape = (rows, coarse)
    lanes = lax.broadcasted_iota(jnp.int32, shape, 1)
    at_left = lanes == 0
    at_right = lanes == coarse - 1
    alpha = jnp.broadcast_to(alpha_ref[0][:, 0:1], shape)
    for k in range(planes):
        total = in_ref[k, 0]
        if k % 2 == 0 and k > 0:
            total = total + in_ref[k - 1, 1]
        if k % 2 == 1 and k + 1 < planes:
            total = total + in_ref[k + 1, 1]
        total = total * sixth
        force[k] = total
        values[k] = total
    values[planes] = jnp.zeros(shape, F32)

    def applied(k, under, here, over):
        left = jnp.where(at_left, 0.0, pltpu.roll(here, 1, 1))
        right = jnp.where(at_right, 0.0, pltpu.roll(here, coarse - 1, 1))
        return (force[k] + alpha * here) + sixth * ((under + over) + (left + right))

    def step(counter, carry):
        under = jnp.zeros(shape, F32)
        here = values[0]
        for k in range(planes):
            over = values[k + 1]
            values[k] = applied(k, under, here, over)
            under, here = here, over
        return carry

    lax.fori_loop(0, 2 * SWEEPS - 2, step, 0)

    under = jnp.zeros(shape, F32)
    here = values[0]
    for k in range(planes):
        over = values[k + 1]
        black = applied(k, under, here, over)
        mean = 0.5 * (here + black)
        swing = 0.5 * (here - black)
        swing = jnp.where((lanes + k) % 2 == 0, swing, -swing)
        if paired:
            fields = [mean + pltpu.roll(swing, rows // 2, 0)]
        else:
            fields = [mean, swing]
        for f, field in enumerate(fields):
            out_ref[k, 2 * f] = field
            if k > 0:
                out_ref[k - 1, 2 * f + 1] = field
            if k == planes - 1:
                out_ref[k, 2 * f + 1] = field
        under, here = here, over


def sweep_stage(position, received):
    devices, _, rows, coarse = received.shape
    fields = 2 if rows % 2 == 0 else 4
    modes = mode_order(coarse, devices) + 1
    alpha = np.cos(np.pi * modes / (coarse + 1)) / 3.0
    table = jnp.asarray(np.tile(alpha.reshape(devices, rows, 1), (1, 1, 128)), F32)
    return pl.pallas_call(
        sweep_kernel,
        out_shape=jax.ShapeDtypeStruct((devices, fields, rows, coarse), F32),
        grid_spec=pltpu.PrefetchScalarGridSpec(
            num_scalar_prefetch=1,
            grid=(1,),
            in_specs=[
                pl.BlockSpec((devices, 2, rows, coarse), lambda i, pos: (0, 0, 0, 0)),
                pl.BlockSpec((1, rows, 128), lambda i, pos: (pos[0], 0, 0)),
            ],
            out_specs=pl.BlockSpec((devices, fields, rows, coarse), lambda i, pos: (0, 0, 0, 0)),
            scratch_shapes=[
                pltpu.VMEM((devices + 1, rows, coarse), F32),
                pltpu.VMEM((devices, rows, coarse), F32),
            ],
        ),
        name="sweep_stage",
    )(position[None], received, table)


def finish_kernel(in_ref, back_ref, pt_ref, pot_hbm, out_hbm, corr_ref, pot, out, parts, wide, pot_sem, out_sem):
    devices, fields, rows, coarse = in_ref.shape
    fine = 2 * coarse
    loads, stores = [], []
    for f in (0, 1):
        for c in range(fine // LANES):
            lanes = pl.ds(c * LANES, LANES)
            at = f * (fine // LANES) + c
            loads.append(pltpu.make_async_copy(pot_hbm.at[f, :, lanes], pot.at[f, c], pot_sem.at[at]))
            stores.append(pltpu.make_async_copy(out.at[f, c], out_hbm.at[f, :, lanes], out_sem.at[at]))
    for load in loads:
        load.start()

    def plane(which):
        total = jnp.dot(
            back_ref[0], in_ref[:, which].reshape(coarse, coarse),
            precision=HIGHEST, preferred_element_type=F32,
        )
        if fields == 4:
            total = total + jnp.dot(
                back_ref[1], in_ref[:, which + 2].reshape(coarse, coarse),
                precision=HIGHEST, preferred_element_type=F32,
            )
        return total

    block = 64
    own = plane(0)
    corr_ref[0] = own
    for f in (0, 1):
        value = own if f == 0 else 0.5 * (corr_ref[0] + plane(1))
        for part, piece in enumerate(split3(value)):
            parts[part] = piece
        wide[0:coarse, :] = dot3(parts, 0, pt_ref[...])
        wide[coarse : coarse + 1, :] = wide[coarse - 1 : coarse, :]
        for c in range(fine // LANES):
            lanes = pl.ds(c * LANES, LANES)
            at = f * (fine // LANES) + c
            loads[at].wait()
            for start in range(0, coarse, block):
                here = wide[pl.ds(start, block), lanes]
                after = wide[pl.ds(start + 1, block), lanes]
                evens = pl.ds(2 * start, block, stride=2)
                odds = pl.ds(2 * start + 1, block, stride=2)
                out[f, c, evens, :] = pot[f, c, evens, :] + here
                out[f, c, odds, :] = pot[f, c, odds, :] + 0.5 * (here + after)
            stores[at].start()
    for store in stores:
        store.wait()


def finish_stage(potential, received):
    devices, fields, rows, coarse = received.shape
    fine = 2 * coarse
    order = mode_order(coarse, devices)
    sine = sine_matrix(coarse)
    back = [sine[order].T]
    if fields == 4:
        back.append(sine[coarse - 1 - order].T)
    return pl.pallas_call(
        finish_kernel,
        out_shape=(
            jax.ShapeDtypeStruct((2, fine, fine), F32),
            jax.ShapeDtypeStruct((1, coarse, coarse), F32),
        ),
        in_specs=[VMEM, VMEM, VMEM, ANY],
        out_specs=(ANY, VMEM),
        scratch_shapes=[
            pltpu.VMEM((2, fine // LANES, fine, LANES), F32),
            pltpu.VMEM((2, fine // LANES, fine, LANES), F32),
            pltpu.VMEM((3, coarse, coarse), BF16),
            pltpu.VMEM((coarse + PAD, fine), F32),
            pltpu.SemaphoreType.DMA((2 * (fine // LANES),)),
            pltpu.SemaphoreType.DMA((2 * (fine // LANES),)),
        ],
        name="finish_stage",
    )(received, jnp.asarray(np.stack(back), F32), jnp.asarray(prolongation(coarse).T, BF16), potential)


def per_device(potential, source, side_faces, end_faces):
    devices = lax.axis_size("grp") * lax.axis_size("mem")
    position = (lax.axis_index("grp") * lax.axis_size("mem") + lax.axis_index("mem")).astype(jnp.int32)
    last = jnp.int32(devices - 1)
    own, near, far = fine_stage(position, last, potential, source, side_faces, end_faces)
    near = lax.ppermute(near, AXES, [(i, i ^ 1) for i in range(devices)])
    sent = rows_stage(devices, own, near, far)
    received = lax.all_to_all(sent, AXES, 0, 0, tiled=True)
    solved = sweep_stage(position, received)
    returned = lax.all_to_all(solved, AXES, 0, 0, tiled=True)
    return finish_stage(potential, returned)


def solution(mesh):
    split = P(AXES, None, None)
    return jax.shard_map(
        per_device,
        mesh=mesh,
        in_specs=(split, split, split, P()),
        out_specs=(split, split),
        check_vma=False,
    )
```

time: 319 us -> 64.6 us (0.20)
  starting transfers between devices: 114 us -> 0.08 us
  local copies, waits for them, and re-layouts: 83 us -> 0.71 us
  waiting for transfers between devices: 83.7 us -> 1.73 us
  blocking collectives: 0 us -> 41.3 us
  other arithmetic: 34.2 us -> 0.66 us
  Pallas kernels: 0 us -> 18.4 us
    ppermute x36 -> x1, starting transfers between devices: 114 us -> 0.08 us  [per_device(): near = lax.ppermute(near, AXES, [(i, i ^ 1) for i in range(devices)])]
    ppermute x36 -> x1, waiting for transfers between devices: 83.7 us -> 1.73 us  [per_device(): near = lax.ppermute(near, AXES, [(i, i ^ 1) for i in range(devices)])]
    slice x48 -> x0, local copies, waits for them, and re-layouts: 55.1 us -> none  [the longest x2 16.7 us: restrict_axis(): even_part = lax.slice_in_dim(values, 0, None, 2, direction)]
    all_to_all x0 -> x2, blocking collectives: none -> 41.3 us  [the longest x1 22.4 us: per_device(): received = lax.all_to_all(sent, AXES, 0, 0, tiled=True)]
    pallas_call x0 -> x4, Pallas kernels: none -> 18.4 us  [the longest x1 5.51 us: fine_stage(): pl.pallas_call(fine_kernel, out_shape=(plane, plane, plane), in_specs=[SM...]
    select_n x16 -> x0, other arithmetic: 15.4 us -> none  [one_sweep(): values = jnp.where(update, (forcing + neighbours) / 6.0, values)]
    concatenate x20 -> x0, local copies, waits for them, and re-layouts: 14.2 us -> none  [the longest x8 6.44 us: side_sum(): left_cells = jnp.concatenate([left_face, values[:, :, :-1]], 2)]
    add x5 -> x0, other arithmetic: 10.3 us -> none  [the longest x3 6.34 us: restrict_axis(): return 0.5 * even_part + 0.25 * (odd_part + earlier)]
  transfers between devices with their start and end apart: 36 -> 1, of which waited for: 27 -> 1; matrix products, arithmetic and copies ran while one was open for 11% -> 0% of each run, Pallas kernels for 0% -> 0%
where the time goes in v1:
time: 64.6 us; the launch traced here: 63.6 us
  blocking collectives  41.3 us (64%)
  Pallas kernels  18.4 us (28%)
  waiting for transfers between devices  1.73 us (3%)
  local copies, waits for them, and re-layouts  0.71 us (1%)
  other arithmetic  0.66 us (1%)
  between operations  0.65 us (1%)
    all_to_all x1, blocking collectives, per_device(): received = lax.all_to_all(sent, AXES, 0, 0, tiled=True)  22.4 us
    all_to_all x1, blocking collectives, per_device(): returned = lax.all_to_all(solved, AXES, 0, 0, tiled=True)  18.9 us
    pallas_call x1, Pallas kernels, fine_stage(): pl.pallas_call(fine_kernel, out_shape=(plane, plane, plane), in_specs=[SM...  5.51 us
    pallas_call x1, Pallas kernels, finish_stage(): pl.pallas_call(finish_kernel, out_shape=(jax.ShapeDtypeStruct((2, fine, f...  5.25 us
    pallas_call x1, Pallas kernels, sweep_stage(): pl.pallas_call(sweep_kernel, out_shape=jax.ShapeDtypeStruct((devices, fie...  5.03 us
    pallas_call x1, Pallas kernels, rows_stage(): pl.pallas_call(rows_kernel, out_shape=jax.ShapeDtypeStruct((devices, 2, c...  2.6 us
    ppermute x1, waiting for transfers between devices, per_device(): near = lax.ppermute(near, AXES, [(i, i ^ 1) for i in range(devices)])  1.73 us
  transfers between devices with their start and end apart: 1, of which 1 were waited for; matrix products, arithmetic and copies ran while one was open for 0% of the time, Pallas kernels for 0%

profile of v1, /device:TPU:1, one launch (start us, length us, event | category | flops | bytes accessed | tf_op | source)
XLA Modules:
  0.0 63.6 jit_solution(843685958664544434)
XLA Ops:
  0.6 0.7 %pad_add_fusion.pos_ref = s32[2]{0:T(128)} fusion(s32[1]{0:T(128)} %constant.24.clone.1, s32[1]{0:T(128)} %bitcast.pos_ref), kind=kLoop, calls=%fused_computation | loop fusion | flops 2 | bytes 16 | tf_op jit(solution)/shard_map/stack | solution.py:180
  1.3 5.5 %fine_stage.1 = (f32[256,256]{1,0:T(8,128)}, f32[256,256]{1,0:T(8,128)}, f32[256,256]{1,0:T(8,128)}) custom-call(s32[2]{0:T(128)} %pad_add_fusion.pos_ref, f32[2,512,512]{2,1,0:T(8,128)} %pot_hbm.3, f32[2,512,512]{2,1,0:T(8,128)} %src_hbm.1, f32[1,4,256]{2,1,0:T(4,128)} %side_ref.1, f32[2,256,256]{2,1,0:T(8,128)} %end_hbm.1, ...), custom_call_target="tpu_custom_call" | custom-call | tf_op jit(solution)/shard_map/fine_stage/pallas_call | solution.py:165
  6.8 0.1 collective-permute-start
  6.9 1.7 %collective-permute-done.near_ref = f32[256,256]{1,0:T(8,128)S(1)} collective-permute-done((f32[256,256]{1,0:T(8,128)}, f32[256,256]{1,0:T(8,128)S(1)}, u32[]{:S(2)}, u32[]{:S(2)}) %collective-permute-start) | collective-permute-done | bytes 262176 | tf_op jit(solution)/shard_map/ppermute | solution.py:370
  8.6 0.0 copy-start
  8.6 0.7 %copy-done = f32[256,256]{1,0:T(8,128)} copy-done((f32[256,256]{1,0:T(8,128)}, f32[256,256]{1,0:T(8,128)S(1)}, u32[]{:S(2)}) %copy-start) | copy-done | bytes 262168
  9.3 2.6 %rows_stage.1 = f32[32,2,8,256]{3,2,1,0:T(8,128)} custom-call(f32[256,256]{1,0:T(8,128)} %get-tuple-element.5.own_ref, f32[256,256]{1,0:T(8,128)} %copy-done, f32[256,256]{1,0:T(8,128)} %get-tuple-element.7.far_ref, f32[256,256]{1,0:T(8,128)} %constant.27.clone.sine_ref), custom_call_target="tpu_custom_call" | custom-call | tf_op jit(solution)/shard_map/rows_stage/pallas_call | solution.py:195
  11.9 22.4 %all_to_all.10.in_ref = f32[32,2,8,256]{3,2,1,0:T(8,128)} all-to-all(f32[32,2,8,256]{3,2,1,0:T(8,128)} %rows_stage.1), channel_id=1, replica_groups=mesh['grp'=8,'mem'=4] {'grp','mem'}, dimensions={0} | all-to-all | bytes 1048576 | tf_op jit(solution)/shard_map/all_to_all | solution.py:372
  34.4 5.0 %sweep_stage.1 = f32[32,2,8,256]{3,2,1,0:T(8,128)} custom-call(s32[1]{0:T(128)} %bitcast.pos_ref, f32[32,2,8,256]{3,2,1,0:T(8,128)} %all_to_all.10.in_ref, f32[32,8,128]{2,1,0:T(8,128)} %constant.28.clone.alpha_ref), custom_call_target="tpu_custom_call" | custom-call | tf_op jit(solution)/shard_map/sweep_stage/pallas_call | solution.py:267
  39.4 18.9 %all_to_all.11.in_ref = f32[32,2,8,256]{3,2,1,0:T(8,128)} all-to-all(f32[32,2,8,256]{3,2,1,0:T(8,128)} %sweep_stage.1), channel_id=1, replica_groups=mesh['grp'=8,'mem'=4] {'grp','mem'}, dimensions={0} | all-to-all | bytes 1048576 | tf_op jit(solution)/shard_map/all_to_all | solution.py:374
  58.3 5.3 %finish_stage.1 = (f32[2,512,512]{2,1,0:T(8,128)}, f32[1,256,256]{2,1,0:T(8,128)}) custom-call(f32[32,2,8,256]{3,2,1,0:T(8,128)} %all_to_all.11.in_ref, f32[1,256,256]{2,1,0:T(8,128)} %constant.29.clone.back_ref, bf16[256,512]{1,0:T(8,128)(2,1)} %constant.30.clone.pt_ref, f32[2,512,512]{2,1,0:T(8,128)} %pot_hbm.3), custom_call_target="tpu_custom_call" | custom-call | tf_op jit(solution)/shard_map/finish_stage/pallas_call | solution.py:345
Async XLA Ops:
  6.8 1.8 %collective-permute-start = (f32[256,256]{1,0:T(8,128)}, f32[256,256]{1,0:T(8,128)S(1)}, u32[]{:S(2)}, u32[]{:S(2)}) collective-permute-start(f32[256,256]{1,0:T(8,128)} %get-tuple-element.6), channel_id=1, source_target_pairs={{0,1},{1,0},{2,3},{3,2},{4,5},{5,4},{6,7},{7,6},{8,9},{9,8},{10,11... | collective-permute-start | bytes 786440 | tf_op jit(solution)/shard_map/ppermute | solution.py:370
  8.6 0.7 %copy-start = (f32[256,256]{1,0:T(8,128)}, f32[256,256]{1,0:T(8,128)S(1)}, u32[]{:S(2)}) copy-start(f32[256,256]{1,0:T(8,128)S(1)} %collective-permute-done.near_ref) | copy-start | bytes 786436

commit v2 on v1

--- a/solution.py
+++ b/solution.py
@@ -1,5 +1,3 @@
-import functools
-
 import jax
 import jax.numpy as jnp
 import numpy as np
@@ -16,8 +14,21 @@
 BF16 = jnp.bfloat16
 HIGHEST = lax.Precision.HIGHEST
 VMEM = pl.BlockSpec(memory_space=pltpu.VMEM)
-SMEM = pl.BlockSpec(memory_space=pltpu.SMEM)
 ANY = pl.BlockSpec(memory_space=pl.ANY)
+HBM = pl.BlockSpec(memory_space=pltpu.HBM)
+
+
+def place():
+    members = lax.axis_size("mem")
+    return lax.axis_index("grp") * members + lax.axis_index("mem"), lax.axis_size("grp") * members
+
+
+def in_hbm(array):
+    return pltpu.with_memory_space_constraint(array, pltpu.HBM)
+
+
+def room(mebibytes):
+    return pltpu.CompilerParams(vmem_limit_bytes=mebibytes << 20)
 
 
 def restriction(fine):
@@ -74,14 +85,14 @@
 
 
 def fine_kernel(
-    pos_ref, pot_hbm, src_hbm, side_ref, end_hbm, rt_ref, gt_ref,
+    pot_hbm, src_hbm, side_hbm, end_hbm, rt_hbm, gt_hbm,
     own_ref, near_ref, far_ref,
-    pot, src, end, mid, parts, sem, end_sem,
+    pot, src, side_buf, end, rt_ref, gt_ref, mid, parts, sem, small_sem,
 ):
     fine = pot_hbm.shape[1]
     coarse = fine // 2
-    position = pos_ref[0]
-    last = pos_ref[1]
+    position, devices = place()
+    last = devices - 1
     copies = []
     for plane in (0, 1):
         for c in range(fine // LANES):
@@ -95,8 +106,14 @@
                 )
                 copies[-1].start()
     at_end = jnp.where(position == last, 1, 0)
-    end_copy = pltpu.make_async_copy(end_hbm.at[at_end], end, end_sem)
-    end_copy.start()
+    small = [
+        pltpu.make_async_copy(rt_hbm, rt_ref, small_sem.at[0]),
+        pltpu.make_async_copy(gt_hbm, gt_ref, small_sem.at[1]),
+        pltpu.make_async_copy(side_hbm, side_buf, small_sem.at[2]),
+        pltpu.make_async_copy(end_hbm.at[at_end], end, small_sem.at[3]),
+    ]
+    for copy in small:
+        copy.start()
     edge = jnp.zeros((2, fine // LANES, PAD, LANES), F32)
     for buf in (pot, src):
         buf[:, :, 0:PAD, :] = edge
@@ -134,19 +151,20 @@
                 for part, value in enumerate(split3(combined)):
                     parts[6 + 3 * plane + part, where, columns] = value
 
+    for copy in small:
+        copy.wait()
     down = dot3(parts, 0, rt_ref[...])
     up = dot3(parts, 9, rt_ref[...]) + 0.25 * dot3(parts, 3, gt_ref[...])
     own = dot3(parts, 6, rt_ref[...]) + 0.5 * dot3(parts, 0, gt_ref[...]) + up
 
     row_ids = lax.broadcasted_iota(jnp.int32, (coarse, coarse), 0)
     col_ids = lax.broadcasted_iota(jnp.int32, (coarse, coarse), 1)
-    side = side_ref[0]
+    side = side_buf[0]
     columns = jnp.transpose(jnp.concatenate([side, side], 0))
     own = own + jnp.where(row_ids == 0, side[0:1], 0.0)
     own = own + jnp.where(row_ids == coarse - 1, side[1:2], 0.0)
     own = own + jnp.where(col_ids == 0, columns[:, 2:3], 0.0)
     own = own + jnp.where(col_ids == coarse - 1, columns[:, 3:4], 0.0)
-    end_copy.wait()
     beside_end = jnp.logical_or(position == 0, position == last)
     own_ref[...] = own + jnp.where(beside_end, end[...], 0.0)
     is_even = lax.rem(position, 2) == 0
@@ -154,7 +172,7 @@
     far_ref[...] = jnp.where(is_even, down, up)
 
 
-def fine_stage(position, last, potential, source, side_faces, end_faces):
+def fine_stage(potential, source, side_faces, end_faces):
     fine = potential.shape[1]
     coarse = fine // 2
     r = restriction(fine)
@@ -165,19 +183,23 @@
     return pl.pallas_call(
         fine_kernel,
         out_shape=(plane, plane, plane),
-        in_specs=[SMEM, ANY, ANY, VMEM, ANY, VMEM, VMEM],
+        in_specs=[HBM] * 6,
         out_specs=(VMEM, VMEM, VMEM),
         scratch_shapes=[
             pltpu.VMEM((2, fine // LANES, fine + 2 * PAD, LANES), F32),
             pltpu.VMEM((2, fine // LANES, fine + 2 * PAD, LANES), F32),
+            pltpu.VMEM((1, 4, coarse), F32),
             pltpu.VMEM((coarse, coarse), F32),
+            pltpu.VMEM((fine, coarse), BF16),
+            pltpu.VMEM((fine, coarse), BF16),
             pltpu.VMEM((coarse, fine), F32),
             pltpu.VMEM((12, coarse, fine), BF16),
             pltpu.SemaphoreType.DMA((4 * (fine // LANES),)),
-            pltpu.SemaphoreType.DMA,
+            pltpu.SemaphoreType.DMA((4,)),
         ],
+        compiler_params=room(20),
         name="fine_stage",
-    )(jnp.stack([position, last]), potential, source, side_faces, end_faces, rt, gt)
+    )(in_hbm(potential), in_hbm(source), in_hbm(side_faces), in_hbm(end_faces), in_hbm(rt), in_hbm(gt))
 
 
 def rows_kernel(own_ref, near_ref, far_ref, sine_ref, out_ref):
@@ -197,11 +219,12 @@
         out_shape=jax.ShapeDtypeStruct((devices, 2, coarse // devices, coarse), F32),
         in_specs=[VMEM] * 4,
         out_specs=VMEM,
+        compiler_params=room(8),
         name="rows_stage",
     )(own, near, far, sine)
 
 
-def sweep_kernel(pos_ref, in_ref, alpha_ref, out_ref, values, force):
+def sweep_kernel(in_ref, alpha_ref, out_ref, values, force):
     planes, _, rows, coarse = in_ref.shape
     paired = rows % 2 == 0
     sixth = 1.0 / 6.0
@@ -209,7 +232,7 @@
     lanes = lax.broadcasted_iota(jnp.int32, shape, 1)
     at_left = lanes == 0
     at_right = lanes == coarse - 1
-    alpha = jnp.broadcast_to(alpha_ref[0][:, 0:1], shape)
+    alpha = jnp.broadcast_to(alpha_ref[place()[0]][:, 0:1], shape)
     for k in range(planes):
         total = in_ref[k, 0]
         if k % 2 == 0 and k > 0:
@@ -258,7 +281,7 @@
         under, here = here, over
 
 
-def sweep_stage(position, received):
+def sweep_stage(received):
     devices, _, rows, coarse = received.shape
     fields = 2 if rows % 2 == 0 else 4
     modes = mode_order(coarse, devices) + 1
@@ -267,21 +290,15 @@
     return pl.pallas_call(
         sweep_kernel,
         out_shape=jax.ShapeDtypeStruct((devices, fields, rows, coarse), F32),
-        grid_spec=pltpu.PrefetchScalarGridSpec(
-            num_scalar_prefetch=1,
-            grid=(1,),
-            in_specs=[
-                pl.BlockSpec((devices, 2, rows, coarse), lambda i, pos: (0, 0, 0, 0)),
-                pl.BlockSpec((1, rows, 128), lambda i, pos: (pos[0], 0, 0)),
-            ],
-            out_specs=pl.BlockSpec((devices, fields, rows, coarse), lambda i, pos: (0, 0, 0, 0)),
-            scratch_shapes=[
-                pltpu.VMEM((devices + 1, rows, coarse), F32),
-                pltpu.VMEM((devices, rows, coarse), F32),
-            ],
-        ),
+        in_specs=[VMEM, VMEM],
+        out_specs=VMEM,
+        scratch_shapes=[
+            pltpu.VMEM((devices + 1, rows, coarse), F32),
+            pltpu.VMEM((devices, rows, coarse), F32),
+        ],
+        compiler_params=room(8 if rows % 8 == 0 else 24),
         name="sweep_stage",
-    )(position[None], received, table)
+    )(received, table)
 
 
 def finish_kernel(in_ref, back_ref, pt_ref, pot_hbm, out_hbm, corr_ref, pot, out, parts, wide, pot_sem, out_sem):
@@ -358,19 +375,18 @@
             pltpu.SemaphoreType.DMA((2 * (fine // LANES),)),
             pltpu.SemaphoreType.DMA((2 * (fine // LANES),)),
         ],
+        compiler_params=room(16),
         name="finish_stage",
     )(received, jnp.asarray(np.stack(back), F32), jnp.asarray(prolongation(coarse).T, BF16), potential)
 
 
 def per_device(potential, source, side_faces, end_faces):
     devices = lax.axis_size("grp") * lax.axis_size("mem")
-    position = (lax.axis_index("grp") * lax.axis_size("mem") + lax.axis_index("mem")).astype(jnp.int32)
-    last = jnp.int32(devices - 1)
-    own, near, far = fine_stage(position, last, potential, source, side_faces, end_faces)
+    own, near, far = fine_stage(potential, source, side_faces, end_faces)
     near = lax.ppermute(near, AXES, [(i, i ^ 1) for i in range(devices)])
     sent = rows_stage(devices, own, near, far)
     received = lax.all_to_all(sent, AXES, 0, 0, tiled=True)
-    solved = sweep_stage(position, received)
+    solved = sweep_stage(received)
     returned = lax.all_to_all(solved, AXES, 0, 0, tiled=True)
     return finish_stage(potential, returned)
 

time: 64.6 us -> 55.7 us (0.86)
  Pallas kernels: 18.4 us -> 12 us
  blocking collectives: 41.3 us -> 40.5 us
  local copies, waits for them, and re-layouts: 0.71 us -> 0.02 us
  other arithmetic: 0.66 us -> 0 us
    pallas_call x1, Pallas kernels: 2.6 us -> 0.61 us  [rows_stage(): pl.pallas_call(rows_kernel, out_shape=jax.ShapeDtypeStruct((devices, 2, c...]
    pallas_call x1, Pallas kernels: 5.03 us -> 3.2 us  [sweep_stage(): pl.pallas_call(sweep_kernel, out_shape=jax.ShapeDtypeStruct((devices, fie...]
    pallas_call x1, Pallas kernels: 5.51 us -> 3.91 us  [fine_stage(): pl.pallas_call(fine_kernel, out_shape=(plane, plane, plane), in_specs=[HB...]
    pallas_call x1, Pallas kernels: 5.25 us -> 4.3 us  [finish_stage(): pl.pallas_call(finish_kernel, out_shape=(jax.ShapeDtypeStruct((2, fine, f...]
    unnamed x2 -> x10, local copies, waits for them, and re-layouts: 0.71 us -> 0.02 us
    another operation x1 -> x0, other arithmetic: 0.66 us -> none  [fine_stage(): jnp.stack([position, last])]
where the time goes in v2:
time: 55.7 us; the launch traced here: 54.9 us
  blocking collectives  40.5 us (73%)
  Pallas kernels  12 us (22%)
  waiting for transfers between devices  1.52 us (3%)
  between operations  0.68 us (1%)
    all_to_all x1, blocking collectives, per_device(): received = lax.all_to_all(sent, AXES, 0, 0, tiled=True)  22.1 us
    all_to_all x1, blocking collectives, per_device(): returned = lax.all_to_all(solved, AXES, 0, 0, tiled=True)  18.4 us
    pallas_call x1, Pallas kernels, finish_stage(): pl.pallas_call(finish_kernel, out_shape=(jax.ShapeDtypeStruct((2, fine, f...  4.3 us
    pallas_call x1, Pallas kernels, fine_stage(): pl.pallas_call(fine_kernel, out_shape=(plane, plane, plane), in_specs=[HB...  3.91 us
    pallas_call x1, Pallas kernels, sweep_stage(): pl.pallas_call(sweep_kernel, out_shape=jax.ShapeDtypeStruct((devices, fie...  3.2 us
    ppermute x1, waiting for transfers between devices, per_device(): near = lax.ppermute(near, AXES, [(i, i ^ 1) for i in range(devices)])  1.52 us
  transfers between devices with their start and end apart: 1, of which 1 were waited for; matrix products, arithmetic and copies ran while one was open for 0% of the time, Pallas kernels for 0%

profile of v2, /device:TPU:1, one launch (start us, length us, event | category | flops | bytes accessed | tf_op | source)
XLA Modules:
  0.0 54.9 jit_solution(6591444539747413922)
XLA Ops:
  0.6 0.0 copy-start.3
  0.6 3.9 %fine_stage.1 = (f32[256,256]{1,0:T(8,128)S(1)}, f32[256,256]{1,0:T(8,128)S(1)}, f32[256,256]{1,0:T(8,128)S(1)}) custom-call(f32[2,512,512]{2,1,0:T(8,128)} %pot_hbm.3, f32[2,512,512]{2,1,0:T(8,128)} %src_hbm.1, f32[1,4,256]{2,1,0:T(4,128)} %side_hbm.1, f32[2,256,256]{2,1,0:T(8,128)} %end_hbm.1, bf16[512,256]{1,0:T(8,128)(2,1)} %constant.12.clone.rt_hbm, ...), custom_call_target="tpu_custom_call" | custom-call | tf_op jit(solution)/shard_map/fine_stage/pallas_call | solution.py:183
  4.6 0.0 copy-start.4
  4.6 0.1 collective-permute-start
  4.7 1.5 %collective-permute-done.near_ref = f32[256,256]{1,0:T(8,128)S(1)} collective-permute-done((f32[256,256]{1,0:T(8,128)S(1)}, f32[256,256]{1,0:T(8,128)S(1)}, u32[]{:S(2)}, u32[]{:S(2)}) %collective-permute-start) | collective-permute-done | bytes 262176 | tf_op jit(solution)/shard_map/ppermute | solution.py:386
  6.2 0.0 copy-done.3
  6.2 0.0 copy-start
  6.2 0.0 copy-start.1
  6.2 0.0 copy-start.2
  6.2 0.6 %rows_stage.1 = f32[32,2,8,256]{3,2,1,0:T(8,128)S(1)} custom-call(f32[256,256]{1,0:T(8,128)S(1)} %get-tuple-element.5.own_ref, f32[256,256]{1,0:T(8,128)S(1)} %collective-permute-done.near_ref, f32[256,256]{1,0:T(8,128)S(1)} %get-tuple-element.7.far_ref, f32[256,256]{1,0:T(8,128)S(1)} %copy-done.3), custom_call_target="tpu_custom_call" | custom-call | tf_op jit(solution)/shard_map/rows_stage/pallas_call | solution.py:217
  6.8 22.1 %all_to_all.10.in_ref = f32[32,2,8,256]{3,2,1,0:T(8,128)S(1)} all-to-all(f32[32,2,8,256]{3,2,1,0:T(8,128)S(1)} %rows_stage.1), channel_id=1, replica_groups=mesh['grp'=8,'mem'=4] {'grp','mem'}, dimensions={0} | all-to-all | bytes 1048576 | tf_op jit(solution)/shard_map/all_to_all | solution.py:388
  28.9 0.0 copy-done.4
  28.9 3.2 %sweep_stage.1 = f32[32,2,8,256]{3,2,1,0:T(8,128)S(1)} custom-call(f32[32,2,8,256]{3,2,1,0:T(8,128)S(1)} %all_to_all.10.in_ref, f32[32,8,128]{2,1,0:T(8,128)S(1)} %copy-done.4), custom_call_target="tpu_custom_call" | custom-call | tf_op jit(solution)/shard_map/sweep_stage/pallas_call | solution.py:290
  32.1 18.4 %all_to_all.11.in_ref = f32[32,2,8,256]{3,2,1,0:T(8,128)S(1)} all-to-all(f32[32,2,8,256]{3,2,1,0:T(8,128)S(1)} %sweep_stage.1), channel_id=1, replica_groups=mesh['grp'=8,'mem'=4] {'grp','mem'}, dimensions={0} | all-to-all | bytes 1048576 | tf_op jit(solution)/shard_map/all_to_all | solution.py:390
  50.5 0.0 copy-done
  50.5 0.0 copy-done.1
  50.5 0.0 copy-done.2
  50.6 4.3 %finish_stage.1 = (f32[2,512,512]{2,1,0:T(8,128)}, f32[1,256,256]{2,1,0:T(8,128)}) custom-call(f32[32,2,8,256]{3,2,1,0:T(8,128)S(1)} %all_to_all.11.in_ref, f32[1,256,256]{2,1,0:T(8,128)S(1)} %copy-done.2, bf16[256,512]{1,0:T(8,128)(2,1)S(1)} %copy-done.1, f32[2,512,512]{2,1,0:T(8,128)S(1)} %copy-done), custom_call_target="tpu_custom_call" | custom-call | tf_op jit(solution)/shard_map/finish_stage/pallas_call | solution.py:362
Async XLA Ops:
  0.6 5.5 %copy-start.3 = (f32[256,256]{1,0:T(8,128)S(1)}, f32[256,256]{1,0:T(8,128)}, u32[]{:S(2)}) copy-start(f32[256,256]{1,0:T(8,128)} %constant.14.clone.sine_ref) | copy-start | bytes 786436
  4.6 24.4 %copy-start.4 = (f32[32,8,128]{2,1,0:T(8,128)S(1)}, f32[32,8,128]{2,1,0:T(8,128)}, u32[]{:S(2)}) copy-start(f32[32,8,128]{2,1,0:T(8,128)} %constant.15.clone.alpha_ref) | copy-start | bytes 393220
  4.6 1.6 %collective-permute-start = (f32[256,256]{1,0:T(8,128)S(1)}, f32[256,256]{1,0:T(8,128)S(1)}, u32[]{:S(2)}, u32[]{:S(2)}) collective-permute-start(f32[256,256]{1,0:T(8,128)S(1)} %get-tuple-element.6), channel_id=1, source_target_pairs={{0,1},{1,0},{2,3},{3,2},{4,5},{5,4},{6,7},{7,6},{8,9},{9,8},{10,11... | collective-permute-start | bytes 786440 | tf_op jit(solution)/shard_map/ppermute | solution.py:386
  6.2 44.4 %copy-start = (f32[2,512,512]{2,1,0:T(8,128)S(1)}, f32[2,512,512]{2,1,0:T(8,128)}, u32[]{:S(2)}) copy-start(f32[2,512,512]{2,1,0:T(8,128)} %pot_hbm.3) | copy-start | bytes 6291460
  6.2 44.4 %copy-start.1 = (bf16[256,512]{1,0:T(8,128)(2,1)S(1)}, bf16[256,512]{1,0:T(8,128)(2,1)}, u32[]{:S(2)}) copy-start(bf16[256,512]{1,0:T(8,128)(2,1)} %constant.17.clone.pt_ref) | copy-start | bytes 786436
  6.2 44.4 %copy-start.2 = (f32[1,256,256]{2,1,0:T(8,128)S(1)}, f32[1,256,256]{2,1,0:T(8,128)}, u32[]{:S(2)}) copy-start(f32[1,256,256]{2,1,0:T(8,128)} %constant.16.clone.back_ref) | copy-start | bytes 786436

commit v3 on v2

v3 whole, which is shorter than its diff:
```python
import jax
import jax.numpy as jnp
import numpy as np
from jax import lax
from jax.experimental import pallas as pl
from jax.experimental.pallas import tpu as pltpu
from jax.sharding import PartitionSpec as P

SWEEPS = 8
AXES = ("grp", "mem")
PAD = 8
LANES = 128
F32 = jnp.float32
BF16 = jnp.bfloat16
VMEM = pl.BlockSpec(memory_space=pltpu.VMEM)
ANY = pl.BlockSpec(memory_space=pl.ANY)
HBM = pl.BlockSpec(memory_space=pltpu.HBM)


def place():
    members = lax.axis_size("mem")
    return lax.axis_index("grp") * members + lax.axis_index("mem"), lax.axis_size("grp") * members


def in_hbm(array):
    return pltpu.with_memory_space_constraint(array, pltpu.HBM)


def room(mebibytes):
    return pltpu.CompilerParams(vmem_limit_bytes=mebibytes << 20)


def restriction(fine):
    matrix = np.zeros((fine // 2, fine))
    for i in range(fine // 2):
        matrix[i, 2 * i] = 0.5
        matrix[i, 2 * i + 1] = 0.25
        if i > 0:
            matrix[i, 2 * i - 1] = 0.25
    return matrix


def neighbour_sum(n):
    return np.eye(n, k=1) + np.eye(n, k=-1)


def prolongation(coarse):
    matrix = np.zeros((2 * coarse, coarse))
    for i in range(coarse):
        matrix[2 * i, i] = 1.0
        matrix[2 * i + 1, i] += 0.5
        matrix[2 * i + 1, min(i + 1, coarse - 1)] += 0.5
    return matrix


def mode_order(n, devices):
    rows = n // devices
    if rows % 2:
        return np.arange(n)
    half = rows // 2
    low = np.arange(n // 2).reshape(devices, half)
    return np.concatenate([low, n - 1 - low], 1).reshape(-1)


def sine_matrix(n):
    index = np.arange(1, n + 1)
    return np.sqrt(2.0 / (n + 1)) * np.sin(np.pi * np.outer(index, index) / (n + 1))


def split3(x):
    high = x.astype(BF16)
    rest = x - high.astype(F32)
    mid = rest.astype(BF16)
    low = (rest - mid.astype(F32)).astype(BF16)
    return high, mid, low


def split_matrix(matrix, count):
    parts, rest = [], np.asarray(matrix, np.float64)
    for _ in range(count):
        parts.append(rest.astype(jnp.bfloat16))
        rest = rest - parts[-1].astype(np.float64)
    return jnp.asarray(np.stack(parts))


def dot6(matrix_ref, x):
    x = split3(x)
    total = None
    for left, right in ((2, 0), (0, 2), (1, 1), (1, 0), (0, 1), (0, 0)):
        term = jnp.dot(matrix_ref[left], x[right], preferred_element_type=F32)
        total = term if total is None else total + term
    return total


def dot3(parts_ref, first, weights):
    total = None
    for part in (2, 1, 0):
        term = jnp.dot(parts_ref[first + part], weights, preferred_element_type=F32)
        total = term if total is None else total + term
    return total


def restricted_rows(buf, index, start, block):
    def rows(offset):
        return buf[index + (pl.ds(PAD + 2 * start + offset, block, stride=2), slice(None))]

    return rows


def beside(parts, lanes):
    count = len(parts)
    after = [pltpu.roll(part, 1, 1) for part in parts]
    before = [pltpu.roll(part, LANES - 1, 1) for part in parts]
    sums = []
    for c in range(count):
        left = jnp.where(lanes == 0, after[c - 1] if c > 0 else 0.0, after[c])
        right = jnp.where(lanes == LANES - 1, before[c + 1] if c + 1 < count else 0.0, before[c])
        sums.append(left + right)
    return sums


def sent_kernel(
    pot_hbm, src_hbm, rt_hbm,
    near_ref, far_ref, rest_ref, pot, src0,
    src, rt_ref, mid, parts, sem, small_sem,
):
    fine = pot_hbm.shape[1]
    coarse = fine // 2
    blocks = fine // LANES
    cut = fine // 2 + 2 * PAD
    position, _ = place()
    groups = []
    for hbm, plane, buf, index in (
        (pot_hbm, 0, pot, (0,)), (pot_hbm, 1, pot, (1,)), (src_hbm, 1, src, ()), (src_hbm, 0, src0, ()),
    ):
        for first, size in ((0, cut), (cut, fine - cut)):
            group = []
            for c in range(blocks):
                group.append(
                    pltpu.make_async_copy(
                        hbm.at[plane, pl.ds(first, size), pl.ds(c * LANES, LANES)],
                        buf.at[index + (c, pl.ds(PAD + first, size), slice(None))],
                        sem.at[len(groups) * blocks + c],
                    )
                )
            groups.append(group)
    for group in groups[:2]:
        for copy in group:
            copy.start()
    matrix = pltpu.make_async_copy(rt_hbm, rt_ref, small_sem)
    matrix.start()
    for group in groups[2:]:
        for copy in group:
            copy.start()
    edge = jnp.zeros((blocks, PAD, LANES), F32)
    for ref in (pot.at[0], pot.at[1], src, src0):
        ref[:, 0:PAD, :] = edge
        ref[:, PAD + fine : PAD + fine + PAD, :] = edge

    half_not_first = jnp.where(position > 0, 0.5, 0.0).astype(F32)
    block = 32
    lanes = lax.broadcasted_iota(jnp.int32, (block, LANES), 1)
    row_ids = lax.broadcasted_iota(jnp.int32, (block, LANES), 0)

    def chunk(plane, start):
        where = pl.ds(start, block)
        quad, around = [], []
        for c in range(blocks):
            rows = restricted_rows(pot, (plane, c), start, block)
            even = rows(0)
            twice = even + even
            quad.append(twice + (rows(1) + rows(-1)))
            outer = rows(-2) + rows(2)
            if start == 0:
                outer = outer - jnp.where(row_ids == 0, even, 0.0)
            around.append(outer - twice)
        sums = beside(quad, lanes)
        for c in range(blocks):
            columns = pl.ds(c * LANES, LANES)
            whole = (around[c] + sums[c]) - 4.0 * quad[c]
            if plane == 0:
                mid[where, columns] = quad[c]
                rest_ref[where, columns] = whole + half_not_first * quad[c]
                value = quad[c]
            else:
                rows = restricted_rows(src, (c,), start, block)
                even = rows(0)
                source = (even + even) + (rows(1) + rows(-1))
                value = (whole + 0.25 * source) + ((quad[c] + quad[c]) + mid[where, columns])
            for part, piece in enumerate(split3(value)):
                parts[3 * plane + part, where, columns] = piece

    starts = range(0, coarse, block)
    for start in starts:
        if start == 0 or start == coarse // 2:
            for copy in groups[0 if start == 0 else 1]:
                copy.wait()
        chunk(0, start)
    for group in groups[2:6]:
        for copy in group:
            copy.wait()
    matrix.wait()
    down = 0.25 * dot3(parts, 0, rt_ref[...])
    for start in starts:
        chunk(1, start)
    up = 0.25 * dot3(parts, 3, rt_ref[...])
    is_even = lax.rem(position, 2) == 0
    near_ref[...] = jnp.where(is_even, up, down)
    far_ref[...] = jnp.where(is_even, down, up)
    for group in groups[6:]:
        for copy in group:
            copy.wait()


def restriction_matrix(fine):
    return jnp.asarray(restriction(fine).T, BF16)


def sent_stage(potential, source):
    fine = potential.shape[1]
    coarse = fine // 2
    blocks = fine // LANES
    plane = jax.ShapeDtypeStruct((coarse, coarse), F32)
    held = (blocks, fine + 2 * PAD, LANES)
    return pl.pallas_call(
        sent_kernel,
        out_shape=(
            plane,
            plane,
            jax.ShapeDtypeStruct((coarse, fine), F32),
            jax.ShapeDtypeStruct((2,) + held, F32),
            jax.ShapeDtypeStruct(held, F32),
        ),
        in_specs=[HBM] * 3,
        out_specs=(VMEM,) * 5,
        scratch_shapes=[
            pltpu.VMEM(held, F32),
            pltpu.VMEM((fine, coarse), BF16),
            pltpu.VMEM((coarse, fine), F32),
            pltpu.VMEM((6, coarse, fine), BF16),
            pltpu.SemaphoreType.DMA((8 * blocks,)),
            pltpu.SemaphoreType.DMA,
        ],
        compiler_params=room(20),
        name="sent_stage",
    )(in_hbm(potential), in_hbm(source), in_hbm(restriction_matrix(fine)))


def own_kernel(src0, rest_ref, near_ref, far_ref, side_ref, end_hbm, rt_ref, sine_ref, own_ref, sent_ref, end, parts, end_sem):
    coarse, fine = rest_ref.shape
    position, devices = place()
    last = devices - 1
    end_copy = pltpu.make_async_copy(end_hbm.at[jnp.where(position == last, 1, 0)], end, end_sem)
    end_copy.start()
    block = 64
    for c in range(fine // LANES):
        columns = pl.ds(c * LANES, LANES)
        for start in range(0, coarse, block):
            where = pl.ds(start, block)
            rows = restricted_rows(src0, (c,), start, block)
            even = rows(0)
            value = rest_ref[where, columns] + 0.25 * ((even + even) + (rows(1) + rows(-1)))
            for part, piece in enumerate(split3(value)):
                parts[part, where, columns] = piece
    sent_ref[...] = dot6(sine_ref, far_ref[...])
    up = jnp.where(lax.rem(position, 2) == 0, near_ref[...], far_ref[...])
    own_ref[...] = 0.5 * dot3(parts, 0, rt_ref[...]) + up
    side = side_ref[0]
    columns = jnp.transpose(jnp.concatenate([side, side], 0))
    own_ref[0:1, :] += side[0:1]
    own_ref[coarse - 1 : coarse, :] += side[1:2]
    lanes = lax.broadcasted_iota(jnp.int32, (coarse, LANES), 1)
    own_ref[:, 0:LANES] += jnp.where(lanes == 0, columns[:, 2:3], 0.0)
    own_ref[:, coarse - LANES : coarse] += jnp.where(lanes == LANES - 1, columns[:, 3:4], 0.0)
    end_copy.wait()

    @pl.when(jnp.logical_or(position == 0, position == last))
    def _():
        own_ref[...] += end[...]


def own_stage(devices, src0, rest, near, far, side_faces, end_faces):
    coarse, fine = rest.shape
    return pl.pallas_call(
        own_kernel,
        out_shape=(
            jax.ShapeDtypeStruct((coarse, coarse), F32),
            jax.ShapeDtypeStruct((coarse, coarse), F32),
        ),
        in_specs=[VMEM] * 5 + [HBM, VMEM, VMEM],
        out_specs=(VMEM, VMEM),
        scratch_shapes=[
            pltpu.VMEM((coarse, coarse), F32),
            pltpu.VMEM((3, coarse, fine), BF16),
            pltpu.SemaphoreType.DMA,
        ],
        compiler_params=room(12),
        name="own_stage",
    )(src0, rest, near, far, side_faces, in_hbm(end_faces), restriction_matrix(fine), row_transform(coarse, devices))


def rows_kernel(own_ref, near_ref, sine_ref, far_ref, out_ref):
    devices, _, rows, coarse = out_ref.shape
    first = dot6(sine_ref, own_ref[...] + near_ref[...])
    out_ref[:, 0] = first.reshape(devices, rows, coarse)
    out_ref[:, 1] = far_ref[...].reshape(devices, rows, coarse)


def row_transform(coarse, devices):
    return split_matrix(sine_matrix(coarse)[mode_order(coarse, devices)], 3)


def rows_stage(devices, own, near, far):
    coarse = own.shape[0]
    shape = (devices, 2, coarse // devices, coarse)
    return pl.pallas_call(
        rows_kernel,
        out_shape=jax.ShapeDtypeStruct(shape, F32),
        in_specs=[VMEM] * 4,
        out_specs=VMEM,
        compiler_params=room(8),
        name="rows_stage",
    )(own, near, row_transform(coarse, devices), far)


def sweep_kernel(in_ref, alpha_ref, out_ref, values, force):
    planes, _, rows, coarse = in_ref.shape
    paired = rows % 2 == 0
    sixth = 1.0 / 6.0
    shape = (rows, LANES)
    count = coarse // LANES
    lanes = lax.broadcasted_iota(jnp.int32, shape, 1)
    alpha = jnp.broadcast_to(alpha_ref[place()[0]][:, 0:1], shape)
    zero = [jnp.zeros(shape, F32)] * count
    columns = [pl.ds(c * LANES, LANES) for c in range(count)]
    for k in range(planes):
        total = in_ref[k, 0]
        if k % 2 == 0 and k > 0:
            total = total + in_ref[k - 1, 1]
        if k % 2 == 1 and k + 1 < planes:
            total = total + in_ref[k + 1, 1]
        total = total * sixth
        force[k] = total
        values[k] = total

    def held(k):
        return [values[k, :, columns[c]] for c in range(count)]

    def applied(k, under, here, over):
        sums = beside(here, lanes)
        return [
            (force[k, :, columns[c]] + alpha * here[c]) + sixth * ((under[c] + over[c]) + sums[c])
            for c in range(count)
        ]

    def step(counter, carry):
        under, here = zero, held(0)
        for k in range(planes):
            over = held(k + 1) if k + 1 < planes else zero
            for c, value in enumerate(applied(k, under, here, over)):
                values[k, :, columns[c]] = value
            under, here = here, over
        return carry

    lax.fori_loop(0, 2 * SWEEPS - 2, step, 0)

    under, here = zero, held(0)
    for k in range(planes):
        over = held(k + 1) if k + 1 < planes else zero
        black = applied(k, under, here, over)
        for c in range(count):
            mean = 0.5 * (here[c] + black[c])
            swing = 0.5 * (here[c] - black[c])
            swing = jnp.where((lanes + k) % 2 == 0, swing, -swing)
            fields = [mean + pltpu.roll(swing, rows // 2, 0)] if paired else [mean, swing]
            for f, field in enumerate(fields):
                store_solved(out_ref, planes, k, c, f * rows, field)
        under, here = here, over


def packed_sweep_kernel(in_ref, alpha_ref, out_ref, red, black, red_force, black_force):
    planes, _, rows, coarse = in_ref.shape
    slots = planes // 2
    half = rows // 2
    sixth = 1.0 / 6.0
    shape = (rows, LANES)
    count = coarse // LANES
    lanes = lax.broadcasted_iota(jnp.int32, shape, 1)
    first = lax.broadcasted_iota(jnp.int32, shape, 0) < half
    alpha = alpha_ref[place()[0]]
    zero = jnp.zeros(shape, F32)
    columns = [pl.ds(c * LANES, LANES) for c in range(count)]
    signs = [jnp.where((lanes + q) % 2 == 0, 1.0, -1.0) for q in (0, 1)]

    def forcing(k, c):
        total = in_ref[k, 0, :, columns[c]]
        if k % 2 == 0 and k > 0:
            total = total + in_ref[k - 1, 1, :, columns[c]]
        if k % 2 == 1 and k + 1 < planes:
            total = total + in_ref[k + 1, 1, :, columns[c]]
        return total

    def swapped(x):
        return pltpu.roll(x, half, 0)

    for q in range(slots):
        for c in range(count):
            one, two = forcing(q, c), forcing(q + slots, c)
            low = jnp.where(first, one, swapped(two)) * (0.5 * sixth)
            high = jnp.where(first, swapped(one), two) * (0.5 * sixth * signs[q % 2])
            red_force[q, :, columns[c]] = low + high
            black_force[q, :, columns[c]] = low - high
            red[q, :, columns[c]] = low + high

    def update(target, force, other):
        def held(q):
            return [other[q, :, columns[c]] for c in range(count)]

        here, end = held(0), held(slots - 1)
        under = [jnp.where(first, zero, swapped(x)) for x in end]
        beyond = [jnp.where(first, swapped(x), zero) for x in here]
        for q in range(slots):
            over = held(q + 1) if q + 1 < slots else beyond
            sums = beside(here, lanes)
            for c in range(count):
                target[q, :, columns[c]] = (force[q, :, columns[c]] + alpha * here[c]) + sixth * (
                    (under[c] + over[c]) + sums[c]
                )
            under, here = here, over

    update(black, black_force, red)

    def sweep(counter, carry):
        update(red, red_force, black)
        update(black, black_force, red)
        return carry

    lax.fori_loop(0, SWEEPS - 1, sweep, 0)

    for q in range(slots):
        for c in range(count):
            on_red, on_black = red[q, :, columns[c]], black[q, :, columns[c]]
            low = on_red + on_black
            high = signs[q % 2] * (on_red - on_black)
            store_solved(out_ref, planes, q, c, 0, jnp.where(first, low, swapped(high)))
            store_solved(out_ref, planes, q + slots, c, 0, jnp.where(first, swapped(low), high))


def store_solved(out_ref, planes, k, c, first_row, field):
    rows = field.shape[0]
    coarse = out_ref.shape[2] // 3 * 2
    where = pl.ds(first_row, rows)
    out_ref[k, where, pl.ds(c * LANES, LANES)] = field
    if k >= 2 and k % 2 == 0 or k == planes - 1:
        half = coarse // 2
        before = k - 2 if k < planes - 1 else k - 1
        side = c * LANES // half
        out_ref[before + side, where, pl.ds(coarse + c * LANES - side * half, LANES)] = field


def sweep_stage(received):
    devices, _, rows, coarse = received.shape
    packed = rows == 8 and devices % 4 == 0
    fields = 1 if rows % 2 == 0 else 2
    modes = (mode_order(coarse, devices) + 1).reshape(devices, rows)
    if packed:
        modes = np.concatenate([modes[:, : rows // 2]] * 2, 1)
    alpha = np.cos(np.pi * modes / (coarse + 1)) / 3.0
    table = jnp.asarray(np.tile(alpha[:, :, None], (1, 1, LANES)), F32)
    shape = (devices // 2 if packed else devices, rows, coarse)
    return pl.pallas_call(
        packed_sweep_kernel if packed else sweep_kernel,
        out_shape=jax.ShapeDtypeStruct((devices, fields * rows, coarse + coarse // 2), F32),
        in_specs=[VMEM, VMEM],
        out_specs=VMEM,
        scratch_shapes=[pltpu.VMEM(shape, F32)] * (4 if packed else 2),
        compiler_params=room(8 if rows % 8 == 0 else 24),
        name="sweep_stage",
    )(received, table)


def back_kernel(in_ref, back_ref, corr_ref, swap_ref, extra_ref):
    devices, held, width = in_ref.shape
    coarse = corr_ref.shape[0]
    rows = coarse // devices
    fields = held // rows
    position, _ = place()

    def product(first, size):
        total = None
        for f in range(fields):
            part = in_ref[:, f * rows : (f + 1) * rows, first : first + size].reshape(coarse, size)
            high = part.astype(BF16)
            low = (part - high.astype(F32)).astype(BF16)
            for left, right in ((1, high), (0, low), (0, high)):
                term = jnp.dot(back_ref[2 * f + left], right, preferred_element_type=F32)
                total = term if total is None else total + term
        return total

    both = product(0, width)
    own, extra = both[:, 0:coarse], both[:, coarse:]
    corr_ref[...] = own
    extra_ref[...] = extra
    is_even = lax.rem(position, 2) == 0

    @pl.when(is_even)
    def _():
        swap_ref[:, 0 : width - coarse] = extra
        swap_ref[:, width - coarse :] = extra

    @pl.when(jnp.logical_not(is_even))
    def _():
        swap_ref[...] = own


def back_stage(coarse, received):
    devices, held, width = received.shape
    rows = coarse // devices
    order = mode_order(coarse, devices)
    sine = sine_matrix(coarse)
    back = [sine[order].T]
    if held > rows:
        back.append(sine[coarse - 1 - order].T)
    return pl.pallas_call(
        back_kernel,
        out_shape=(
            jax.ShapeDtypeStruct((coarse, coarse), F32),
            jax.ShapeDtypeStruct((coarse, coarse), F32),
            jax.ShapeDtypeStruct((coarse, width - coarse), F32),
        ),
        in_specs=[VMEM, VMEM],
        out_specs=(VMEM,) * 3,
        compiler_params=room(8),
        name="back_stage",
    )(received, jnp.concatenate([split_matrix(matrix, 2) for matrix in back]))


def add_prolonged(value, pt_ref, pot, plane, out_hbm, out, parts, wide, sem):
    coarse = value.shape[0]
    fine = 2 * coarse
    block = 64
    for part, piece in enumerate(split3(value)):
        parts[part] = piece
    stores = []
    for n in range(0, fine, coarse):
        wide[0:coarse, :] = dot3(parts, 0, pt_ref[:, n : n + coarse])
        wide[coarse : coarse + 1, :] = wide[coarse - 1 : coarse, :]
        for c in range(n // LANES, (n + coarse) // LANES):
            lanes = pl.ds(c * LANES - n, LANES)
            for start in range(0, coarse, block):
                here = wide[pl.ds(start, block), lanes]
                after = wide[pl.ds(start + 1, block), lanes]
                for odd, value in ((0, here), (1, 0.5 * (here + after))):
                    old = pot[plane, c, pl.ds(PAD + 2 * start + odd, block, stride=2), :]
                    out[c, pl.ds(2 * start + odd, block, stride=2), :] = old + value
            stores.append(
                pltpu.make_async_copy(out.at[c], out_hbm.at[plane, :, pl.ds(c * LANES, LANES)], sem.at[c])
            )
            stores[-1].start()
    for store in stores:
        store.wait()


def even_kernel(own_ref, pt_ref, pot, out_hbm, corr_hbm, out, parts, wide, sem, corr_sem):
    copy = pltpu.make_async_copy(own_ref, corr_hbm.at[0], corr_sem)
    copy.start()
    add_prolonged(own_ref[...], pt_ref, pot, 0, out_hbm, out, parts, wide, sem)
    copy.wait()


def odd_kernel(own_ref, swapped_ref, extra_ref, pt_ref, pot, held_hbm, out_hbm, out, parts, wide, sem):
    position, devices = place()
    own = own_ref[...]
    swapped = swapped_ref[...]
    half = extra_ref.shape[1]
    is_even = lax.rem(position, 2) == 0
    right = jnp.where(is_even, swapped[:, half:], extra_ref[...])
    above = jnp.concatenate([swapped[:, :half], right], 1)
    above = jnp.where(position == devices - 1, own, above)
    add_prolonged(0.5 * (own + above), pt_ref, pot, 1, out_hbm, out, parts, wide, sem)


def plane_stage(name, kernel, operands, pot, held):
    coarse = operands[0].shape[0]
    fine = 2 * coarse
    pt = jnp.asarray(prolongation(coarse).T, BF16)
    arguments = list(operands) + [pt, pot]
    specs = [VMEM] * len(arguments)
    scratch = [
        pltpu.VMEM((fine // LANES, fine, LANES), F32),
        pltpu.VMEM((3, coarse, coarse), BF16),
        pltpu.VMEM((coarse + PAD, coarse), F32),
        pltpu.SemaphoreType.DMA((fine // LANES,)),
    ]
    outs = [jax.ShapeDtypeStruct((2, fine, fine), F32)]
    if held is None:
        outs.append(jax.ShapeDtypeStruct((1, coarse, coarse), F32))
        scratch.append(pltpu.SemaphoreType.DMA)
    else:
        arguments.append(held)
        specs.append(ANY)
    return pl.pallas_call(
        kernel,
        out_shape=outs,
        in_specs=specs,
        out_specs=[HBM] * len(outs),
        scratch_shapes=scratch,
        input_output_aliases={} if held is None else {len(arguments) - 1: 0},
        compiler_params=room(8),
        name=name,
    )(*arguments)


def per_device(potential, source, side_faces, end_faces):
    devices = lax.axis_size("grp") * lax.axis_size("mem")
    coarse = side_faces.shape[2]
    in_chip = [(i, i ^ 1) for i in range(devices)]
    near, far, rest, pot, src0 = sent_stage(potential, source)
    arrived = lax.ppermute(near, AXES, in_chip)
    own, far = own_stage(devices, src0, rest, near, far, side_faces, end_faces)
    sent = rows_stage(devices, own, arrived, far)
    received = lax.all_to_all(sent, AXES, 0, 0, tiled=True)
    solved = sweep_stage(received)
    returned = lax.all_to_all(solved, AXES, 0, 0, tiled=True)
    own, swapped, extra = back_stage(coarse, returned)
    swapped = lax.ppermute(swapped, AXES, in_chip)
    corrected, correction = plane_stage("even_stage", even_kernel, (own,), pot, None)
    (corrected,) = plane_stage("odd_stage", odd_kernel, (own, swapped, extra), pot, corrected)
    return corrected, correction


def solution(mesh):
    split = P(AXES, None, None)
    return jax.shard_map(
        per_device,
        mesh=mesh,
        in_specs=(split, split, split, P()),
        out_specs=(split, split),
        check_vma=False,
    )
```

time: 55.7 us -> 50.7 us (0.910); the launches traced: 54.9 us -> 50.4 us
  blocking collectives: 40.5 us -> 37.8 us
  waiting for transfers between devices: 1.52 us -> 0.01 us
  Pallas kernels: 12 us -> 10.6 us
  starting transfers between devices: 0.08 us -> 1.25 us
    all_to_all x1, blocking collectives: 18.4 us -> 15.6 us  [per_device(): returned = lax.all_to_all(solved, AXES, 0, 0, tiled=True)]
    ppermute x1 -> x2, waiting for transfers between devices: 1.52 us -> 0.01 us  [the longest x1 0.01 us: per_device(): arrived = lax.ppermute(near, AXES, in_chip)]
    pallas_call x4 -> x7, Pallas kernels: 12 us -> 10.6 us  [the longest x1 3.73 us: sent_stage(): pl.pallas_call(sent_kernel, out_shape=(plane, plane, jax.ShapeDtypeStruct...]
    ppermute x1 -> x2, starting transfers between devices: 0.08 us -> 1.25 us  [the longest x1 1.17 us: per_device(): swapped = lax.ppermute(swapped, AXES, in_chip)]
  transfers between devices with their start and end apart: 1 -> 2, of which waited for: 1 -> 0; matrix products, arithmetic and copies ran while one was open for 0% -> 0% of each run, Pallas kernels for 0% -> 6%
where the time goes in v3:
time: 50.7 us; the launch traced here: 50.4 us
  blocking collectives  37.8 us (75%)
  Pallas kernels  10.6 us (21%)
  starting transfers between devices  1.25 us (2%)
  between operations  0.76 us (1%)
    all_to_all x1, blocking collectives, per_device(): received = lax.all_to_all(sent, AXES, 0, 0, tiled=True)  22.2 us
    all_to_all x1, blocking collectives, per_device(): returned = lax.all_to_all(solved, AXES, 0, 0, tiled=True)  15.6 us
    pallas_call x1, Pallas kernels, sent_stage(): pl.pallas_call(sent_kernel, out_shape=(plane, plane, jax.ShapeDtypeStruct...  3.73 us
    pallas_call x2, Pallas kernels, plane_stage(): pl.pallas_call(kernel, out_shape=outs, in_specs=specs, out_specs=[HBM] *...  2.93 us
    pallas_call x1, Pallas kernels, sweep_stage(): pl.pallas_call(packed_sweep_kernel if packed else sweep_kernel, out_shape...  1.66 us
    pallas_call x1, Pallas kernels, own_stage(): pl.pallas_call(own_kernel, out_shape=(jax.ShapeDtypeStruct((coarse, coars...  1.5 us
    ppermute x1, starting transfers between devices, per_device(): swapped = lax.ppermute(swapped, AXES, in_chip)  1.17 us
  transfers between devices with their start and end apart: 2, of which 0 were waited for; matrix products, arithmetic and copies ran while one was open for 0% of the time, Pallas kernels for 6%

profile of v3, /device:TPU:1, one launch (start us, length us, event | category | flops | bytes accessed | tf_op | source)
XLA Modules:
  0.0 50.4 jit_solution(2986076436968229694)
XLA Ops:
  0.6 0.0 copy-start
  0.6 0.0 copy-start.2
  0.7 0.0 copy-start.5
  0.7 3.7 %sent_stage.1 = (f32[256,256]{1,0:T(8,128)S(1)}, f32[256,256]{1,0:T(8,128)S(1)}, f32[256,512]{1,0:T(8,128)S(1)}, f32[2,4,528,128]{3,2,1,0:T(8,128)S(1)}, f32[4,528,128]{2,1,0:T(8,128)S(1)}) custom-call(f32[2,512,512]{2,1,0:T(8,128)} %pot_hbm.1, f32[2,512,512]{2,1,0:T(8,128)} %src_hbm.1, bf16[512,256]{1,0:T(8,128)(2,1)} %constant.10.clone.rt_hbm.rt_ref), custom_call_target="tpu_custom_call" | custom-call | tf_op jit(solution)/shard_map/sent_stage/pallas_call | solution.py:225
  4.4 0.1 collective-permute-start
  4.5 0.0 copy-done
  4.5 0.0 copy-done.2
  4.5 0.0 copy-done.5
  4.5 1.5 %own_stage.1 = (f32[256,256]{1,0:T(8,128)S(1)}, f32[256,256]{1,0:T(8,128)S(1)}) custom-call(f32[4,528,128]{2,1,0:T(8,128)S(1)} %get-tuple-element.14.src0, f32[256,512]{1,0:T(8,128)S(1)} %get-tuple-element.15.rest_ref, f32[256,256]{1,0:T(8,128)S(1)} %get-tuple-element.16.near_ref, f32[256,256]{1,0:T(8,128)S(1)} %get-tuple-element.17.far_ref, ...), custom_call_target="tpu_custom_call" | custom-call | tf_op jit(solution)/shard_map/own_stage/pallas_call | solution.py:284
  6.0 0.0 copy-start.4
  6.0 0.0 collective-permute-done.near_ref
  6.0 0.0 copy-start.3
  6.1 0.4 rows_stage.1
  6.5 0.0 copy-start.1
  6.5 22.2 %all_to_all.10.in_ref = f32[32,2,8,256]{3,2,1,0:T(8,128)S(1)} all-to-all(f32[32,2,8,256]{3,2,1,0:T(8,128)S(1)} %rows_stage.1), channel_id=1, replica_groups=mesh['grp'=8,'mem'=4] {'grp','mem'}, dimensions={0} | all-to-all | bytes 1048576 | tf_op jit(solution)/shard_map/all_to_all | solution.py:622
  28.7 0.0 copy-done.4
  28.7 1.7 %sweep_stage.1 = f32[32,8,384]{2,1,0:T(8,128)S(1)} custom-call(f32[32,2,8,256]{3,2,1,0:T(8,128)S(1)} %all_to_all.10.in_ref, f32[32,8,128]{2,1,0:T(8,128)S(1)} %copy-done.4), custom_call_target="tpu_custom_call" | custom-call | tf_op jit(solution)/shard_map/sweep_stage/pallas_call | solution.py:471
  30.4 15.6 %all_to_all.11.in_ref = f32[32,8,384]{2,1,0:T(8,128)S(1)} all-to-all(f32[32,8,384]{2,1,0:T(8,128)S(1)} %sweep_stage.1), channel_id=1, replica_groups=mesh['grp'=8,'mem'=4] {'grp','mem'}, dimensions={0} | all-to-all | bytes 786432 | tf_op jit(solution)/shard_map/all_to_all | solution.py:624
  45.9 0.0 copy-done.3
  45.9 0.4 back_stage.1
  46.3 1.2 %collective-permute-start.1 = (f32[256,256]{1,0:T(8,128)S(1)}, f32[256,256]{1,0:T(8,128)S(1)}, u32[]{:S(2)}, u32[]{:S(2)}) collective-permute-start(f32[256,256]{1,0:T(8,128)S(1)} %get-tuple-element.21), channel_id=1, source_target_pairs={{0,1},{1,0},{2,3},{3,2},{4,5},{5,4},{6,7},{7,6},{8,9},{9,8},{10,11... | collective-permute-start | bytes 786440 | tf_op jit(solution)/shard_map/ppermute | solution.py:626
  47.5 0.0 copy-done.1
  47.5 1.5 %even_stage.1 = (f32[2,512,512]{2,1,0:T(8,128)}, f32[1,256,256]{2,1,0:T(8,128)}) custom-call(f32[256,256]{1,0:T(8,128)S(1)} %get-tuple-element.20.own_ref, bf16[256,512]{1,0:T(8,128)(2,1)S(1)} %copy-done.1, f32[2,4,528,128]{3,2,1,0:T(8,128)S(1)} %get-tuple-element.23.pot), custom_call_target="tpu_custom_call" | custom-call | tf_op jit(solution)/shard_map/even_stage/pallas_call | solution.py:602
  49.0 0.0 collective-permute-done.1.swapped_ref
  49.0 1.5 %odd_stage.1 = f32[2,512,512]{2,1,0:T(8,128)} custom-call(f32[256,256]{1,0:T(8,128)S(1)} %get-tuple-element.20.own_ref, f32[256,256]{1,0:T(8,128)S(1)} %collective-permute-done.1.swapped_ref, f32[256,128]{1,0:T(8,128)S(1)} %get-tuple-element.22.extra_ref, bf16[256,512]{1,0:T(8,128)(2,1)S(1)} %copy-done.1, ...), custom_call_target="tpu_custom_call", output_to_operand_aliasing={{}: (5, {})} | custom-call | tf_op jit(solution)/shard_map/odd_stage/pallas_call | solution.py:602
Async XLA Ops:
  0.6 3.9 %copy-start = (bf16[3,256,256]{2,1,0:T(8,128)(2,1)S(1)}, bf16[3,256,256]{2,1,0:T(8,128)(2,1)}, u32[]{:S(2)}) copy-start(bf16[3,256,256]{2,1,0:T(8,128)(2,1)} %constant.11.clone.sine_ref) | copy-start | bytes 1179652
  0.6 3.9 %copy-start.2 = (bf16[512,256]{1,0:T(8,128)(2,1)S(1)}, bf16[512,256]{1,0:T(8,128)(2,1)}, u32[]{:S(2)}) copy-start(bf16[512,256]{1,0:T(8,128)(2,1)} %constant.10.clone.rt_hbm.rt_ref) | copy-start | bytes 786436
  0.7 3.8 %copy-start.5 = (f32[1,4,256]{2,1,0:T(4,128)S(1)}, f32[1,4,256]{2,1,0:T(4,128)}, u32[]{:S(2)}) copy-start(f32[1,4,256]{2,1,0:T(4,128)} %side_ref.1) | copy-start | bytes 12292
  4.4 1.6 %collective-permute-start = (f32[256,256]{1,0:T(8,128)S(1)}, f32[256,256]{1,0:T(8,128)S(1)}, u32[]{:S(2)}, u32[]{:S(2)}) collective-permute-start(f32[256,256]{1,0:T(8,128)S(1)} %get-tuple-element.16.near_ref), channel_id=1, source_target_pairs={{0,1},{1,0},{2,3},{3,2},{4,5},{5,4},{6,7},{7,6},{8,9},{9,8},{10,11... | collective-permute-start | bytes 786440 | tf_op jit(solution)/shard_map/ppermute | solution.py:619
  6.0 22.7 %copy-start.4 = (f32[32,8,128]{2,1,0:T(8,128)S(1)}, f32[32,8,128]{2,1,0:T(8,128)}, u32[]{:S(2)}) copy-start(f32[32,8,128]{2,1,0:T(8,128)} %constant.12.clone.alpha_ref) | copy-start | bytes 393220
  6.0 39.9 %copy-start.3 = (bf16[2,256,256]{2,1,0:T(8,128)(2,1)S(1)}, bf16[2,256,256]{2,1,0:T(8,128)(2,1)}, u32[]{:S(2)}) copy-start(bf16[2,256,256]{2,1,0:T(8,128)(2,1)} %constant.13.clone.back_ref) | copy-start | bytes 786436
  6.5 41.0 %copy-start.1 = (bf16[256,512]{1,0:T(8,128)(2,1)S(1)}, bf16[256,512]{1,0:T(8,128)(2,1)}, u32[]{:S(2)}) copy-start(bf16[256,512]{1,0:T(8,128)(2,1)} %constant.14.clone.pt_ref) | copy-start | bytes 786436
  46.3 2.6 %collective-permute-start.1 = (f32[256,256]{1,0:T(8,128)S(1)}, f32[256,256]{1,0:T(8,128)S(1)}, u32[]{:S(2)}, u32[]{:S(2)}) collective-permute-start(f32[256,256]{1,0:T(8,128)S(1)} %get-tuple-element.21), channel_id=1, source_target_pairs={{0,1},{1,0},{2,3},{3,2},{4,5},{5,4},{6,7},{7,6},{8,9},{9,8},{10,11... | collective-permute-start | bytes 786440 | tf_op jit(solution)/shard_map/ppermute | solution.py:626

commit v4 on v3

--- a/solution.py
+++ b/solution.py
@@ -119,21 +119,33 @@
     return sums
 
 
+def around(rows, even, row_ids, start):
+    outer = rows(-2) + rows(2)
+    if start == 0:
+        outer = outer - jnp.where(row_ids == 0, even, 0.0)
+    return outer - (even + even)
+
+
+def in_plane(quad, outer, lanes):
+    sums = beside(quad, lanes)
+    return [(outer[c] + sums[c]) - 4.0 * quad[c] for c in range(len(quad))]
+
+
 def sent_kernel(
-    pot_hbm, src_hbm, rt_hbm,
-    near_ref, far_ref, rest_ref, pot, src0,
-    src, rt_ref, mid, parts, sem, small_sem,
+    pot_hbm, src_hbm, end_hbm, rt_hbm, sine_hbm,
+    near_ref, far_ref, pot, src0, end, rt_ref, sine_ref,
+    src, mid, parts, sem, small_sem,
 ):
     fine = pot_hbm.shape[1]
     coarse = fine // 2
     blocks = fine // LANES
     cut = fine // 2 + 2 * PAD
-    position, _ = place()
+    position, devices = place()
     groups = []
     for hbm, plane, buf, index in (
         (pot_hbm, 0, pot, (0,)), (pot_hbm, 1, pot, (1,)), (src_hbm, 1, src, ()), (src_hbm, 0, src0, ()),
     ):
-        for first, size in ((0, cut), (cut, fine - cut)):
+        for first, size in ((0, fine),):
             group = []
             for c in range(blocks):
                 group.append(
@@ -144,79 +156,93 @@
                     )
                 )
             groups.append(group)
-    for group in groups[:2]:
+    for group in groups[:1]:
         for copy in group:
             copy.start()
-    matrix = pltpu.make_async_copy(rt_hbm, rt_ref, small_sem)
+    matrix = pltpu.make_async_copy(rt_hbm, rt_ref, small_sem.at[0])
     matrix.start()
-    for group in groups[2:]:
+    for group in groups[1:3]:
         for copy in group:
             copy.start()
+    for copy in groups[3]:
+        copy.start(priority=1)
+    sine = pltpu.make_async_copy(sine_hbm, sine_ref, small_sem.at[1])
+    sine.start()
+    last = devices - 1
+    at_end = jnp.logical_or(position == 0, position == last)
+    end_copy = pltpu.make_async_copy(end_hbm.at[jnp.where(position == last, 1, 0)], end, small_sem.at[2])
+
+    @pl.when(at_end)
+    def _():
+        end_copy.start()
+
     edge = jnp.zeros((blocks, PAD, LANES), F32)
     for ref in (pot.at[0], pot.at[1], src, src0):
         ref[:, 0:PAD, :] = edge
         ref[:, PAD + fine : PAD + fine + PAD, :] = edge
 
-    half_not_first = jnp.where(position > 0, 0.5, 0.0).astype(F32)
     block = 32
     lanes = lax.broadcasted_iota(jnp.int32, (block, LANES), 1)
     row_ids = lax.broadcasted_iota(jnp.int32, (block, LANES), 0)
 
     def chunk(plane, start):
         where = pl.ds(start, block)
-        quad, around = [], []
+        quad, whole = [], []
         for c in range(blocks):
             rows = restricted_rows(pot, (plane, c), start, block)
             even = rows(0)
-            twice = even + even
-            quad.append(twice + (rows(1) + rows(-1)))
-            outer = rows(-2) + rows(2)
-            if start == 0:
-                outer = outer - jnp.where(row_ids == 0, even, 0.0)
-            around.append(outer - twice)
-        sums = beside(quad, lanes)
+            quad.append((even + even) + (rows(1) + rows(-1)))
+            if plane == 1:
+                whole.append(around(rows, even, row_ids, start))
+        if plane == 1:
+            whole = in_plane(quad, whole, lanes)
         for c in range(blocks):
             columns = pl.ds(c * LANES, LANES)
-            whole = (around[c] + sums[c]) - 4.0 * quad[c]
             if plane == 0:
                 mid[where, columns] = quad[c]
-                rest_ref[where, columns] = whole + half_not_first * quad[c]
-                value = quad[c]
+                pieces(0, where, columns, quad[c])
             else:
                 rows = restricted_rows(src, (c,), start, block)
                 even = rows(0)
                 source = (even + even) + (rows(1) + rows(-1))
-                value = (whole + 0.25 * source) + ((quad[c] + quad[c]) + mid[where, columns])
-            for part, piece in enumerate(split3(value)):
-                parts[3 * plane + part, where, columns] = piece
+                value = (whole[c] + 0.25 * source) + ((quad[c] + quad[c]) + mid[where, columns])
+                pieces(3, where, columns, value)
+
+    def pieces(first, where, columns, value):
+        for part, piece in enumerate(split3(value)):
+            parts[first + part, where, columns] = piece
 
     starts = range(0, coarse, block)
+    for copy in groups[0]:
+        copy.wait()
     for start in starts:
-        if start == 0 or start == coarse // 2:
-            for copy in groups[0 if start == 0 else 1]:
-                copy.wait()
         chunk(0, start)
-    for group in groups[2:6]:
+    for group in groups[1:3]:
         for copy in group:
             copy.wait()
     matrix.wait()
-    down = 0.25 * dot3(parts, 0, rt_ref[...])
     for start in starts:
         chunk(1, start)
+    down = 0.25 * dot3(parts, 0, rt_ref[...])
     up = 0.25 * dot3(parts, 3, rt_ref[...])
     is_even = lax.rem(position, 2) == 0
     near_ref[...] = jnp.where(is_even, up, down)
     far_ref[...] = jnp.where(is_even, down, up)
-    for group in groups[6:]:
+    for group in groups[3:]:
         for copy in group:
             copy.wait()
+    sine.wait()
+
+    @pl.when(at_end)
+    def _():
+        end_copy.wait()
 
 
 def restriction_matrix(fine):
     return jnp.asarray(restriction(fine).T, BF16)
 
 
-def sent_stage(potential, source):
+def sent_stage(devices, potential, source, end_faces):
     fine = potential.shape[1]
     coarse = fine // 2
     blocks = fine // LANES
@@ -227,41 +253,54 @@
         out_shape=(
             plane,
             plane,
-            jax.ShapeDtypeStruct((coarse, fine), F32),
             jax.ShapeDtypeStruct((2,) + held, F32),
             jax.ShapeDtypeStruct(held, F32),
+            plane,
+            jax.ShapeDtypeStruct((fine, coarse), BF16),
+            jax.ShapeDtypeStruct((3, coarse, coarse), BF16),
         ),
-        in_specs=[HBM] * 3,
-        out_specs=(VMEM,) * 5,
+        in_specs=[HBM] * 5,
+        out_specs=(VMEM,) * 7,
         scratch_shapes=[
             pltpu.VMEM(held, F32),
-            pltpu.VMEM((fine, coarse), BF16),
             pltpu.VMEM((coarse, fine), F32),
             pltpu.VMEM((6, coarse, fine), BF16),
             pltpu.SemaphoreType.DMA((8 * blocks,)),
-            pltpu.SemaphoreType.DMA,
+            pltpu.SemaphoreType.DMA((3,)),
         ],
         compiler_params=room(20),
         name="sent_stage",
-    )(in_hbm(potential), in_hbm(source), in_hbm(restriction_matrix(fine)))
-
-
-def own_kernel(src0, rest_ref, near_ref, far_ref, side_ref, end_hbm, rt_ref, sine_ref, own_ref, sent_ref, end, parts, end_sem):
-    coarse, fine = rest_ref.shape
+    )(
+        in_hbm(potential), in_hbm(source), in_hbm(end_faces),
+        in_hbm(restriction_matrix(fine)), in_hbm(row_transform(coarse, devices)),
+    )
+
+
+def own_kernel(src0, pot, near_ref, far_ref, side_ref, end, rt_ref, sine_ref, own_ref, sent_ref, parts):
+    fine, coarse = rt_ref.shape
     position, devices = place()
     last = devices - 1
-    end_copy = pltpu.make_async_copy(end_hbm.at[jnp.where(position == last, 1, 0)], end, end_sem)
-    end_copy.start()
-    block = 64
-    for c in range(fine // LANES):
-        columns = pl.ds(c * LANES, LANES)
-        for start in range(0, coarse, block):
-            where = pl.ds(start, block)
+    half_not_first = jnp.where(position > 0, 0.5, 0.0).astype(F32)
+    block = 32
+    shape = (block, LANES)
+    lanes = lax.broadcasted_iota(jnp.int32, shape, 1)
+    row_ids = lax.broadcasted_iota(jnp.int32, shape, 0)
+    for start in range(0, coarse, block):
+        where = pl.ds(start, block)
+        quad, outer = [], []
+        for c in range(fine // LANES):
+            rows = restricted_rows(pot, (0, c), start, block)
+            even = rows(0)
+            quad.append((even + even) + (rows(1) + rows(-1)))
+            outer.append(around(rows, even, row_ids, start))
+        whole = in_plane(quad, outer, lanes)
+        for c in range(fine // LANES):
             rows = restricted_rows(src0, (c,), start, block)
             even = rows(0)
-            value = rest_ref[where, columns] + 0.25 * ((even + even) + (rows(1) + rows(-1)))
+            source = (even + even) + (rows(1) + rows(-1))
+            value = (whole[c] + half_not_first * quad[c]) + 0.25 * source
             for part, piece in enumerate(split3(value)):
-                parts[part, where, columns] = piece
+                parts[part, where, pl.ds(c * LANES, LANES)] = piece
     sent_ref[...] = dot6(sine_ref, far_ref[...])
     up = jnp.where(lax.rem(position, 2) == 0, near_ref[...], far_ref[...])
     own_ref[...] = 0.5 * dot3(parts, 0, rt_ref[...]) + up
@@ -272,31 +311,26 @@
     lanes = lax.broadcasted_iota(jnp.int32, (coarse, LANES), 1)
     own_ref[:, 0:LANES] += jnp.where(lanes == 0, columns[:, 2:3], 0.0)
     own_ref[:, coarse - LANES : coarse] += jnp.where(lanes == LANES - 1, columns[:, 3:4], 0.0)
-    end_copy.wait()
 
     @pl.when(jnp.logical_or(position == 0, position == last))
     def _():
         own_ref[...] += end[...]
 
 
-def own_stage(devices, src0, rest, near, far, side_faces, end_faces):
-    coarse, fine = rest.shape
+def own_stage(src0, pot, near, far, side_faces, end, rt, sine):
+    fine, coarse = rt.shape
     return pl.pallas_call(
         own_kernel,
         out_shape=(
             jax.ShapeDtypeStruct((coarse, coarse), F32),
             jax.ShapeDtypeStruct((coarse, coarse), F32),
         ),
-        in_specs=[VMEM] * 5 + [HBM, VMEM, VMEM],
+        in_specs=[VMEM] * 8,
         out_specs=(VMEM, VMEM),
-        scratch_shapes=[
-            pltpu.VMEM((coarse, coarse), F32),
-            pltpu.VMEM((3, coarse, fine), BF16),
-            pltpu.SemaphoreType.DMA,
-        ],
+        scratch_shapes=[pltpu.VMEM((3, coarse, fine), BF16)],
         compiler_params=room(12),
         name="own_stage",
-    )(src0, rest, near, far, side_faces, in_hbm(end_faces), restriction_matrix(fine), row_transform(coarse, devices))
+    )(src0, pot, near, far, side_faces, end, rt, sine)
 
 
 def rows_kernel(own_ref, near_ref, sine_ref, far_ref, out_ref):
@@ -310,7 +344,7 @@
     return split_matrix(sine_matrix(coarse)[mode_order(coarse, devices)], 3)
 
 
-def rows_stage(devices, own, near, far):
+def rows_stage(devices, own, near, far, sine):
     coarse = own.shape[0]
     shape = (devices, 2, coarse // devices, coarse)
     return pl.pallas_call(
@@ -320,7 +354,7 @@
         out_specs=VMEM,
         compiler_params=room(8),
         name="rows_stage",
-    )(own, near, row_transform(coarse, devices), far)
+    )(own, near, sine, far)
 
 
 def sweep_kernel(in_ref, alpha_ref, out_ref, values, force):
@@ -615,10 +649,10 @@
     devices = lax.axis_size("grp") * lax.axis_size("mem")
     coarse = side_faces.shape[2]
     in_chip = [(i, i ^ 1) for i in range(devices)]
-    near, far, rest, pot, src0 = sent_stage(potential, source)
+    near, far, pot, src0, end, rt, sine = sent_stage(devices, potential, source, end_faces)
     arrived = lax.ppermute(near, AXES, in_chip)
-    own, far = own_stage(devices, src0, rest, near, far, side_faces, end_faces)
-    sent = rows_stage(devices, own, arrived, far)
+    own, far = own_stage(src0, pot, near, far, side_faces, end, rt, sine)
+    sent = rows_stage(devices, own, arrived, far, sine)
     received = lax.all_to_all(sent, AXES, 0, 0, tiled=True)
     solved = sweep_stage(received)
     returned = lax.all_to_all(solved, AXES, 0, 0, tiled=True)

time: 50.7 us -> 50 us (0.986)
  Pallas kernels: 10.6 us -> 9.61 us
    pallas_call x1, Pallas kernels: 1.5 us -> 0.99 us  [own_stage(): pl.pallas_call(own_kernel, out_shape=(jax.ShapeDtypeStruct((coarse, coars...]
  transfers between devices with their start and end apart: 2 -> 2, of which waited for: 0 -> 1; matrix products, arithmetic and copies ran while one was open for 0% -> 0% of each run, Pallas kernels for 6% -> 5%
where the time goes in v4:
time: 50 us; the launch traced here: 49.8 us
  blocking collectives  37.7 us (75%)
  Pallas kernels  9.61 us (19%)
  starting transfers between devices  1.25 us (2%)
  between operations  0.71 us (1%)
  waiting for transfers between devices  0.51 us (1%)
    all_to_all x1, blocking collectives, per_device(): received = lax.all_to_all(sent, AXES, 0, 0, tiled=True)  22.1 us
    all_to_all x1, blocking collectives, per_device(): returned = lax.all_to_all(solved, AXES, 0, 0, tiled=True)  15.6 us
    pallas_call x1, Pallas kernels, sent_stage(): pl.pallas_call(sent_kernel, out_shape=(plane, plane, jax.ShapeDtypeStruct...  3.24 us
    pallas_call x2, Pallas kernels, plane_stage(): pl.pallas_call(kernel, out_shape=outs, in_specs=specs, out_specs=[HBM] *...  2.93 us
    pallas_call x1, Pallas kernels, sweep_stage(): pl.pallas_call(packed_sweep_kernel if packed else sweep_kernel, out_shape...  1.66 us
    ppermute x1, starting transfers between devices, per_device(): swapped = lax.ppermute(swapped, AXES, in_chip)  1.17 us
  transfers between devices with their start and end apart: 2, of which 1 were waited for; matrix products, arithmetic and copies ran while one was open for 0% of the time, Pallas kernels for 5%

profile of v4, /device:TPU:1, one launch (start us, length us, event | category | flops | bytes accessed | tf_op | source)
XLA Modules:
  0.0 49.8 jit_solution(1813076032731997819)
XLA Ops:
  0.6 0.0 copy-start.3
  0.6 3.2 %sent_stage.1 = (f32[256,256]{1,0:T(8,128)S(1)}, f32[256,256]{1,0:T(8,128)S(1)}, f32[2,4,528,128]{3,2,1,0:T(8,128)S(1)}, f32[4,528,128]{2,1,0:T(8,128)S(1)}, f32...) custom-call(f32[2,512,512]{2,1,0:T(8,128)} %pot_hbm.1, ...), custom_call_target="tpu_custom_call" | custom-call | tf_op jit(solution)/shard_map/sent_stage/pallas_call | solution.py:251
  3.9 0.1 collective-permute-start
  4.0 0.0 copy-done.3
  4.0 1.0 %own_stage.1 = (f32[256,256]{1,0:T(8,128)S(1)}, f32[256,256]{1,0:T(8,128)S(1)}) custom-call(f32[4,528,128]{2,1,0:T(8,128)S(1)} %get-tuple-element.16.src0, f32[2,4,528,128]{3,2,1,0:T(8,128)S(1)} %get-tuple-element.17.pot, f32[256,256]{1,0:T(8,128)S(1)} %get-tuple-element.18.near_ref, f32[256,256]{1,0:T(8,128)S(1)} %get-tuple-element.19.far_ref, ...), custom_call_target="tpu_custom_call" | custom-call | tf_op jit(solution)/shard_map/own_stage/pallas_call | solution.py:322
  5.0 0.0 copy-start.2
  5.0 0.5 %collective-permute-done.near_ref = f32[256,256]{1,0:T(8,128)S(1)} collective-permute-done((f32[256,256]{1,0:T(8,128)S(1)}, f32[256,256]{1,0:T(8,128)S(1)}, u32[]{:S(2)}, u32[]{:S(2)}) %collective-permute-start) | collective-permute-done | bytes 262176 | tf_op jit(solution)/shard_map/ppermute | solution.py:653
  5.5 0.0 copy-start.1
  5.5 0.4 rows_stage.1
  5.9 0.0 copy-start
  5.9 22.1 %all_to_all.10.in_ref = f32[32,2,8,256]{3,2,1,0:T(8,128)S(1)} all-to-all(f32[32,2,8,256]{3,2,1,0:T(8,128)S(1)} %rows_stage.1), channel_id=1, replica_groups=mesh['grp'=8,'mem'=4] {'grp','mem'}, dimensions={0} | all-to-all | bytes 1048576 | tf_op jit(solution)/shard_map/all_to_all | solution.py:656
  28.0 0.0 copy-done.2
  28.0 1.7 %sweep_stage.1 = f32[32,8,384]{2,1,0:T(8,128)S(1)} custom-call(f32[32,2,8,256]{3,2,1,0:T(8,128)S(1)} %all_to_all.10.in_ref, f32[32,8,128]{2,1,0:T(8,128)S(1)} %copy-done.2), custom_call_target="tpu_custom_call" | custom-call | tf_op jit(solution)/shard_map/sweep_stage/pallas_call | solution.py:505
  29.7 15.6 %all_to_all.11.in_ref = f32[32,8,384]{2,1,0:T(8,128)S(1)} all-to-all(f32[32,8,384]{2,1,0:T(8,128)S(1)} %sweep_stage.1), channel_id=1, replica_groups=mesh['grp'=8,'mem'=4] {'grp','mem'}, dimensions={0} | all-to-all | bytes 786432 | tf_op jit(solution)/shard_map/all_to_all | solution.py:658
  45.3 0.0 copy-done.1
  45.3 0.4 back_stage.1
  45.7 1.2 %collective-permute-start.1 = (f32[256,256]{1,0:T(8,128)S(1)}, f32[256,256]{1,0:T(8,128)S(1)}, u32[]{:S(2)}, u32[]{:S(2)}) collective-permute-start(f32[256,256]{1,0:T(8,128)S(1)} %get-tuple-element.26), channel_id=1, source_target_pairs={{0,1},{1,0},{2,3},{3,2},{4,5},{5,4},{6,7},{7,6},{8,9},{9,8},{10,11... | collective-permute-start | bytes 786440 | tf_op jit(solution)/shard_map/ppermute | solution.py:660
  46.8 0.0 copy-done
  46.8 1.5 %even_stage.1 = (f32[2,512,512]{2,1,0:T(8,128)}, f32[1,256,256]{2,1,0:T(8,128)}) custom-call(f32[256,256]{1,0:T(8,128)S(1)} %get-tuple-element.25.own_ref, bf16[256,512]{1,0:T(8,128)(2,1)S(1)} %copy-done, f32[2,4,528,128]{3,2,1,0:T(8,128)S(1)} %get-tuple-element.17.pot), custom_call_target="tpu_custom_call" | custom-call | tf_op jit(solution)/shard_map/even_stage/pallas_call | solution.py:636
  48.3 0.0 collective-permute-done.1.swapped_ref
  48.3 1.5 %odd_stage.1 = f32[2,512,512]{2,1,0:T(8,128)} custom-call(f32[256,256]{1,0:T(8,128)S(1)} %get-tuple-element.25.own_ref, f32[256,256]{1,0:T(8,128)S(1)} %collective-permute-done.1.swapped_ref, f32[256,128]{1,0:T(8,128)S(1)} %get-tuple-element.27.extra_ref, bf16[256,512]{1,0:T(8,128)(2,1)S(1)} %copy-done, ...), custom_call_target="tpu_custom_call", output_to_operand_aliasing={{}: (5, {})} | custom-call | tf_op jit(solution)/shard_map/odd_stage/pallas_call | solution.py:636
Async XLA Ops:
  0.6 3.3 %copy-start.3 = (f32[1,4,256]{2,1,0:T(4,128)S(1)}, f32[1,4,256]{2,1,0:T(4,128)}, u32[]{:S(2)}) copy-start(f32[1,4,256]{2,1,0:T(4,128)} %side_ref.1) | copy-start | bytes 12292
  3.9 1.6 %collective-permute-start = (f32[256,256]{1,0:T(8,128)S(1)}, f32[256,256]{1,0:T(8,128)S(1)}, u32[]{:S(2)}, u32[]{:S(2)}) collective-permute-start(f32[256,256]{1,0:T(8,128)S(1)} %get-tuple-element.18.near_ref), channel_id=1, source_target_pairs={{0,1},{1,0},{2,3},{3,2},{4,5},{5,4},{6,7},{7,6},{8,9},{9,8},{10,11... | collective-permute-start | bytes 786440 | tf_op jit(solution)/shard_map/ppermute | solution.py:653
  5.0 23.1 %copy-start.2 = (f32[32,8,128]{2,1,0:T(8,128)S(1)}, f32[32,8,128]{2,1,0:T(8,128)}, u32[]{:S(2)}) copy-start(f32[32,8,128]{2,1,0:T(8,128)} %constant.12.clone.alpha_ref) | copy-start | bytes 393220
  5.5 39.8 %copy-start.1 = (bf16[2,256,256]{2,1,0:T(8,128)(2,1)S(1)}, bf16[2,256,256]{2,1,0:T(8,128)(2,1)}, u32[]{:S(2)}) copy-start(bf16[2,256,256]{2,1,0:T(8,128)(2,1)} %constant.13.clone.back_ref) | copy-start | bytes 786436
  5.9 40.9 %copy-start = (bf16[256,512]{1,0:T(8,128)(2,1)S(1)}, bf16[256,512]{1,0:T(8,128)(2,1)}, u32[]{:S(2)}) copy-start(bf16[256,512]{1,0:T(8,128)(2,1)} %constant.14.clone.pt_ref) | copy-start | bytes 786436
  45.7 2.6 %collective-permute-start.1 = (f32[256,256]{1,0:T(8,128)S(1)}, f32[256,256]{1,0:T(8,128)S(1)}, u32[]{:S(2)}, u32[]{:S(2)}) collective-permute-start(f32[256,256]{1,0:T(8,128)S(1)} %get-tuple-element.26), channel_id=1, source_target_pairs={{0,1},{1,0},{2,3},{3,2},{4,5},{5,4},{6,7},{7,6},{8,9},{9,8},{10,11... | collective-permute-start | bytes 786440 | tf_op jit(solution)/shard_map/ppermute | solution.py:660

commit v5 on v4

--- a/solution.py
+++ b/solution.py
@@ -132,7 +132,7 @@
 
 
 def sent_kernel(
-    pot_hbm, src_hbm, end_hbm, rt_hbm, sine_hbm,
+    pot_hbm, src_hbm, end_hbm, sine_hbm,
     near_ref, far_ref, pot, src0, end, rt_ref, sine_ref,
     src, mid, parts, sem, small_sem,
 ):
@@ -159,8 +159,6 @@
     for group in groups[:1]:
         for copy in group:
             copy.start()
-    matrix = pltpu.make_async_copy(rt_hbm, rt_ref, small_sem.at[0])
-    matrix.start()
     for group in groups[1:3]:
         for copy in group:
             copy.start()
@@ -176,6 +174,9 @@
     def _():
         end_copy.start()
 
+    offset = lax.broadcasted_iota(jnp.int32, rt_ref.shape, 0) - 2 * lax.broadcasted_iota(jnp.int32, rt_ref.shape, 1)
+    beside_even = jnp.where(jnp.abs(offset) == 1, 0.25, 0.0)
+    rt_ref[...] = jnp.where(offset == 0, 0.5, beside_even).astype(BF16)
     edge = jnp.zeros((blocks, PAD, LANES), F32)
     for ref in (pot.at[0], pot.at[1], src, src0):
         ref[:, 0:PAD, :] = edge
@@ -220,7 +221,6 @@
     for group in groups[1:3]:
         for copy in group:
             copy.wait()
-    matrix.wait()
     for start in starts:
         chunk(1, start)
     down = 0.25 * dot3(parts, 0, rt_ref[...])
@@ -259,7 +259,7 @@
             jax.ShapeDtypeStruct((fine, coarse), BF16),
             jax.ShapeDtypeStruct((3, coarse, coarse), BF16),
         ),
-        in_specs=[HBM] * 5,
+        in_specs=[HBM] * 4,
         out_specs=(VMEM,) * 7,
         scratch_shapes=[
             pltpu.VMEM(held, F32),
@@ -272,7 +272,7 @@
         name="sent_stage",
     )(
         in_hbm(potential), in_hbm(source), in_hbm(end_faces),
-        in_hbm(restriction_matrix(fine)), in_hbm(row_transform(coarse, devices)),
+        in_hbm(row_transform(coarse, devices)),
     )
 
 
@@ -469,7 +469,7 @@
         update(black, black_force, red)
         return carry
 
-    lax.fori_loop(0, SWEEPS - 1, sweep, 0)
+    lax.fori_loop(0, SWEEPS - 1, sweep, 0, unroll=True)
 
     for q in range(slots):
         for c in range(count):
@@ -513,69 +513,67 @@
     )(received, table)
 
 
-def back_kernel(in_ref, back_ref, corr_ref, swap_ref, extra_ref):
-    devices, held, width = in_ref.shape
-    coarse = corr_ref.shape[0]
+def back_product(in_ref, back_ref, first, size):
+    devices, held, _ = in_ref.shape
+    coarse = back_ref.shape[1]
     rows = coarse // devices
-    fields = held // rows
-    position, _ = place()
-
-    def product(first, size):
-        total = None
-        for f in range(fields):
-            part = in_ref[:, f * rows : (f + 1) * rows, first : first + size].reshape(coarse, size)
-            high = part.astype(BF16)
-            low = (part - high.astype(F32)).astype(BF16)
-            for left, right in ((1, high), (0, low), (0, high)):
-                term = jnp.dot(back_ref[2 * f + left], right, preferred_element_type=F32)
-                total = term if total is None else total + term
-        return total
-
-    both = product(0, width)
-    own, extra = both[:, 0:coarse], both[:, coarse:]
-    corr_ref[...] = own
-    extra_ref[...] = extra
-    is_even = lax.rem(position, 2) == 0
-
-    @pl.when(is_even)
-    def _():
-        swap_ref[:, 0 : width - coarse] = extra
-        swap_ref[:, width - coarse :] = extra
-
-    @pl.when(jnp.logical_not(is_even))
-    def _():
-        swap_ref[...] = own
-
-
-def back_stage(coarse, received):
-    devices, held, width = received.shape
-    rows = coarse // devices
+    total = None
+    for f in range(held // rows):
+        part = in_ref[:, f * rows : (f + 1) * rows, first : first + size].reshape(coarse, size)
+        high = part.astype(BF16)
+        low = (part - high.astype(F32)).astype(BF16)
+        for left, right in ((1, high), (0, low), (0, high)):
+            term = jnp.dot(back_ref[2 * f + left], right, preferred_element_type=F32)
+            total = term if total is None else total + term
+    return total
+
+
+def by_parity(even, odd):
+    is_even = lax.rem(place()[0], 2) == 0
+    pl.when(is_even)(even)
+    pl.when(jnp.logical_not(is_even))(odd)
+
+
+def swap_kernel(in_ref, back_ref, swap_ref):
+    coarse = swap_ref.shape[0]
+    half = in_ref.shape[2] - coarse
+
+    def even():
+        swap_ref[:, 0:half] = back_product(in_ref, back_ref, coarse, half)
+        swap_ref[:, half:] = jnp.zeros((coarse, coarse - half), F32)
+
+    def odd():
+        swap_ref[...] = back_product(in_ref, back_ref, 0, coarse)
+
+    by_parity(even, odd)
+
+
+def back_matrices(coarse, devices, held):
     order = mode_order(coarse, devices)
     sine = sine_matrix(coarse)
     back = [sine[order].T]
-    if held > rows:
+    if held > coarse // devices:
         back.append(sine[coarse - 1 - order].T)
+    return jnp.concatenate([split_matrix(matrix, 2) for matrix in back])
+
+
+def swap_stage(coarse, received, back):
     return pl.pallas_call(
-        back_kernel,
-        out_shape=(
-            jax.ShapeDtypeStruct((coarse, coarse), F32),
-            jax.ShapeDtypeStruct((coarse, coarse), F32),
-            jax.ShapeDtypeStruct((coarse, width - coarse), F32),
-        ),
+        swap_kernel,
+        out_shape=jax.ShapeDtypeStruct((coarse, coarse), F32),
         in_specs=[VMEM, VMEM],
-        out_specs=(VMEM,) * 3,
+        out_specs=VMEM,
         compiler_params=room(8),
-        name="back_stage",
-    )(received, jnp.concatenate([split_matrix(matrix, 2) for matrix in back]))
-
-
-def add_prolonged(value, pt_ref, pot, plane, out_hbm, out, parts, wide, sem):
+        name="swap_stage",
+    )(received, back)
+
+
+def add_prolonged(value, pt_ref, pot, plane, out, parts, wide, ready):
     coarse = value.shape[0]
     fine = 2 * coarse
     block = 64
     for part, piece in enumerate(split3(value)):
         parts[part] = piece
-    stores = []
     for n in range(0, fine, coarse):
         wide[0:coarse, :] = dot3(parts, 0, pt_ref[:, n : n + coarse])
         wide[coarse : coarse + 1, :] = wide[coarse - 1 : coarse, :]
@@ -587,22 +585,40 @@
                 for odd, value in ((0, here), (1, 0.5 * (here + after))):
                     old = pot[plane, c, pl.ds(PAD + 2 * start + odd, block, stride=2), :]
                     out[c, pl.ds(2 * start + odd, block, stride=2), :] = old + value
-            stores.append(
-                pltpu.make_async_copy(out.at[c], out_hbm.at[plane, :, pl.ds(c * LANES, LANES)], sem.at[c])
+            ready(c)
+
+
+def even_kernel(in_ref, back_ref, swap_ref, pt_ref, pot, own_ref, extra_ref, out_ref, parts, wide):
+    coarse, half = extra_ref.shape
+
+    def even():
+        own_ref[...] = back_product(in_ref, back_ref, 0, coarse)
+        extra_ref[...] = swap_ref[:, 0:half]
+
+    def odd():
+        own_ref[...] = swap_ref[...]
+        extra_ref[...] = back_product(in_ref, back_ref, coarse, half)
+
+    by_parity(even, odd)
+    add_prolonged(own_ref[...], pt_ref, pot, 0, out_ref, parts, wide, lambda c: None)
+
+
+def odd_kernel(
+    own_ref, swapped_ref, extra_ref, even_ref, pt_ref, pot, out_hbm, corr_hbm, out, parts, wide, sem, corr_sem
+):
+    stores = [
+        [
+            pltpu.make_async_copy(
+                buf.at[c], out_hbm.at[plane, :, pl.ds(c * LANES, LANES)], sem.at[plane * out.shape[0] + c]
             )
-            stores[-1].start()
-    for store in stores:
-        store.wait()
-
-
-def even_kernel(own_ref, pt_ref, pot, out_hbm, corr_hbm, out, parts, wide, sem, corr_sem):
+            for c in range(out.shape[0])
+        ]
+        for plane, buf in ((0, even_ref), (1, out))
+    ]
+    for store in stores[0]:
+        store.start()
     copy = pltpu.make_async_copy(own_ref, corr_hbm.at[0], corr_sem)
     copy.start()
-    add_prolonged(own_ref[...], pt_ref, pot, 0, out_hbm, out, parts, wide, sem)
-    copy.wait()
-
-
-def odd_kernel(own_ref, swapped_ref, extra_ref, pt_ref, pot, held_hbm, out_hbm, out, parts, wide, sem):
     position, devices = place()
     own = own_ref[...]
     swapped = swapped_ref[...]
@@ -611,38 +627,58 @@
     right = jnp.where(is_even, swapped[:, half:], extra_ref[...])
     above = jnp.concatenate([swapped[:, :half], right], 1)
     above = jnp.where(position == devices - 1, own, above)
-    add_prolonged(0.5 * (own + above), pt_ref, pot, 1, out_hbm, out, parts, wide, sem)
-
-
-def plane_stage(name, kernel, operands, pot, held):
-    coarse = operands[0].shape[0]
+    add_prolonged(
+        0.5 * (own + above), pt_ref, pot, 1, out, parts, wide, lambda c: stores[1][c].start()
+    )
+    for store in stores[0] + stores[1]:
+        store.wait()
+    copy.wait()
+
+
+def prolong_matrix(coarse):
+    return jnp.asarray(prolongation(coarse).T, BF16)
+
+
+def plane_scratch(coarse):
+    return [pltpu.VMEM((3, coarse, coarse), BF16), pltpu.VMEM((coarse + PAD, coarse), F32)]
+
+
+def even_stage(received, back, swap, pot):
+    coarse = swap.shape[0]
     fine = 2 * coarse
-    pt = jnp.asarray(prolongation(coarse).T, BF16)
-    arguments = list(operands) + [pt, pot]
-    specs = [VMEM] * len(arguments)
-    scratch = [
-        pltpu.VMEM((fine // LANES, fine, LANES), F32),
-        pltpu.VMEM((3, coarse, coarse), BF16),
-        pltpu.VMEM((coarse + PAD, coarse), F32),
-        pltpu.SemaphoreType.DMA((fine // LANES,)),
-    ]
-    outs = [jax.ShapeDtypeStruct((2, fine, fine), F32)]
-    if held is None:
-        outs.append(jax.ShapeDtypeStruct((1, coarse, coarse), F32))
-        scratch.append(pltpu.SemaphoreType.DMA)
-    else:
-        arguments.append(held)
-        specs.append(ANY)
     return pl.pallas_call(
-        kernel,
-        out_shape=outs,
-        in_specs=specs,
-        out_specs=[HBM] * len(outs),
-        scratch_shapes=scratch,
-        input_output_aliases={} if held is None else {len(arguments) - 1: 0},
+        even_kernel,
+        out_shape=(
+            jax.ShapeDtypeStruct((coarse, coarse), F32),
+            jax.ShapeDtypeStruct((coarse, received.shape[2] - coarse), F32),
+            jax.ShapeDtypeStruct((fine // LANES, fine, LANES), F32),
+        ),
+        in_specs=[VMEM] * 5,
+        out_specs=(VMEM,) * 3,
+        scratch_shapes=plane_scratch(coarse),
         compiler_params=room(8),
-        name=name,
-    )(*arguments)
+        name="even_stage",
+    )(received, back, swap, prolong_matrix(coarse), pot)
+
+
+def odd_stage(own, swapped, extra, even, pot):
+    coarse = own.shape[0]
+    fine = 2 * coarse
+    blocks = fine // LANES
+    return pl.pallas_call(
+        odd_kernel,
+        out_shape=(
+            jax.ShapeDtypeStruct((2, fine, fine), F32),
+            jax.ShapeDtypeStruct((1, coarse, coarse), F32),
+        ),
+        in_specs=[VMEM] * 6,
+        out_specs=(HBM, HBM),
+        scratch_shapes=[pltpu.VMEM((blocks, fine, LANES), F32)]
+        + plane_scratch(coarse)
+        + [pltpu.SemaphoreType.DMA((2 * blocks,)), pltpu.SemaphoreType.DMA],
+        compiler_params=room(8),
+        name="odd_stage",
+    )(own, swapped, extra, even, prolong_matrix(coarse), pot)
 
 
 def per_device(potential, source, side_faces, end_faces):
@@ -656,11 +692,11 @@
     received = lax.all_to_all(sent, AXES, 0, 0, tiled=True)
     solved = sweep_stage(received)
     returned = lax.all_to_all(solved, AXES, 0, 0, tiled=True)
-    own, swapped, extra = back_stage(coarse, returned)
-    swapped = lax.ppermute(swapped, AXES, in_chip)
-    corrected, correction = plane_stage("even_stage", even_kernel, (own,), pot, None)
-    (corrected,) = plane_stage("odd_stage", odd_kernel, (own, swapped, extra), pot, corrected)
-    return corrected, correction
+    back = back_matrices(coarse, devices, returned.shape[1])
+    swap = swap_stage(coarse, returned, back)
+    swapped = lax.ppermute(swap, AXES, in_chip)
+    own, extra, even = even_stage(returned, back, swap, pot)
+    return odd_stage(own, swapped, extra, even, pot)
 
 
 def solution(mesh):

time: 50 us -> 49.6 us (level)
  Pallas kernels: 9.61 us -> 8.44 us
    pallas_call x3, Pallas kernels: 3.32 us -> 2.53 us  [the longest x1 1.55 us: odd_stage(): pl.pallas_call(odd_kernel, out_shape=(jax.ShapeDtypeStruct((2, fine, fine...]
  transfers between devices with their start and end apart: 2 -> 2, of which waited for: 1 -> 2; matrix products, arithmetic and copies ran while one was open for 0% -> 0% of each run, Pallas kernels for 5% -> 3%
where the time goes in v5:
time: 49.6 us; the launch traced here: 49 us
  blocking collectives  37.7 us (76%)
  Pallas kernels  8.44 us (17%)
  starting transfers between devices  1.25 us (3%)
  waiting for transfers between devices  0.95 us (2%)
  between operations  0.7 us (1%)
    all_to_all x1, blocking collectives, per_device(): received = lax.all_to_all(sent, AXES, 0, 0, tiled=True)  22.1 us
    all_to_all x1, blocking collectives, per_device(): returned = lax.all_to_all(solved, AXES, 0, 0, tiled=True)  15.6 us
    pallas_call x1, Pallas kernels, sent_stage(): pl.pallas_call(sent_kernel, out_shape=(plane, plane, jax.ShapeDtypeStruct...  3.16 us
    pallas_call x1, Pallas kernels, odd_stage(): pl.pallas_call(odd_kernel, out_shape=(jax.ShapeDtypeStruct((2, fine, fine...  1.55 us
    pallas_call x1, Pallas kernels, sweep_stage(): pl.pallas_call(packed_sweep_kernel if packed else sweep_kernel, out_shape...  1.37 us
    ppermute x1, starting transfers between devices, per_device(): swapped = lax.ppermute(swap, AXES, in_chip)  1.17 us
  transfers between devices with their start and end apart: 2, of which 2 were waited for; matrix products, arithmetic and copies ran while one was open for 0% of the time, Pallas kernels for 3%

profile of v5, /device:TPU:1, one launch (start us, length us, event | category | flops | bytes accessed | tf_op | source)
XLA Modules:
  0.0 49.0 jit_solution(8284823548920337334)
XLA Ops:
  0.6 0.0 copy-start.3
  0.6 3.2 %sent_stage.1 = (f32[256,256]{1,0:T(8,128)S(1)}, f32[256,256]{1,0:T(8,128)S(1)}, f32[2,4,528,128]{3,2,1,0:T(8,128)S(1)}, f32[4,528,128]{2,1,0:T(8,128)S(1)}, f32...) custom-call(f32[2,512,512]{2,1,0:T(8,128)} %pot_hbm.1, ...), custom_call_target="tpu_custom_call" | custom-call | tf_op jit(solution)/shard_map/sent_stage/pallas_call | solution.py:251
  3.8 0.1 collective-permute-start
  3.9 0.0 copy-done.3
  3.9 1.0 %own_stage.1 = (f32[256,256]{1,0:T(8,128)S(1)}, f32[256,256]{1,0:T(8,128)S(1)}) custom-call(f32[4,528,128]{2,1,0:T(8,128)S(1)} %get-tuple-element.14.src0, f32[2,4,528,128]{3,2,1,0:T(8,128)S(1)} %get-tuple-element.15.pot, f32[256,256]{1,0:T(8,128)S(1)} %get-tuple-element.16.near_ref, f32[256,256]{1,0:T(8,128)S(1)} %get-tuple-element.17.far_ref, ...), custom_call_target="tpu_custom_call" | custom-call | tf_op jit(solution)/shard_map/own_stage/pallas_call | solution.py:322
  4.9 0.0 copy-start.2
  4.9 0.5 %collective-permute-done.near_ref = f32[256,256]{1,0:T(8,128)S(1)} collective-permute-done((f32[256,256]{1,0:T(8,128)S(1)}, f32[256,256]{1,0:T(8,128)S(1)}, u32[]{:S(2)}, u32[]{:S(2)}) %collective-permute-start) | collective-permute-done | bytes 262176 | tf_op jit(solution)/shard_map/ppermute | solution.py:689
  5.4 0.0 copy-start.1
  5.4 0.4 rows_stage.1
  5.8 0.0 copy-start
  5.8 22.1 %all_to_all.10.in_ref = f32[32,2,8,256]{3,2,1,0:T(8,128)S(1)} all-to-all(f32[32,2,8,256]{3,2,1,0:T(8,128)S(1)} %rows_stage.1), channel_id=1, replica_groups=mesh['grp'=8,'mem'=4] {'grp','mem'}, dimensions={0} | all-to-all | bytes 1048576 | tf_op jit(solution)/shard_map/all_to_all | solution.py:692
  27.9 0.0 copy-done.2
  28.0 1.4 %sweep_stage.1 = f32[32,8,384]{2,1,0:T(8,128)S(1)} custom-call(f32[32,2,8,256]{3,2,1,0:T(8,128)S(1)} %all_to_all.10.in_ref, f32[32,8,128]{2,1,0:T(8,128)S(1)} %copy-done.2), custom_call_target="tpu_custom_call" | custom-call | tf_op jit(solution)/shard_map/sweep_stage/pallas_call | solution.py:505
  29.3 15.6 %all_to_all.11.in_ref = f32[32,8,384]{2,1,0:T(8,128)S(1)} all-to-all(f32[32,8,384]{2,1,0:T(8,128)S(1)} %sweep_stage.1), channel_id=1, replica_groups=mesh['grp'=8,'mem'=4] {'grp','mem'}, dimensions={0} | all-to-all | bytes 786432 | tf_op jit(solution)/shard_map/all_to_all | solution.py:694
  44.9 0.0 copy-done.1
  44.9 0.3 swap_stage.1.swap_ref
  45.2 1.2 %collective-permute-start.1 = (f32[256,256]{1,0:T(8,128)S(1)}, f32[256,256]{1,0:T(8,128)S(1)}, u32[]{:S(2)}, u32[]{:S(2)}) collective-permute-start(f32[256,256]{1,0:T(8,128)S(1)} %swap_stage.1.swap_ref), channel_id=1, source_target_pairs={{0,1},{1,0},{2,3},{3,2},{4,5},{5,4},{6,7},{7,6},{8,9},{9,8},{10,11... | collective-permute-start | bytes 786440 | tf_op jit(solution)/shard_map/ppermute | solution.py:697
  46.3 0.0 copy-done
  46.3 0.7 %even_stage.1 = (f32[256,256]{1,0:T(8,128)S(1)}, f32[256,128]{1,0:T(8,128)S(1)}, f32[4,512,128]{2,1,0:T(8,128)S(1)}) custom-call(f32[32,8,384]{2,1,0:T(8,128)S(1)} %all_to_all.11.in_ref, bf16[2,256,256]{2,1,0:T(8,128)(2,1)S(1)} %copy-done.1, f32[256,256]{1,0:T(8,128)S(1)} %swap_stage.1.swap_ref, bf16[256,512]{1,0:T(8,128)(2,1)S(1)} %copy-done, ...), custom_call_target="tpu_custom_call" | custom-call | tf_op jit(solution)/shard_map/even_stage/pallas_call | solution.py:649
  47.1 0.4 collective-permute-done.1.swapped_ref
  47.5 1.5 %odd_stage.1 = (f32[2,512,512]{2,1,0:T(8,128)}, f32[1,256,256]{2,1,0:T(8,128)}) custom-call(f32[256,256]{1,0:T(8,128)S(1)} %get-tuple-element.23.own_ref, f32[256,256]{1,0:T(8,128)S(1)} %collective-permute-done.1.swapped_ref, f32[256,128]{1,0:T(8,128)S(1)} %get-tuple-element.24.extra_ref, f32[4,512,128]{2,1,0:T(8,128)S(1)} %get-tuple-element.25.even_ref, ...), custom_call_target="tpu_custom_call" | custom-call | tf_op jit(solution)/shard_map/odd_stage/pallas_call | solution.py:668
Async XLA Ops:
  0.6 3.3 %copy-start.3 = (f32[1,4,256]{2,1,0:T(4,128)S(1)}, f32[1,4,256]{2,1,0:T(4,128)}, u32[]{:S(2)}) copy-start(f32[1,4,256]{2,1,0:T(4,128)} %side_ref.1) | copy-start | bytes 12292
  3.8 1.6 %collective-permute-start = (f32[256,256]{1,0:T(8,128)S(1)}, f32[256,256]{1,0:T(8,128)S(1)}, u32[]{:S(2)}, u32[]{:S(2)}) collective-permute-start(f32[256,256]{1,0:T(8,128)S(1)} %get-tuple-element.16.near_ref), channel_id=1, source_target_pairs={{0,1},{1,0},{2,3},{3,2},{4,5},{5,4},{6,7},{7,6},{8,9},{9,8},{10,11... | collective-permute-start | bytes 786440 | tf_op jit(solution)/shard_map/ppermute | solution.py:689
  4.9 23.1 %copy-start.2 = (f32[32,8,128]{2,1,0:T(8,128)S(1)}, f32[32,8,128]{2,1,0:T(8,128)}, u32[]{:S(2)}) copy-start(f32[32,8,128]{2,1,0:T(8,128)} %constant.9.clone.alpha_ref) | copy-start | bytes 393220
  5.4 39.5 %copy-start.1 = (bf16[2,256,256]{2,1,0:T(8,128)(2,1)S(1)}, bf16[2,256,256]{2,1,0:T(8,128)(2,1)}, u32[]{:S(2)}) copy-start(bf16[2,256,256]{2,1,0:T(8,128)(2,1)} %constant.10.clone.back_ref) | copy-start | bytes 786436
  5.8 40.5 %copy-start = (bf16[256,512]{1,0:T(8,128)(2,1)S(1)}, bf16[256,512]{1,0:T(8,128)(2,1)}, u32[]{:S(2)}) copy-start(bf16[256,512]{1,0:T(8,128)(2,1)} %constant.11.clone.pt_ref) | copy-start | bytes 786436
  45.2 2.3 %collective-permute-start.1 = (f32[256,256]{1,0:T(8,128)S(1)}, f32[256,256]{1,0:T(8,128)S(1)}, u32[]{:S(2)}, u32[]{:S(2)}) collective-permute-start(f32[256,256]{1,0:T(8,128)S(1)} %swap_stage.1.swap_ref), channel_id=1, source_target_pairs={{0,1},{1,0},{2,3},{3,2},{4,5},{5,4},{6,7},{7,6},{8,9},{9,8},{10,11... | collective-permute-start | bytes 786440 | tf_op jit(solution)/shard_map/ppermute | solution.py:697

commit v6 on v5

--- a/solution.py
+++ b/solution.py
@@ -165,7 +165,7 @@
     for copy in groups[3]:
         copy.start(priority=1)
     sine = pltpu.make_async_copy(sine_hbm, sine_ref, small_sem.at[1])
-    sine.start()
+    sine.start(priority=1)
     last = devices - 1
     at_end = jnp.logical_or(position == 0, position == last)
     end_copy = pltpu.make_async_copy(end_hbm.at[jnp.where(position == last, 1, 0)], end, small_sem.at[2])
@@ -520,11 +520,8 @@
     total = None
     for f in range(held // rows):
         part = in_ref[:, f * rows : (f + 1) * rows, first : first + size].reshape(coarse, size)
-        high = part.astype(BF16)
-        low = (part - high.astype(F32)).astype(BF16)
-        for left, right in ((1, high), (0, low), (0, high)):
-            term = jnp.dot(back_ref[2 * f + left], right, preferred_element_type=F32)
-            total = term if total is None else total + term
+        term = dot6(back_ref.at[pl.ds(3 * f, 3)], part)
+        total = term if total is None else total + term
     return total
 
 
@@ -554,7 +551,7 @@
     back = [sine[order].T]
     if held > coarse // devices:
         back.append(sine[coarse - 1 - order].T)
-    return jnp.concatenate([split_matrix(matrix, 2) for matrix in back])
+    return jnp.concatenate([split_matrix(matrix, 3) for matrix in back])
 
 
 def swap_stage(coarse, received, back):
@@ -563,7 +560,7 @@
         out_shape=jax.ShapeDtypeStruct((coarse, coarse), F32),
         in_specs=[VMEM, VMEM],
         out_specs=VMEM,
-        compiler_params=room(8),
+        compiler_params=room(16),
         name="swap_stage",
     )(received, back)
 
@@ -656,7 +653,7 @@
         in_specs=[VMEM] * 5,
         out_specs=(VMEM,) * 3,
         scratch_shapes=plane_scratch(coarse),
-        compiler_params=room(8),
+        compiler_params=room(16),
         name="even_stage",
     )(received, back, swap, prolong_matrix(coarse), pot)
 

time: 49.6 us -> 49.7 us (level)
  transfers between devices with their start and end apart: 2 -> 2, of which waited for: 2 -> 2; matrix products, arithmetic and copies ran while one was open for 0% -> 0% of each run, Pallas kernels for 3% -> 4%
where the time goes in v6:
time: 49.7 us; the launch traced here: 49.1 us
  blocking collectives  37.7 us (76%)
  Pallas kernels  8.65 us (17%)
  starting transfers between devices  1.26 us (3%)
  waiting for transfers between devices  0.84 us (2%)
  between operations  0.7 us (1%)
    all_to_all x1, blocking collectives, per_device(): received = lax.all_to_all(sent, AXES, 0, 0, tiled=True)  22.1 us
    all_to_all x1, blocking collectives, per_device(): returned = lax.all_to_all(solved, AXES, 0, 0, tiled=True)  15.6 us
    pallas_call x1, Pallas kernels, sent_stage(): pl.pallas_call(sent_kernel, out_shape=(plane, plane, jax.ShapeDtypeStruct...  3.16 us
    pallas_call x1, Pallas kernels, odd_stage(): pl.pallas_call(odd_kernel, out_shape=(jax.ShapeDtypeStruct((2, fine, fine...  1.55 us
    pallas_call x1, Pallas kernels, sweep_stage(): pl.pallas_call(packed_sweep_kernel if packed else sweep_kernel, out_shape...  1.37 us
    ppermute x1, starting transfers between devices, per_device(): swapped = lax.ppermute(swap, AXES, in_chip)  1.17 us
  transfers between devices with their start and end apart: 2, of which 2 were waited for; matrix products, arithmetic and copies ran while one was open for 0% of the time, Pallas kernels for 4%

profile of v6, /device:TPU:1, one launch (start us, length us, event | category | flops | bytes accessed | tf_op | source)
XLA Modules:
  0.0 49.1 jit_solution(6075083151369884310)
XLA Ops:
  0.6 0.0 copy-start.3
  0.6 3.2 %sent_stage.1 = (f32[256,256]{1,0:T(8,128)S(1)}, f32[256,256]{1,0:T(8,128)S(1)}, f32[2,4,528,128]{3,2,1,0:T(8,128)S(1)}, f32[4,528,128]{2,1,0:T(8,128)S(1)}, f32...) custom-call(f32[2,512,512]{2,1,0:T(8,128)} %pot_hbm.1, ...), custom_call_target="tpu_custom_call" | custom-call | tf_op jit(solution)/shard_map/sent_stage/pallas_call | solution.py:251
  3.8 0.1 collective-permute-start
  3.9 0.0 copy-done.3
  3.9 1.0 %own_stage.1 = (f32[256,256]{1,0:T(8,128)S(1)}, f32[256,256]{1,0:T(8,128)S(1)}) custom-call(f32[4,528,128]{2,1,0:T(8,128)S(1)} %get-tuple-element.14.src0, f32[2,4,528,128]{3,2,1,0:T(8,128)S(1)} %get-tuple-element.15.pot, f32[256,256]{1,0:T(8,128)S(1)} %get-tuple-element.16.near_ref, f32[256,256]{1,0:T(8,128)S(1)} %get-tuple-element.17.far_ref, ...), custom_call_target="tpu_custom_call" | custom-call | tf_op jit(solution)/shard_map/own_stage/pallas_call | solution.py:322
  4.9 0.0 copy-start.2
  4.9 0.5 %collective-permute-done.near_ref = f32[256,256]{1,0:T(8,128)S(1)} collective-permute-done((f32[256,256]{1,0:T(8,128)S(1)}, f32[256,256]{1,0:T(8,128)S(1)}, u32[]{:S(2)}, u32[]{:S(2)}) %collective-permute-start) | collective-permute-done | bytes 262176 | tf_op jit(solution)/shard_map/ppermute | solution.py:686
  5.4 0.0 copy-start
  5.4 0.4 rows_stage.1
  5.8 0.0 copy-start.1
  5.8 22.1 %all_to_all.10.in_ref = f32[32,2,8,256]{3,2,1,0:T(8,128)S(1)} all-to-all(f32[32,2,8,256]{3,2,1,0:T(8,128)S(1)} %rows_stage.1), channel_id=1, replica_groups=mesh['grp'=8,'mem'=4] {'grp','mem'}, dimensions={0} | all-to-all | bytes 1048576 | tf_op jit(solution)/shard_map/all_to_all | solution.py:689
  27.9 0.0 copy-done.2
  27.9 1.4 %sweep_stage.1 = f32[32,8,384]{2,1,0:T(8,128)S(1)} custom-call(f32[32,2,8,256]{3,2,1,0:T(8,128)S(1)} %all_to_all.10.in_ref, f32[32,8,128]{2,1,0:T(8,128)S(1)} %copy-done.2), custom_call_target="tpu_custom_call" | custom-call | tf_op jit(solution)/shard_map/sweep_stage/pallas_call | solution.py:505
  29.3 15.6 %all_to_all.11.in_ref = f32[32,8,384]{2,1,0:T(8,128)S(1)} all-to-all(f32[32,8,384]{2,1,0:T(8,128)S(1)} %sweep_stage.1), channel_id=1, replica_groups=mesh['grp'=8,'mem'=4] {'grp','mem'}, dimensions={0} | all-to-all | bytes 786432 | tf_op jit(solution)/shard_map/all_to_all | solution.py:691
  44.9 0.0 copy-done
  44.9 0.4 swap_stage.1.swap_ref
  45.3 1.2 %collective-permute-start.1 = (f32[256,256]{1,0:T(8,128)S(1)}, f32[256,256]{1,0:T(8,128)S(1)}, u32[]{:S(2)}, u32[]{:S(2)}) collective-permute-start(f32[256,256]{1,0:T(8,128)S(1)} %swap_stage.1.swap_ref), channel_id=1, source_target_pairs={{0,1},{1,0},{2,3},{3,2},{4,5},{5,4},{6,7},{7,6},{8,9},{9,8},{10,11... | collective-permute-start | bytes 786440 | tf_op jit(solution)/shard_map/ppermute | solution.py:694
  46.4 0.0 copy-done.1
  46.4 0.8 %even_stage.1 = (f32[256,256]{1,0:T(8,128)S(1)}, f32[256,128]{1,0:T(8,128)S(1)}, f32[4,512,128]{2,1,0:T(8,128)S(1)}) custom-call(f32[32,8,384]{2,1,0:T(8,128)S(1)} %all_to_all.11.in_ref, bf16[3,256,256]{2,1,0:T(8,128)(2,1)S(1)} %copy-done, f32[256,256]{1,0:T(8,128)S(1)} %swap_stage.1.swap_ref, bf16[256,512]{1,0:T(8,128)(2,1)S(1)} %copy-done.1, ...), custom_call_target="tpu_custom_call" | custom-call | tf_op jit(solution)/shard_map/even_stage/pallas_call | solution.py:646
  47.3 0.3 collective-permute-done.1.swapped_ref
  47.6 1.5 %odd_stage.1 = (f32[2,512,512]{2,1,0:T(8,128)}, f32[1,256,256]{2,1,0:T(8,128)}) custom-call(f32[256,256]{1,0:T(8,128)S(1)} %get-tuple-element.23.own_ref, f32[256,256]{1,0:T(8,128)S(1)} %collective-permute-done.1.swapped_ref, f32[256,128]{1,0:T(8,128)S(1)} %get-tuple-element.24.extra_ref, f32[4,512,128]{2,1,0:T(8,128)S(1)} %get-tuple-element.25.even_ref, ...), custom_call_target="tpu_custom_call" | custom-call | tf_op jit(solution)/shard_map/odd_stage/pallas_call | solution.py:665
Async XLA Ops:
  0.6 3.3 %copy-start.3 = (f32[1,4,256]{2,1,0:T(4,128)S(1)}, f32[1,4,256]{2,1,0:T(4,128)}, u32[]{:S(2)}) copy-start(f32[1,4,256]{2,1,0:T(4,128)} %side_ref.1) | copy-start | bytes 12292
  3.8 1.6 %collective-permute-start = (f32[256,256]{1,0:T(8,128)S(1)}, f32[256,256]{1,0:T(8,128)S(1)}, u32[]{:S(2)}, u32[]{:S(2)}) collective-permute-start(f32[256,256]{1,0:T(8,128)S(1)} %get-tuple-element.16.near_ref), channel_id=1, source_target_pairs={{0,1},{1,0},{2,3},{3,2},{4,5},{5,4},{6,7},{7,6},{8,9},{9,8},{10,11... | collective-permute-start | bytes 786440 | tf_op jit(solution)/shard_map/ppermute | solution.py:686
  4.9 23.1 %copy-start.2 = (f32[32,8,128]{2,1,0:T(8,128)S(1)}, f32[32,8,128]{2,1,0:T(8,128)}, u32[]{:S(2)}) copy-start(f32[32,8,128]{2,1,0:T(8,128)} %constant.9.clone.alpha_ref) | copy-start | bytes 393220
  5.4 39.5 %copy-start = (bf16[3,256,256]{2,1,0:T(8,128)(2,1)S(1)}, bf16[3,256,256]{2,1,0:T(8,128)(2,1)}, u32[]{:S(2)}) copy-start(bf16[3,256,256]{2,1,0:T(8,128)(2,1)} %constant.10.clone.back_ref) | copy-start | bytes 1179652
  5.8 40.6 %copy-start.1 = (bf16[256,512]{1,0:T(8,128)(2,1)S(1)}, bf16[256,512]{1,0:T(8,128)(2,1)}, u32[]{:S(2)}) copy-start(bf16[256,512]{1,0:T(8,128)(2,1)} %constant.11.clone.pt_ref) | copy-start | bytes 786436
  45.3 2.3 %collective-permute-start.1 = (f32[256,256]{1,0:T(8,128)S(1)}, f32[256,256]{1,0:T(8,128)S(1)}, u32[]{:S(2)}, u32[]{:S(2)}) collective-permute-start(f32[256,256]{1,0:T(8,128)S(1)} %swap_stage.1.swap_ref), channel_id=1, source_target_pairs={{0,1},{1,0},{2,3},{3,2},{4,5},{5,4},{6,7},{7,6},{8,9},{9,8},{10,11... | collective-permute-start | bytes 786440 | tf_op jit(solution)/shard_map/ppermute | solution.py:694

commit v7 on v6

--- a/solution.py
+++ b/solution.py
@@ -51,6 +51,27 @@
         matrix[2 * i + 1, i] += 0.5
         matrix[2 * i + 1, min(i + 1, coarse - 1)] += 0.5
     return matrix
+
+
+def column_order(coarse):
+    columns = np.arange(coarse)
+    return np.concatenate([columns[0::2], columns[1::2]]) if coarse == 2 * LANES else columns
+
+
+def ordering(coarse, back):
+    held = lax.broadcasted_iota(jnp.int32, (coarse, coarse), 0 if back else 1)
+    natural = lax.broadcasted_iota(jnp.int32, (coarse, coarse), 1 if back else 0)
+    if coarse == 2 * LANES:
+        held = jnp.where(held < LANES, 2 * held, 2 * (held - LANES) + 1)
+    return jnp.where(held == natural, 1.0, 0.0).astype(BF16)
+
+
+def dot_exact(x, weights):
+    total = None
+    for part in reversed(split3(x)):
+        term = jnp.dot(part, weights, preferred_element_type=F32)
+        total = term if total is None else total + term
+    return total
 
 
 def mode_order(n, devices):
@@ -129,6 +150,22 @@
 def in_plane(quad, outer, lanes):
     sums = beside(quad, lanes)
     return [(outer[c] + sums[c]) - 4.0 * quad[c] for c in range(len(quad))]
+
+
+def beside_columns(parts, lanes):
+    if len(parts) != 2:
+        return beside(parts, lanes)
+    even, odd = parts
+    return [
+        odd + jnp.where(lanes == 0, 0.0, pltpu.roll(odd, 1, 1)),
+        even + jnp.where(lanes == LANES - 1, 0.0, pltpu.roll(even, LANES - 1, 1)),
+    ]
+
+
+def column_sign(lanes, count, k, c):
+    if count == 2:
+        return jnp.full(lanes.shape, 1.0 if (k + c) % 2 == 0 else -1.0, F32)
+    return jnp.where((lanes + k) % 2 == 0, 1.0, -1.0)
 
 
 def sent_kernel(
@@ -174,7 +211,10 @@
     def _():
         end_copy.start()
 
-    offset = lax.broadcasted_iota(jnp.int32, rt_ref.shape, 0) - 2 * lax.broadcasted_iota(jnp.int32, rt_ref.shape, 1)
+    target = lax.broadcasted_iota(jnp.int32, rt_ref.shape, 1)
+    if coarse == 2 * LANES:
+        target = jnp.where(target < LANES, 2 * target, 2 * (target - LANES) + 1)
+    offset = lax.broadcasted_iota(jnp.int32, rt_ref.shape, 0) - 2 * target
     beside_even = jnp.where(jnp.abs(offset) == 1, 0.25, 0.0)
     rt_ref[...] = jnp.where(offset == 0, 0.5, beside_even).astype(BF16)
     edge = jnp.zeros((blocks, PAD, LANES), F32)
@@ -306,15 +346,17 @@
     own_ref[...] = 0.5 * dot3(parts, 0, rt_ref[...]) + up
     side = side_ref[0]
     columns = jnp.transpose(jnp.concatenate([side, side], 0))
-    own_ref[0:1, :] += side[0:1]
-    own_ref[coarse - 1 : coarse, :] += side[1:2]
+    order = ordering(coarse, False)
+    ends = dot_exact(jnp.concatenate([side, side], 0), order)
+    own_ref[0:1, :] += ends[0:1]
+    own_ref[coarse - 1 : coarse, :] += ends[1:2]
     lanes = lax.broadcasted_iota(jnp.int32, (coarse, LANES), 1)
     own_ref[:, 0:LANES] += jnp.where(lanes == 0, columns[:, 2:3], 0.0)
     own_ref[:, coarse - LANES : coarse] += jnp.where(lanes == LANES - 1, columns[:, 3:4], 0.0)
 
     @pl.when(jnp.logical_or(position == 0, position == last))
     def _():
-        own_ref[...] += end[...]
+        own_ref[...] += dot_exact(end[...], order)
 
 
 def own_stage(src0, pot, near, far, side_faces, end, rt, sine):
@@ -381,7 +423,7 @@
         return [values[k, :, columns[c]] for c in range(count)]
 
     def applied(k, under, here, over):
-        sums = beside(here, lanes)
+        sums = beside_columns(here, lanes)
         return [
             (force[k, :, columns[c]] + alpha * here[c]) + sixth * ((under[c] + over[c]) + sums[c])
             for c in range(count)
@@ -405,7 +447,7 @@
         for c in range(count):
             mean = 0.5 * (here[c] + black[c])
             swing = 0.5 * (here[c] - black[c])
-            swing = jnp.where((lanes + k) % 2 == 0, swing, -swing)
+            swing = swing * column_sign(lanes, count, k, c)
             fields = [mean + pltpu.roll(swing, rows // 2, 0)] if paired else [mean, swing]
             for f, field in enumerate(fields):
                 store_solved(out_ref, planes, k, c, f * rows, field)
@@ -424,7 +466,7 @@
     alpha = alpha_ref[place()[0]]
     zero = jnp.zeros(shape, F32)
     columns = [pl.ds(c * LANES, LANES) for c in range(count)]
-    signs = [jnp.where((lanes + q) % 2 == 0, 1.0, -1.0) for q in (0, 1)]
+    signs = [[column_sign(lanes, count, q, c) for c in range(count)] for q in (0, 1)]
 
     def forcing(k, c):
         total = in_ref[k, 0, :, columns[c]]
@@ -441,7 +483,7 @@
         for c in range(count):
             one, two = forcing(q, c), forcing(q + slots, c)
             low = jnp.where(first, one, swapped(two)) * (0.5 * sixth)
-            high = jnp.where(first, swapped(one), two) * (0.5 * sixth * signs[q % 2])
+            high = jnp.where(first, swapped(one), two) * (0.5 * sixth * signs[q % 2][c])
             red_force[q, :, columns[c]] = low + high
             black_force[q, :, columns[c]] = low - high
             red[q, :, columns[c]] = low + high
@@ -455,7 +497,7 @@
         beyond = [jnp.where(first, swapped(x), zero) for x in here]
         for q in range(slots):
             over = held(q + 1) if q + 1 < slots else beyond
-            sums = beside(here, lanes)
+            sums = beside_columns(here, lanes)
             for c in range(count):
                 target[q, :, columns[c]] = (force[q, :, columns[c]] + alpha * here[c]) + sixth * (
                     (under[c] + over[c]) + sums[c]
@@ -475,7 +517,7 @@
         for c in range(count):
             on_red, on_black = red[q, :, columns[c]], black[q, :, columns[c]]
             low = on_red + on_black
-            high = signs[q % 2] * (on_red - on_black)
+            high = signs[q % 2][c] * (on_red - on_black)
             store_solved(out_ref, planes, q, c, 0, jnp.where(first, low, swapped(high)))
             store_solved(out_ref, planes, q + slots, c, 0, jnp.where(first, swapped(low), high))
 
@@ -585,7 +627,7 @@
             ready(c)
 
 
-def even_kernel(in_ref, back_ref, swap_ref, pt_ref, pot, own_ref, extra_ref, out_ref, parts, wide):
+def even_kernel(in_ref, back_ref, swap_ref, pt_ref, pot, own_ref, extra_ref, out_ref, corr_ref, parts, wide):
     coarse, half = extra_ref.shape
 
     def even():
@@ -598,10 +640,11 @@
 
     by_parity(even, odd)
     add_prolonged(own_ref[...], pt_ref, pot, 0, out_ref, parts, wide, lambda c: None)
+    corr_ref[...] = dot3(parts, 0, ordering(coarse, True))
 
 
 def odd_kernel(
-    own_ref, swapped_ref, extra_ref, even_ref, pt_ref, pot, out_hbm, corr_hbm, out, parts, wide, sem, corr_sem
+    own_ref, swapped_ref, extra_ref, even_ref, corr_ref, pt_ref, pot, out_hbm, corr_hbm, out, parts, wide, sem, corr_sem
 ):
     stores = [
         [
@@ -614,7 +657,7 @@
     ]
     for store in stores[0]:
         store.start()
-    copy = pltpu.make_async_copy(own_ref, corr_hbm.at[0], corr_sem)
+    copy = pltpu.make_async_copy(corr_ref, corr_hbm.at[0], corr_sem)
     copy.start()
     position, devices = place()
     own = own_ref[...]
@@ -633,7 +676,7 @@
 
 
 def prolong_matrix(coarse):
-    return jnp.asarray(prolongation(coarse).T, BF16)
+    return jnp.asarray(prolongation(coarse).T[column_order(coarse)], BF16)
 
 
 def plane_scratch(coarse):
@@ -649,16 +692,17 @@
             jax.ShapeDtypeStruct((coarse, coarse), F32),
             jax.ShapeDtypeStruct((coarse, received.shape[2] - coarse), F32),
             jax.ShapeDtypeStruct((fine // LANES, fine, LANES), F32),
+            jax.ShapeDtypeStruct((coarse, coarse), F32),
         ),
         in_specs=[VMEM] * 5,
-        out_specs=(VMEM,) * 3,
+        out_specs=(VMEM,) * 4,
         scratch_shapes=plane_scratch(coarse),
         compiler_params=room(16),
         name="even_stage",
     )(received, back, swap, prolong_matrix(coarse), pot)
 
 
-def odd_stage(own, swapped, extra, even, pot):
+def odd_stage(own, swapped, extra, even, corr, pot):
     coarse = own.shape[0]
     fine = 2 * coarse
     blocks = fine // LANES
@@ -668,14 +712,14 @@
             jax.ShapeDtypeStruct((2, fine, fine), F32),
             jax.ShapeDtypeStruct((1, coarse, coarse), F32),
         ),
-        in_specs=[VMEM] * 6,
+        in_specs=[VMEM] * 7,
         out_specs=(HBM, HBM),
         scratch_shapes=[pltpu.VMEM((blocks, fine, LANES), F32)]
         + plane_scratch(coarse)
         + [pltpu.SemaphoreType.DMA((2 * blocks,)), pltpu.SemaphoreType.DMA],
         compiler_params=room(8),
         name="odd_stage",
-    )(own, swapped, extra, even, prolong_matrix(coarse), pot)
+    )(own, swapped, extra, even, corr, prolong_matrix(coarse), pot)
 
 
 def per_device(potential, source, side_faces, end_faces):
@@ -692,8 +736,8 @@
     back = back_matrices(coarse, devices, returned.shape[1])
     swap = swap_stage(coarse, returned, back)
     swapped = lax.ppermute(swap, AXES, in_chip)
-    own, extra, even = even_stage(returned, back, swap, pot)
-    return odd_stage(own, swapped, extra, even, pot)
+    own, extra, even, corr = even_stage(returned, back, swap, pot)
+    return odd_stage(own, swapped, extra, even, corr, pot)
 
 
 def solution(mesh):

time: 49.7 us -> 49.4 us (level)
  no operation moved by 1% of the time
where the time goes in v7:
time: 49.4 us; the launch traced here: 48.9 us
  blocking collectives  37.7 us (76%)
  Pallas kernels  8.55 us (17%)
  starting transfers between devices  1.26 us (3%)
  waiting for transfers between devices  0.72 us (1%)
  between operations  0.69 us (1%)
    all_to_all x1, blocking collectives, per_device(): received = lax.all_to_all(sent, AXES, 0, 0, tiled=True)  22.1 us
    all_to_all x1, blocking collectives, per_device(): returned = lax.all_to_all(solved, AXES, 0, 0, tiled=True)  15.6 us
    pallas_call x1, Pallas kernels, sent_stage(): pl.pallas_call(sent_kernel, out_shape=(plane, plane, jax.ShapeDtypeStruct...  3.16 us
    pallas_call x1, Pallas kernels, odd_stage(): pl.pallas_call(odd_kernel, out_shape=(jax.ShapeDtypeStruct((2, fine, fine...  1.55 us
    ppermute x1, starting transfers between devices, per_device(): swapped = lax.ppermute(swap, AXES, in_chip)  1.17 us
    pallas_call x1, Pallas kernels, sweep_stage(): pl.pallas_call(packed_sweep_kernel if packed else sweep_kernel, out_shape...  1.14 us
    pallas_call x1, Pallas kernels, own_stage(): pl.pallas_call(own_kernel, out_shape=(jax.ShapeDtypeStruct((coarse, coars...  1.01 us
  transfers between devices with their start and end apart: 2, of which 2 were waited for; matrix products, arithmetic and copies ran while one was open for 0% of the time, Pallas kernels for 4%

profile of v7, /device:TPU:1, one launch (start us, length us, event | category | flops | bytes accessed | tf_op | source)
XLA Modules:
  0.0 48.9 jit_solution(3845919360846817439)
XLA Ops:
  0.6 0.0 copy-start.3
  0.6 3.2 %sent_stage.1 = (f32[256,256]{1,0:T(8,128)S(1)}, f32[256,256]{1,0:T(8,128)S(1)}, f32[2,4,528,128]{3,2,1,0:T(8,128)S(1)}, f32[4,528,128]{2,1,0:T(8,128)S(1)}, f32...) custom-call(f32[2,512,512]{2,1,0:T(8,128)} %pot_hbm.1, ...), custom_call_target="tpu_custom_call" | custom-call | tf_op jit(solution)/shard_map/sent_stage/pallas_call | solution.py:291
  3.8 0.1 collective-permute-start
  3.9 0.0 copy-done.3
  3.9 1.0 %own_stage.1 = (f32[256,256]{1,0:T(8,128)S(1)}, f32[256,256]{1,0:T(8,128)S(1)}) custom-call(f32[4,528,128]{2,1,0:T(8,128)S(1)} %get-tuple-element.15.src0, f32[2,4,528,128]{3,2,1,0:T(8,128)S(1)} %get-tuple-element.16.pot, f32[256,256]{1,0:T(8,128)S(1)} %get-tuple-element.17.near_ref, f32[256,256]{1,0:T(8,128)S(1)} %get-tuple-element.18.far_ref, ...), custom_call_target="tpu_custom_call" | custom-call | tf_op jit(solution)/shard_map/own_stage/pallas_call | solution.py:364
  4.9 0.0 copy-start.2
  4.9 0.5 collective-permute-done.near_ref
  5.4 0.0 copy-start
  5.4 0.4 rows_stage.1
  5.8 0.0 copy-start.1
  5.8 22.1 %all_to_all.10.in_ref = f32[32,2,8,256]{3,2,1,0:T(8,128)S(1)} all-to-all(f32[32,2,8,256]{3,2,1,0:T(8,128)S(1)} %rows_stage.1), channel_id=1, replica_groups=mesh['grp'=8,'mem'=4] {'grp','mem'}, dimensions={0} | all-to-all | bytes 1048576 | tf_op jit(solution)/shard_map/all_to_all | solution.py:733
  27.9 0.0 copy-done.2
  27.9 1.1 %sweep_stage.1 = f32[32,8,384]{2,1,0:T(8,128)S(1)} custom-call(f32[32,2,8,256]{3,2,1,0:T(8,128)S(1)} %all_to_all.10.in_ref, f32[32,8,128]{2,1,0:T(8,128)S(1)} %copy-done.2), custom_call_target="tpu_custom_call" | custom-call | tf_op jit(solution)/shard_map/sweep_stage/pallas_call | solution.py:547
  29.1 15.6 %all_to_all.11.in_ref = f32[32,8,384]{2,1,0:T(8,128)S(1)} all-to-all(f32[32,8,384]{2,1,0:T(8,128)S(1)} %sweep_stage.1), channel_id=1, replica_groups=mesh['grp'=8,'mem'=4] {'grp','mem'}, dimensions={0} | all-to-all | bytes 786432 | tf_op jit(solution)/shard_map/all_to_all | solution.py:735
  44.6 0.0 copy-done
  44.7 0.4 swap_stage.1.swap_ref
  45.0 1.2 %collective-permute-start.1 = (f32[256,256]{1,0:T(8,128)S(1)}, f32[256,256]{1,0:T(8,128)S(1)}, u32[]{:S(2)}, u32[]{:S(2)}) collective-permute-start(f32[256,256]{1,0:T(8,128)S(1)} %swap_stage.1.swap_ref), channel_id=1, source_target_pairs={{0,1},{1,0},{2,3},{3,2},{4,5},{5,4},{6,7},{7,6},{8,9},{9,8},{10,11... | collective-permute-start | bytes 786440 | tf_op jit(solution)/shard_map/ppermute | solution.py:738
  46.2 0.0 copy-done.1
  46.2 0.9 %even_stage.1 = (f32[256,256]{1,0:T(8,128)S(1)}, f32[256,128]{1,0:T(8,128)S(1)}, f32[4,512,128]{2,1,0:T(8,128)S(1)}, f32[256,256]{1,0:T(8,128)S(1)}) custom-call(f32[32,8,384]{2,1,0:T(8,128)S(1)} %all_to_all.11.in_ref, bf16[3,256,256]{2,1,0:T(8,128)(2,1)S(1)} %copy-done, f32[256,256]{1,0:T(8,128)S(1)} %swap_stage.1.swap_ref, bf16[256,512]{1,0:T(8,128)(2,1)S(1)} %copy-done.1, ...), custom_call_target="tpu_custom_call" | custom-call | tf_op jit(solution)/shard_map/even_stage/pallas_call | solution.py:689
  47.1 0.2 collective-permute-done.1.swapped_ref
  47.4 1.5 %odd_stage.1 = (f32[2,512,512]{2,1,0:T(8,128)}, f32[1,256,256]{2,1,0:T(8,128)}) custom-call(f32[256,256]{1,0:T(8,128)S(1)} %get-tuple-element.24.own_ref, f32[256,256]{1,0:T(8,128)S(1)} %collective-permute-done.1.swapped_ref, f32[256,128]{1,0:T(8,128)S(1)} %get-tuple-element.25.extra_ref, f32[4,512,128]{2,1,0:T(8,128)S(1)} %get-tuple-element.26.even_ref, ...), custom_call_target="tpu_custom_call" | custom-call | tf_op jit(solution)/shard_map/odd_stage/pallas_call | solution.py:709
Async XLA Ops:
  0.6 3.3 %copy-start.3 = (f32[1,4,256]{2,1,0:T(4,128)S(1)}, f32[1,4,256]{2,1,0:T(4,128)}, u32[]{:S(2)}) copy-start(f32[1,4,256]{2,1,0:T(4,128)} %side_ref.1) | copy-start | bytes 12292
  3.8 1.6 %collective-permute-start = (f32[256,256]{1,0:T(8,128)S(1)}, f32[256,256]{1,0:T(8,128)S(1)}, u32[]{:S(2)}, u32[]{:S(2)}) collective-permute-start(f32[256,256]{1,0:T(8,128)S(1)} %get-tuple-element.17.near_ref), channel_id=1, source_target_pairs={{0,1},{1,0},{2,3},{3,2},{4,5},{5,4},{6,7},{7,6},{8,9},{9,8},{10,11... | collective-permute-start | bytes 786440 | tf_op jit(solution)/shard_map/ppermute | solution.py:730
  4.9 23.0 %copy-start.2 = (f32[32,8,128]{2,1,0:T(8,128)S(1)}, f32[32,8,128]{2,1,0:T(8,128)}, u32[]{:S(2)}) copy-start(f32[32,8,128]{2,1,0:T(8,128)} %constant.9.clone.alpha_ref) | copy-start | bytes 393220
  5.4 39.2 %copy-start = (bf16[3,256,256]{2,1,0:T(8,128)(2,1)S(1)}, bf16[3,256,256]{2,1,0:T(8,128)(2,1)}, u32[]{:S(2)}) copy-start(bf16[3,256,256]{2,1,0:T(8,128)(2,1)} %constant.10.clone.back_ref) | copy-start | bytes 1179652
  5.8 40.4 %copy-start.1 = (bf16[256,512]{1,0:T(8,128)(2,1)S(1)}, bf16[256,512]{1,0:T(8,128)(2,1)}, u32[]{:S(2)}) copy-start(bf16[256,512]{1,0:T(8,128)(2,1)} %constant.11.clone.pt_ref) | copy-start | bytes 786436
  45.0 2.3 %collective-permute-start.1 = (f32[256,256]{1,0:T(8,128)S(1)}, f32[256,256]{1,0:T(8,128)S(1)}, u32[]{:S(2)}, u32[]{:S(2)}) collective-permute-start(f32[256,256]{1,0:T(8,128)S(1)} %swap_stage.1.swap_ref), channel_id=1, source_target_pairs={{0,1},{1,0},{2,3},{3,2},{4,5},{5,4},{6,7},{7,6},{8,9},{9,8},{10,11... | collective-permute-start | bytes 786440 | tf_op jit(solution)/shard_map/ppermute | solution.py:738

commit v8 on v7

--- a/solution.py
+++ b/solution.py
@@ -485,10 +485,10 @@
             low = jnp.where(first, one, swapped(two)) * (0.5 * sixth)
             high = jnp.where(first, swapped(one), two) * (0.5 * sixth * signs[q % 2][c])
             red_force[q, :, columns[c]] = low + high
-            black_force[q, :, columns[c]] = low - high
+            black_force[q, :, columns[c]] = 6.0 * (low - high)
             red[q, :, columns[c]] = low + high
 
-    def update(target, force, other):
+    def update(target, force, other, centre, scale):
         def held(q):
             return [other[q, :, columns[c]] for c in range(count)]
 
@@ -499,23 +499,24 @@
             over = held(q + 1) if q + 1 < slots else beyond
             sums = beside_columns(here, lanes)
             for c in range(count):
-                target[q, :, columns[c]] = (force[q, :, columns[c]] + alpha * here[c]) + sixth * (
-                    (under[c] + over[c]) + sums[c]
-                )
+                around_it = (under[c] + over[c]) + sums[c]
+                if scale is not None:
+                    around_it = scale * around_it
+                target[q, :, columns[c]] = (force[q, :, columns[c]] + centre * here[c]) + around_it
             under, here = here, over
 
-    update(black, black_force, red)
+    update(black, black_force, red, 6.0 * alpha, None)
 
     def sweep(counter, carry):
-        update(red, red_force, black)
-        update(black, black_force, red)
+        update(red, red_force, black, sixth * alpha, sixth * sixth)
+        update(black, black_force, red, 6.0 * alpha, None)
         return carry
 
     lax.fori_loop(0, SWEEPS - 1, sweep, 0, unroll=True)
 
     for q in range(slots):
         for c in range(count):
-            on_red, on_black = red[q, :, columns[c]], black[q, :, columns[c]]
+            on_red, on_black = red[q, :, columns[c]], sixth * black[q, :, columns[c]]
             low = on_red + on_black
             high = signs[q % 2][c] * (on_red - on_black)
             store_solved(out_ref, planes, q, c, 0, jnp.where(first, low, swapped(high)))

time: 49.4 us -> 49.4 us (level)
  no operation moved by 1% of the time
where the time goes in v8:
time: 49.4 us; the launch traced here: 48.9 us
  blocking collectives  37.7 us (76%)
  Pallas kernels  8.55 us (17%)
  starting transfers between devices  1.25 us (3%)
  waiting for transfers between devices  0.72 us (1%)
  between operations  0.69 us (1%)
    all_to_all x1, blocking collectives, per_device(): received = lax.all_to_all(sent, AXES, 0, 0, tiled=True)  22.1 us
    all_to_all x1, blocking collectives, per_device(): returned = lax.all_to_all(solved, AXES, 0, 0, tiled=True)  15.6 us
    pallas_call x1, Pallas kernels, sent_stage(): pl.pallas_call(sent_kernel, out_shape=(plane, plane, jax.ShapeDtypeStruct...  3.16 us
    pallas_call x1, Pallas kernels, odd_stage(): pl.pallas_call(odd_kernel, out_shape=(jax.ShapeDtypeStruct((2, fine, fine...  1.55 us
    ppermute x1, starting transfers between devices, per_device(): swapped = lax.ppermute(swap, AXES, in_chip)  1.17 us
    pallas_call x1, Pallas kernels, sweep_stage(): pl.pallas_call(packed_sweep_kernel if packed else sweep_kernel, out_shape...  1.14 us
    pallas_call x1, Pallas kernels, own_stage(): pl.pallas_call(own_kernel, out_shape=(jax.ShapeDtypeStruct((coarse, coars...  1.01 us
  transfers between devices with their start and end apart: 2, of which 2 were waited for; matrix products, arithmetic and copies ran while one was open for 0% of the time, Pallas kernels for 4%

profile of v8, /device:TPU:1, one launch (start us, length us, event | category | flops | bytes accessed | tf_op | source)
XLA Modules:
  0.0 48.9 jit_solution(14882648255244485740)
XLA Ops:
  0.6 0.0 copy-start.3
  0.6 3.2 %sent_stage.1 = (f32[256,256]{1,0:T(8,128)S(1)}, f32[256,256]{1,0:T(8,128)S(1)}, f32[2,4,528,128]{3,2,1,0:T(8,128)S(1)}, f32[4,528,128]{2,1,0:T(8,128)S(1)}, f32...) custom-call(f32[2,512,512]{2,1,0:T(8,128)} %pot_hbm.1, ...), custom_call_target="tpu_custom_call" | custom-call | tf_op jit(solution)/shard_map/sent_stage/pallas_call | solution.py:291
  3.8 0.1 collective-permute-start
  3.9 0.0 copy-done.3
  3.9 1.0 %own_stage.1 = (f32[256,256]{1,0:T(8,128)S(1)}, f32[256,256]{1,0:T(8,128)S(1)}) custom-call(f32[4,528,128]{2,1,0:T(8,128)S(1)} %get-tuple-element.15.src0, f32[2,4,528,128]{3,2,1,0:T(8,128)S(1)} %get-tuple-element.16.pot, f32[256,256]{1,0:T(8,128)S(1)} %get-tuple-element.17.near_ref, f32[256,256]{1,0:T(8,128)S(1)} %get-tuple-element.18.far_ref, ...), custom_call_target="tpu_custom_call" | custom-call | tf_op jit(solution)/shard_map/own_stage/pallas_call | solution.py:364
  4.9 0.0 copy-start.2
  4.9 0.5 collective-permute-done.near_ref
  5.4 0.0 copy-start
  5.4 0.4 rows_stage.1
  5.8 0.0 copy-start.1
  5.8 22.1 %all_to_all.10.in_ref = f32[32,2,8,256]{3,2,1,0:T(8,128)S(1)} all-to-all(f32[32,2,8,256]{3,2,1,0:T(8,128)S(1)} %rows_stage.1), channel_id=1, replica_groups=mesh['grp'=8,'mem'=4] {'grp','mem'}, dimensions={0} | all-to-all | bytes 1048576 | tf_op jit(solution)/shard_map/all_to_all | solution.py:734
  27.9 0.0 copy-done.2
  27.9 1.1 %sweep_stage.1 = f32[32,8,384]{2,1,0:T(8,128)S(1)} custom-call(f32[32,2,8,256]{3,2,1,0:T(8,128)S(1)} %all_to_all.10.in_ref, f32[32,8,128]{2,1,0:T(8,128)S(1)} %copy-done.2), custom_call_target="tpu_custom_call" | custom-call | tf_op jit(solution)/shard_map/sweep_stage/pallas_call | solution.py:548
  29.1 15.6 %all_to_all.11.in_ref = f32[32,8,384]{2,1,0:T(8,128)S(1)} all-to-all(f32[32,8,384]{2,1,0:T(8,128)S(1)} %sweep_stage.1), channel_id=1, replica_groups=mesh['grp'=8,'mem'=4] {'grp','mem'}, dimensions={0} | all-to-all | bytes 786432 | tf_op jit(solution)/shard_map/all_to_all | solution.py:736
  44.6 0.0 copy-done
  44.6 0.4 swap_stage.1.swap_ref
  45.0 1.2 %collective-permute-start.1 = (f32[256,256]{1,0:T(8,128)S(1)}, f32[256,256]{1,0:T(8,128)S(1)}, u32[]{:S(2)}, u32[]{:S(2)}) collective-permute-start(f32[256,256]{1,0:T(8,128)S(1)} %swap_stage.1.swap_ref), channel_id=1, source_target_pairs={{0,1},{1,0},{2,3},{3,2},{4,5},{5,4},{6,7},{7,6},{8,9},{9,8},{10,11... | collective-permute-start | bytes 786440 | tf_op jit(solution)/shard_map/ppermute | solution.py:739
  46.2 0.0 copy-done.1
  46.2 0.9 %even_stage.1 = (f32[256,256]{1,0:T(8,128)S(1)}, f32[256,128]{1,0:T(8,128)S(1)}, f32[4,512,128]{2,1,0:T(8,128)S(1)}, f32[256,256]{1,0:T(8,128)S(1)}) custom-call(f32[32,8,384]{2,1,0:T(8,128)S(1)} %all_to_all.11.in_ref, bf16[3,256,256]{2,1,0:T(8,128)(2,1)S(1)} %copy-done, f32[256,256]{1,0:T(8,128)S(1)} %swap_stage.1.swap_ref, bf16[256,512]{1,0:T(8,128)(2,1)S(1)} %copy-done.1, ...), custom_call_target="tpu_custom_call" | custom-call | tf_op jit(solution)/shard_map/even_stage/pallas_call | solution.py:690
  47.1 0.2 collective-permute-done.1.swapped_ref
  47.4 1.5 %odd_stage.1 = (f32[2,512,512]{2,1,0:T(8,128)}, f32[1,256,256]{2,1,0:T(8,128)}) custom-call(f32[256,256]{1,0:T(8,128)S(1)} %get-tuple-element.24.own_ref, f32[256,256]{1,0:T(8,128)S(1)} %collective-permute-done.1.swapped_ref, f32[256,128]{1,0:T(8,128)S(1)} %get-tuple-element.25.extra_ref, f32[4,512,128]{2,1,0:T(8,128)S(1)} %get-tuple-element.26.even_ref, ...), custom_call_target="tpu_custom_call" | custom-call | tf_op jit(solution)/shard_map/odd_stage/pallas_call | solution.py:710
Async XLA Ops:
  0.6 3.3 %copy-start.3 = (f32[1,4,256]{2,1,0:T(4,128)S(1)}, f32[1,4,256]{2,1,0:T(4,128)}, u32[]{:S(2)}) copy-start(f32[1,4,256]{2,1,0:T(4,128)} %side_ref.1) | copy-start | bytes 12292
  3.8 1.6 %collective-permute-start = (f32[256,256]{1,0:T(8,128)S(1)}, f32[256,256]{1,0:T(8,128)S(1)}, u32[]{:S(2)}, u32[]{:S(2)}) collective-permute-start(f32[256,256]{1,0:T(8,128)S(1)} %get-tuple-element.17.near_ref), channel_id=1, source_target_pairs={{0,1},{1,0},{2,3},{3,2},{4,5},{5,4},{6,7},{7,6},{8,9},{9,8},{10,11... | collective-permute-start | bytes 786440 | tf_op jit(solution)/shard_map/ppermute | solution.py:731
  4.9 23.0 %copy-start.2 = (f32[32,8,128]{2,1,0:T(8,128)S(1)}, f32[32,8,128]{2,1,0:T(8,128)}, u32[]{:S(2)}) copy-start(f32[32,8,128]{2,1,0:T(8,128)} %constant.9.clone.alpha_ref) | copy-start | bytes 393220
  5.4 39.2 %copy-start = (bf16[3,256,256]{2,1,0:T(8,128)(2,1)S(1)}, bf16[3,256,256]{2,1,0:T(8,128)(2,1)}, u32[]{:S(2)}) copy-start(bf16[3,256,256]{2,1,0:T(8,128)(2,1)} %constant.10.clone.back_ref) | copy-start | bytes 1179652
  5.8 40.4 %copy-start.1 = (bf16[256,512]{1,0:T(8,128)(2,1)S(1)}, bf16[256,512]{1,0:T(8,128)(2,1)}, u32[]{:S(2)}) copy-start(bf16[256,512]{1,0:T(8,128)(2,1)} %constant.11.clone.pt_ref) | copy-start | bytes 786436
  45.0 2.3 %collective-permute-start.1 = (f32[256,256]{1,0:T(8,128)S(1)}, f32[256,256]{1,0:T(8,128)S(1)}, u32[]{:S(2)}, u32[]{:S(2)}) collective-permute-start(f32[256,256]{1,0:T(8,128)S(1)} %swap_stage.1.swap_ref), channel_id=1, source_target_pairs={{0,1},{1,0},{2,3},{3,2},{4,5},{5,4},{6,7},{7,6},{8,9},{9,8},{10,11... | collective-permute-start | bytes 786440 | tf_op jit(solution)/shard_map/ppermute | solution.py:739
